TPU v7x, 32 devices: a whole 2x2x4 slice. The times are simulated.
32 devices in a mesh: context: 8 (over z, y), tensor: 4 (over x, core).
Axes of the slice: x: 2, y: 2, z: 4, core: 2. Of those that a mesh axis runs over, the one named last changes fastest.
Arguments:
- tokens: bfloat16 [4096, 4096], P(('context', 'tensor')), may hold values from -6 to 6
- norm_gain: float32 [4096], replicated, may hold values from 0.5 to 1.5
- in_weight: bfloat16 [4096, 3, 2048], P(None, None, 'tensor'), may hold values from -0.09375 to 0.09375
- short_weight: float32 [3, 3, 2048], P(None, None, 'tensor'), may hold values from -3 to 3
- long_filter: float32 [4096, 2048], P('context', 'tensor'), may hold values from -0.09375 to 0.09375
- skip_gain: float32 [2048], P('tensor'), may hold values from -4 to 4
Outputs:
- block_out: bfloat16 [4096, 2048], P('context', 'tensor')
All inputs are finite; a program needn't handle non-finite values.
Results may differ from a plain program's by a relative error of at most 0.0065.
Values may be sent and summed in bfloat16 or wider, within the bound.
No kernel may reach another device: no remote copies, remote signals or barrier semaphores. Data moves between devices by JAX's collectives and lax.ppermute only.
A program may use at most 128 MiB of HBM per device.

v0:
```python
import math

import jax
import jax.numpy as jnp
from jax import lax
from jax.sharding import PartitionSpec as P

eps = 1e-06


def shifted(x, axis, by):
    peers = lax.axis_size(axis)
    pairs = [(i, i + by) for i in range(peers) if 0 <= i + by < peers]
    return lax.ppermute(x, axis, pairs)


def along_rows(table, block):
    return jnp.einsum("kj,tjc->tkc", table, block, precision=lax.Precision.HIGHEST)


def transposed(stacked, forward):
    dev_count = lax.axis_size("context")
    planes, turn_count, length, channels = stacked.shape
    ranks = jnp.arange(dev_count, dtype=jnp.int32)
    phase_angle = (ranks[:, None] * ranks[None, :] % dev_count).astype(jnp.float32) * (
        2.0 * math.pi / dev_count
    )
    table_re = jnp.cos(phase_angle)
    if forward:
        table_im = -jnp.sin(phase_angle)
    else:
        table_im = jnp.sin(phase_angle)

    def combine_rows(received):
        rows_re = jnp.einsum(
            "fp,tpjc->tfjc", table_re, received[0], precision=lax.Precision.HIGHEST
        ) - jnp.einsum("fp,tpjc->tfjc", table_im, received[1], precision=lax.Precision.HIGHEST)
        rows_im = jnp.einsum(
            "fp,tpjc->tfjc", table_re, received[1], precision=lax.Precision.HIGHEST
        ) + jnp.einsum("fp,tpjc->tfjc", table_im, received[0], precision=lax.Precision.HIGHEST)
        return jnp.stack([rows_re, rows_im])

    sectioned = stacked.reshape(planes, turn_count, 1, length, channels)
    if forward:
        result_grid = lax.all_to_all(
            combine_rows(
                lax.all_to_all(sectioned, "context", split_axis=3, concat_axis=2, tiled=True)
            ),
            "context",
            split_axis=2,
            concat_axis=3,
            tiled=True,
        )
    else:
        result_grid = lax.all_to_all(
            combine_rows(
                lax.all_to_all(sectioned, "context", split_axis=3, concat_axis=2, tiled=True)
            ),
            "context",
            split_axis=2,
            concat_axis=3,
            tiled=True,
        )
    return result_grid.reshape(planes, turn_count, length, channels)


def local(tokens, norm_gain, in_weight, short_weight, long_filter, skip_gain):
    width = tokens.shape[1]
    channels = in_weight.shape[2]
    tap_count = short_weight.shape[0]
    flat_weight = in_weight.reshape(width, 3 * channels)
    values = lax.all_gather(tokens, "tensor", axis=0, tiled=True).astype(jnp.float32)
    inv_rms = lax.rsqrt(jnp.mean(values * values, axis=1, keepdims=True) + eps)
    normed = (values * inv_rms * norm_gain).astype(jnp.bfloat16)
    projected = jnp.dot(normed, flat_weight, preferred_element_type=jnp.float32)
    length = projected.shape[0]
    before = shifted(projected[length - (tap_count - 1) :], "context", 1)
    padded = jnp.concatenate([before, projected], axis=0)
    tap_rows = short_weight.reshape(tap_count, 3 * channels)
    mixed_rows = jnp.zeros_like(projected)
    for tap_index in range(tap_count):
        offset = tap_count - 1 - tap_index
        mixed_rows = mixed_rows + tap_rows[tap_index] * padded[offset : offset + length]
    query_part = mixed_rows[:, :channels]
    key_part = mixed_rows[:, channels : 2 * channels]
    value_part = mixed_rows[:, 2 * channels :]
    gated = key_part * value_part
    dev_count = lax.axis_size("context")
    device = lax.axis_index("context")
    total_points = 2 * dev_count * length
    half_turn = device.astype(jnp.float32) * (math.pi / dev_count)
    source = jnp.concatenate([gated, long_filter], axis=1)
    zero_plane = jnp.zeros_like(source)
    shifted_re = source * jnp.cos(half_turn)
    shifted_im = -source * jnp.sin(half_turn)
    stacked = jnp.stack([jnp.stack([source, shifted_re]), jnp.stack([zero_plane, shifted_im])])
    stacked = transposed(stacked, True)
    turn_ids = jnp.arange(2, dtype=jnp.int32)
    coarse = 2 * device + turn_ids
    positions = jnp.arange(length, dtype=jnp.int32)
    twist_phase = (positions[None, :] * coarse[:, None] % total_points).astype(jnp.float32) * (
        2.0 * math.pi / total_points
    )
    twist_re = jnp.cos(twist_phase)[:, :, None]
    twist_im = -jnp.sin(twist_phase)[:, :, None]
    turned_re = stacked[0] * twist_re - stacked[1] * twist_im
    turned_im = stacked[0] * twist_im + stacked[1] * twist_re
    table_phase = (positions[:, None] * positions[None, :] % length).astype(jnp.float32) * (
        2.0 * math.pi / length
    )
    cos_table = jnp.cos(table_phase)
    sin_table = jnp.sin(table_phase)
    spec_re = along_rows(cos_table, turned_re) + along_rows(sin_table, turned_im)
    spec_im = along_rows(cos_table, turned_im) - along_rows(sin_table, turned_re)
    signal_re = spec_re[:, :, :channels]
    signal_im = spec_im[:, :, :channels]
    filt_re = spec_re[:, :, channels:]
    filt_im = spec_im[:, :, channels:]
    prod_re = signal_re * filt_re - signal_im * filt_im
    prod_im = signal_re * filt_im + signal_im * filt_re
    back_re = along_rows(cos_table, prod_re) - along_rows(sin_table, prod_im)
    back_im = along_rows(sin_table, prod_re) + along_rows(cos_table, prod_im)
    untw_re = back_re * twist_re + back_im * twist_im
    untw_im = back_im * twist_re - back_re * twist_im
    stacked = jnp.stack([untw_re, untw_im])
    stacked = transposed(stacked, False)
    conv = (
        stacked[0, 0] + stacked[0, 1] * jnp.cos(half_turn) - stacked[1, 1] * jnp.sin(half_turn)
    ) / total_points
    block_out = query_part * (conv + skip_gain * gated)
    return block_out.astype(jnp.bfloat16)


def solution(mesh):
    return jax.shard_map(
        local,
        mesh=mesh,
        in_specs=(
            P(("context", "tensor"), None),
            P(),
            P(None, None, "tensor"),
            P(None, None, "tensor"),
            P("context", "tensor"),
            P("tensor"),
        ),
        out_specs=P("context", "tensor"),
        check_vma=False,
    )
```

profile of v0, /device:TPU:0, one launch (start us, length us, event | category | flops | bytes accessed | tf_op | source)
XLA Modules:
  0.0 858.5 jit_solution(13042086948463147038)
XLA Ops:
  6.5 0.0 all-gather.2.cloned.1.call-start
  6.5 0.7 all-gather.2.cloned.1.call-update
  7.3 0.0 copy-start.6
  7.3 17.1 %copy.52 = bf16[4096,3,512]{0,2,1:T(8,128)(2,1)} copy(bf16[4096,3,512]{2,0,1:T(8,128)(2,1)} %param.8) | data formatting | bytes 25165824 | tf_op args[2]
  24.3 21.8 %all-gather.2.cloned.1.call-done = bf16[512,4096]{1,0:T(8,128)(2,1)} async-done(((bf16[128,4096]{1,0:T(8,128)(2,1)}), bf16[512,4096]{1,0:T(8,128)(2,1)}) %all-gather.2.cloned.1.call-update) | async-done | bytes 4194320 | tf_op jit(solution)/shard_map/all_gather | solution.py:72
  46.1 3.2 fusion
  49.4 0.0 copy-done.6
  49.4 0.2 copy-done.1
  49.6 9.4 %fusion.3 = f32[512,1536]{1,0:T(8,128)S(1)} fusion(bf16[4096,1536]{0,1:T(8,128)(2,1)} %bitcast.124, bf16[512,4096]{1,0:T(8,128)(2,1)S(1)} %copy-done.1, f32[4096]{0:T(1024)S(1)} %copy-done.6, f32[512]{0:T(512)S(1)} %add_rsqrt_fusion), kind=kOutput, calls=%fused_computation.7 | convolution fusion | flops 6450839552 | bytes 19941376 | tf_op jit(solution)/shard_map/dot_general | solution.py:75
  59.0 0.0 copy-start.3
  59.0 3.4 collective-permute-start
  62.4 0.0 copy-done.4
  62.7 0.0 copy-done.3
  62.7 1.2 collective-permute-done
  63.8 4.9 fusion.18
  68.7 0.0 copy-start.2
  68.7 0.2 fusion.177
  69.0 0.2 slice_multiply_fusion.2
  69.2 0.8 copy-done.2
  70.0 0.2 maximum_bitcast_fusion.3
  70.1 0.4 fusion.32
  70.5 1.0 maximum_bitcast_fusion.1
  71.5 1.7 maximum_bitcast_fusion
  73.2 7.4 copy.53
  80.6 188.8 %all_to_all.16 = f32[2,2,1,512,1024]{4,1,0,2,3:T(2,128)} all-to-all(f32[2,2,1,512,1024]{4,1,0,2,3:T(2,128)S(1)} %copy.53), channel_id=1, replica_groups=mesh['context'=8,'tensor'=4] {'context'}, dimensions={3} | all-to-all | bytes 16777216 | tf_op jit(solution)/shard_map/all_to_all | solution.py:47
  269.4 9.6 %fusion.167 = (f32[1,2,1,512,1024]{4,1,0,2,3:T(2,128)}, f32[1,2,1,512,1024]{4,1,0,2,3:T(2,128)}) fusion(f32[2,2,1,512,1024]{4,1,0,2,3:T(2,128)} %all_to_all.16), kind=kLoop, calls=%fused_computation.185 | loop fusion | bytes 16777216 | tf_op jit(solution)/shard_map/slice | solution.py:36
  279.0 3.5 copy.84
  282.5 7.8 fusion.9
  290.3 8.1 fusion.7
  298.5 1.4 copy.83
  299.8 8.1 subtract_bitcast_fusion.1
  307.9 8.0 add_bitcast_fusion.1
  315.9 1.7 pad_maximum_fusion
  317.6 8.5 copy.60
  326.1 5.0 all-to-all-start.1
  331.0 0.2 fusion.91
  331.2 181.8 %all-to-all-done.1 = f32[2,2,8,64,1024]{4,3,1,0,2:T(8,128)} async-done(((f32[2,2,8,64,1024]{4,3,1,0,2:T(8,128)}), f32[2,2,8,64,1024]{4,3,1,0,2:T(8,128)}, u32[]{:S(2)}, u32[]{:S(2)}) %all-to-all-start.1) | async-done | bytes 8388640 | tf_op jit(solution)/shard_map/all_to_all | solution.py:45
  513.0 4.3 fusion.166
  517.3 0.5 copy.85
  517.8 0.5 copy.86
  518.3 18.1 %fusion.37 = f32[2,1024,512]{2,1,0:T(8,128)S(1)} fusion(f32[2,512,1024]{2,1,0:T(8,128)S(1)} %bitcast.111, f32[2,512,1024]{2,1,0:T(8,128)S(1)} %bitcast.107, f32[2,512]{1,0:T(2,128)S(1)} %get-tuple-element.21, f32[2,512]{1,0:T(2,128)S(1)} %get-tuple-element.20), kind=kOutput, calls=%fused_computation.59 | convolution fusion | flops 6449266688 | bytes 12591104 | tf_op jit(solution)/shard_map/kj,tjc->tkc/dot_general | solution.py:18
  536.4 18.5 %fusion.38 = f32[2,1024,512]{2,1,0:T(8,128)S(1)} fusion(f32[2,512,1024]{2,1,0:T(8,128)S(1)} %bitcast.112, f32[2,512,1024]{2,1,0:T(8,128)S(1)} %bitcast.108, f32[2,512]{1,0:T(2,128)S(1)} %get-tuple-element.21, f32[2,512]{1,0:T(2,128)S(1)} %get-tuple-element.20), kind=kOutput, calls=%fused_computation.60 | convolution fusion | flops 6449266688 | bytes 12591104 | tf_op jit(solution)/shard_map/kj,tjc->tkc/dot_general | solution.py:18
  554.9 18.2 %add_bitcast_fusion = f32[2,512,1024]{1,2,0:T(8,128)S(1)} fusion(f32[2,1024,512]{2,1,0:T(8,128)S(1)} %fusion.37, f32[2,512,1024]{2,1,0:T(8,128)S(1)} %bitcast.113, f32[2,512,1024]{2,1,0:T(8,128)S(1)} %bitcast.109, f32[2,512]{1,0:T(2,128)S(1)} %get-tuple-element.21, f32[2,512]{1,0:T(2,128)S(1)} %get-tuple-element.20), kind=kOutput, calls=%fused_computation.12 | convolution fusion | flops 6450315264 | bytes 16785408 | tf_op jit(solution)/shard_map/kj,tjc->tkc/dot_general | solution.py:18
  573.1 18.6 %subtract_bitcast_fusion = f32[2,512,1024]{1,2,0:T(8,128)S(1)} fusion(f32[2,1024,512]{2,1,0:T(8,128)S(1)} %fusion.38, f32[2,512,1024]{2,1,0:T(8,128)S(1)} %bitcast.114, f32[2,512,1024]{2,1,0:T(8,128)S(1)} %bitcast.110, f32[2,512]{1,0:T(2,128)S(1)} %get-tuple-element.21, f32[2,512]{1,0:T(2,128)S(1)} %get-tuple-element.20), kind=kOutput, calls=%fused_computation.11 | convolution fusion | flops 6450315264 | bytes 16785408 | tf_op jit(solution)/shard_map/kj,tjc->tkc/dot_general | solution.py:18
  591.8 1.3 multiply_add_fusion.1
  593.1 8.4 fusion.49
  601.5 8.4 fusion.55
  609.9 8.6 %convolution_add_fusion = f32[2,512,512]{2,1,0:T(8,128)S(1)} fusion(f32[2,512,512]{2,1,0:T(8,128)S(1)} %fusion.49, f32[2,512,512]{1,2,0:T(8,128)S(1)} %get-tuple-element.5), kind=kOutput, calls=%fused_computation.54 | convolution fusion | flops 3225419776 | bytes 6291456 | tf_op jit(solution)/shard_map/kj,tjc->tkc/dot_general | solution.py:18
  618.6 8.7 %add_bitcast_fusion.3 = (f32[1,2,512,512]{2,3,1,0:T(8,128)S(1)}, f32[1,2,512,512]{2,3,1,0:T(8,128)S(1)}) fusion(f32[2,512,512]{2,1,0:T(8,128)S(1)} %convolution_add_fusion, f32[2,512]{1,0:T(2,128)S(1)} %get-tuple-element.21, f32[2,512]{1,0:T(2,128)S(1)} %get-tuple-element.20, f32[2,512,512]{2,1,0:T(8,128)S(1)} %fusion.55, ...), kind=kOutput, calls=%fused_computation.41 | convolution fusion | flops 3228565504 | bytes 10493952 | tf_op jit(solution)/shard_map/kj,tjc->tkc/dot_general | solution.py:18
  627.3 2.4 maximum_bitcast_fusion.2
  629.7 7.3 copy.67
  637.0 96.9 %all_to_all.17 = f32[2,2,1,512,512]{4,1,0,2,3:T(2,128)S(1)} all-to-all(f32[2,2,1,512,512]{4,1,0,2,3:T(2,128)} %copy.67), channel_id=1, replica_groups=mesh['context'=8,'tensor'=4] {'context'}, dimensions={3} | all-to-all | bytes 8388608 | tf_op jit(solution)/shard_map/all_to_all | solution.py:57
  733.9 1.4 fusion.168
  735.3 0.4 copy.88
  735.8 3.2 fusion.26
  739.0 3.2 fusion.24
  742.2 0.4 copy.87
  742.6 3.6 subtract_bitcast_fusion.2
  746.2 3.4 add_bitcast_fusion.2
  749.6 0.4 pad_maximum_fusion.1
  750.0 2.4 copy.74
  752.5 96.5 %all_to_all.18 = f32[2,2,8,64,512]{4,3,1,0,2:T(8,128)S(1)} all-to-all(f32[2,2,8,64,512]{4,3,1,0,2:T(8,128)S(1)} %copy.74), channel_id=1, replica_groups=mesh['context'=8,'tensor'=4] {'context'}, dimensions={2} | all-to-all | bytes 8388608 | tf_op jit(solution)/shard_map/all_to_all | solution.py:55
  849.0 0.7 copy.75
  849.7 1.6 fusion.47
  (13 shorter events, 0.1 us)
Async XLA Ops:
  6.5 39.6 %all-gather.2.cloned.1.call-start = ((), (), s32[]{:S(2)}) async-start(), calls=%async_computation.4 | async-start | bytes 5242880 | tf_op jit(solution)/shard_map/all_gather | solution.py:72
  7.3 42.1 %copy-start.6 = (f32[4096]{0:T(1024)S(1)}, f32[4096]{0:T(1024)}, u32[]{:S(2)}) copy-start(f32[4096]{0:T(1024)} %param.7) | copy-start | bytes 49156
  46.1 3.4 copy-start.1
  49.6 12.9 %copy-start.4 = (f32[3,3,512]{2,1,0:T(4,128)S(1)}, f32[3,3,512]{2,1,0:T(4,128)}, u32[]{:S(2)}) copy-start(f32[3,3,512]{2,1,0:T(4,128)} %param.9) | copy-start | bytes 55300
  59.0 3.6 copy-start.3
  59.0 4.8 collective-permute-start
  68.7 1.2 copy-start.2
  290.3 8.2 copy-start
  326.1 186.9 %all-to-all-start.1 = ((f32[2,2,8,64,1024]{4,3,1,0,2:T(8,128)}), f32[2,2,8,64,1024]{4,3,1,0,2:T(8,128)}, u32[]{:S(2)}, u32[]{:S(2)}) async-start(f32[2,2,8,64,1024]{4,3,1,0,2:T(8,128)} %copy.60), calls=%async_computation.1 | async-start | bytes 16777216 | tf_op jit(solution)/shard_map/all_to_all | solution.py:45
  849.0 0.7 copy-start.5
Sparse Core Ops, SparseCore 0:
  8.9 37.1 all-gather.1
where the time goes:
time: 865 us; the launch traced here: 859 us
  blocking collectives  382 us (44%)
  waiting for transfers between devices  205 us (24%)
  matrix products  162 us (19%)
  local copies, waits for them, and re-layouts  66.5 us (8%)
  other arithmetic  19.3 us (2%)
  between operations  14.4 us (2%)
    all_to_all x2, blocking collectives, transposed(): lax.all_to_all(sectioned, 'context', split_axis=3, concat_axis=2, tiled=T...  286 us
    all_to_all x1, waiting for transfers between devices, transposed(): lax.all_to_all(combine_rows(lax.all_to_all(sectioned, 'context', split_ax...  182 us
    dot_general x8, matrix products, along_rows(): jnp.einsum('kj,tjc->tkc', table, block, precision=lax.Precision.HIGHEST)  108 us
    all_to_all x1, blocking collectives, transposed(): lax.all_to_all(combine_rows(lax.all_to_all(sectioned, 'context', split_ax...  96.5 us
    unnamed x21, local copies, waits for them, and re-layouts  24.8 us
    all_gather x1, waiting for transfers between devices, local(): lax.all_gather(tokens, 'tensor', axis=0, tiled=True).astype(jnp.float32)  21.8 us
  transfers between devices with their start and end apart: 3, of which 3 were waited for; matrix products, arithmetic and copies ran while one was open for 2% of the time, Pallas kernels for 0%

commit v1 on v0

v1 whole, which is shorter than its diff:
```python
import functools
import math

import jax
import jax.numpy as jnp
import numpy as np
from jax import lax
from jax.experimental import pallas as pl
from jax.experimental.pallas import tpu as pltpu
from jax.sharding import PartitionSpec as P

eps = 1e-06

FINE = 256
HALF = 64
LANES = 2 * HALF
PAD = 16
BIG = 60 * 1024 * 1024

f32 = jnp.float32
bf16 = jnp.bfloat16


def lane_mask():
    return lax.broadcasted_iota(jnp.int32, (1, LANES), 1) < HALF


def pack_pair(tile):
    low = lane_mask()
    top, bot = tile[:FINE], tile[FINE:]
    return (
        jnp.where(low, top, pltpu.roll(bot, HALF, 1)),
        jnp.where(low, pltpu.roll(top, HALF, 1), bot),
    )


def unpack_pair(first, second):
    low = lane_mask()
    return (
        jnp.where(low, first, pltpu.roll(second, HALF, 1)),
        jnp.where(low, pltpu.roll(first, HALF, 1), second),
    )


def pack_kernel(in_ref, out_ref):
    first, second = pack_pair(in_ref[...])
    out_ref[0] = first.astype(bf16)
    out_ref[1] = second.astype(bf16)


def pack_filter(filt):
    length, channels = filt.shape
    return pl.pallas_call(
        pack_kernel,
        grid=(channels // LANES,),
        in_specs=[pl.BlockSpec((length, LANES), lambda i: (0, i))],
        out_specs=pl.BlockSpec((2, FINE, LANES), lambda i: (i, 0, 0)),
        out_shape=jax.ShapeDtypeStruct((channels // HALF, FINE, LANES), bf16),
        name="pack_filter",
    )(filt)


def pack_any(rows, dev_count):
    length, channels = rows.shape
    each = channels // dev_count
    blocks = rows.astype(bf16).reshape(2, FINE, dev_count, each)
    blocks = jnp.transpose(blocks, (2, 1, 0, 3))
    blocks = jnp.pad(blocks, ((0, 0), (0, 0), (0, 0), (0, HALF - each)))
    return blocks.reshape(dev_count, FINE, LANES)


def project_kernel(taps, me_ref, halo_hbm, *refs):
    blocks = refs[:taps]
    w_ref, tap_ref, q_ref, g_ref, p_ref, x_ref, rows_ref, key_ref, sem = refs[taps:]
    part = pl.program_id(1)
    me = me_ref[0]
    each = blocks[0].shape[0]
    length = each * taps

    @pl.when((pl.program_id(0) == 0) & (part == 0))
    def _():
        copies = [pltpu.make_async_copy(halo_hbm, x_ref.at[pl.ds(0, PAD)], sem.at[taps])]
        for mask, block in enumerate(blocks):
            first = pl.multiple_of(PAD + (me ^ mask) * each, 16)
            copies.append(pltpu.make_async_copy(block, x_ref.at[pl.ds(first, each)], sem.at[mask]))
        for copy in copies:
            copy.start()
        for copy in copies:
            copy.wait()

    rows_ref[...] = jnp.dot(x_ref[...], w_ref[0], preferred_element_type=f32)

    def mixed(s):
        total = tap_ref[0, s][None, :] * rows_ref[PAD : PAD + length]
        for lag in (1, 2):
            total += tap_ref[lag, s][None, :] * rows_ref[PAD - lag : PAD - lag + length]
        return total

    @pl.when(part == 0)
    def _():
        q_ref[...] = mixed(0)

    @pl.when(part == 1)
    def _():
        key_ref[...] = mixed(1)

    @pl.when(part == 2)
    def _():
        gated = key_ref[...] * mixed(2)
        g_ref[...] = gated
        for i in range(gated.shape[1] // LANES):
            first, second = pack_pair(gated[:, i * LANES : (i + 1) * LANES])
            p_ref[2 * i] = first.astype(bf16)
            p_ref[2 * i + 1] = second.astype(bf16)


def project(me, halo, blocks, weight, taps):
    _, width, channels = weight.shape
    each = blocks[0].shape[0]
    length = each * len(blocks)
    cols = min(256, channels)
    flops = 2 * (length + PAD) * width * 3 * channels
    return pl.pallas_call(
        functools.partial(project_kernel, len(blocks)),
        grid_spec=pltpu.PrefetchScalarGridSpec(
            num_scalar_prefetch=1,
            grid=(channels // cols, 3),
            in_specs=[pl.BlockSpec(memory_space=pl.ANY)] * (1 + len(blocks))
            + [
                pl.BlockSpec((1, width, cols), lambda j, s, me: (s, 0, j)),
                pl.BlockSpec((3, 3, cols), lambda j, s, me: (0, 0, j)),
            ],
            out_specs=[
                pl.BlockSpec((length, cols), lambda j, s, me: (0, j)),
                pl.BlockSpec((length, cols), lambda j, s, me: (0, j)),
                pl.BlockSpec((cols // HALF, FINE, LANES), lambda j, s, me: (j, 0, 0)),
            ],
            scratch_shapes=[
                pltpu.VMEM((PAD + length, width), bf16),
                pltpu.VMEM((PAD + length, cols), f32),
                pltpu.VMEM((length, cols), f32),
                pltpu.SemaphoreType.DMA((len(blocks) + 1,)),
            ],
        ),
        out_shape=[
            jax.ShapeDtypeStruct((length, channels), f32),
            jax.ShapeDtypeStruct((length, channels), f32),
            jax.ShapeDtypeStruct((channels // HALF, FINE, LANES), bf16),
        ],
        compiler_params=pltpu.CompilerParams(vmem_limit_bytes=40 * 1024 * 1024),
        cost_estimate=pl.CostEstimate(
            flops=flops, bytes_accessed=2 * 3 * width * channels + 8 * length * channels, transcendentals=0
        ),
        name="project",
    )(me, halo, *blocks, weight, taps)


def coarse_forward(dev_count, x_ref, lane_ref, e_ref, step=16):
    count = dev_count
    half = count // 2
    low = lane_mask()
    sgn = jnp.where(low, 1.0, -1.0).astype(f32)

    def body(i, carry):
        rows = pl.ds(pl.multiple_of(i * step, step), step)
        x = [x_ref[s, rows, :].astype(f32) for s in range(count)]
        plus = [x[s] + x[count - s] for s in range(1, half)]
        minus = [x[s] - x[count - s] for s in range(1, half)]
        for k in range(count + 1):
            even = k % 2 == 0
            re = x[0]
            im = None
            mid = round(math.cos(math.pi * half * k / count))
            if mid:
                re = re + x[half] if mid > 0 else re - x[half]
            mid = round(math.sin(math.pi * half * k / count))
            if mid:
                im = -x[half] if mid > 0 else x[half]
            for s in range(1, half):
                c, d = math.cos(math.pi * s * k / count), math.sin(math.pi * s * k / count)
                if abs(c) > 1e-9:
                    re = re + c * (plus if even else minus)[s - 1]
                if abs(d) > 1e-9:
                    term = (-d) * (minus if even else plus)[s - 1]
                    im = term if im is None else im + term
            c, d = lane_ref[k, 0:1, :], lane_ref[k, 1:2, :]
            if im is None:
                re, im = re * c, re * (-d)
            else:
                re, im = re * c + im * d, im * c - re * d
            e_ref[k, rows, :LANES] = pltpu.roll(re, HALF, 1) + sgn * re
            e_ref[k, rows, LANES:] = sgn * pltpu.roll(im, HALF, 1) + im
        return carry

    lax.fori_loop(0, FINE // step, body, 0)


def coarse_inverse(dev_count, g_ref, y_ref, step=16):
    count = dev_count
    half = count // 2

    def body(i, carry):
        rows = pl.ds(pl.multiple_of(i * step, step), step)
        acc = {}

        def add(name, s, term):
            acc[name, s] = term if (name, s) not in acc else acc[name, s] + term

        for k in range(count + 1):
            even = k % 2 == 0
            re, im = g_ref[k, rows, :LANES], g_ref[k, rows, LANES:]
            add("first", 0, re)
            mid = round(math.cos(math.pi * half * k / count))
            if mid:
                add("mid", 0, re if mid > 0 else -re)
            mid = round(math.sin(math.pi * half * k / count))
            if mid:
                add("mid", 0, -im if mid > 0 else im)
            for s in range(1, half):
                c, d = math.cos(math.pi * s * k / count), math.sin(math.pi * s * k / count)
                if abs(c) > 1e-9:
                    add("a" if even else "b", s, c * re)
                if abs(d) > 1e-9:
                    add("b" if even else "a", -s, (-d) * im)
        y_ref[0, rows, :] = acc["first", 0].astype(bf16)
        y_ref[half, rows, :] = acc["mid", 0].astype(bf16)
        zero = jnp.zeros((step, LANES), f32)
        for s in range(1, half):
            same = acc.get(("a", s), zero)
            flip = acc.get(("b", s), zero)
            same_sin = acc.get(("a", -s), zero)
            flip_sin = acc.get(("b", -s), zero)
            total, diff = same + same_sin, flip + flip_sin
            y_ref[s, rows, :] = (total + diff).astype(bf16)
            y_ref[count - s, rows, :] = (total - diff).astype(bf16)
        return carry

    lax.fori_loop(0, FINE // step, body, 0)


def fine_forward(e, tr, ti, table):
    re, im = e[:, :LANES], e[:, LANES:]
    turned = jnp.concatenate([re * tr - im * ti, re * ti + im * tr], axis=1).astype(bf16)
    both = jnp.dot(table, turned, preferred_element_type=f32)
    return (
        both[:FINE, :LANES] - both[FINE:, LANES:],
        both[:FINE, LANES:] + both[FINE:, :LANES],
    )


def next_turn(turn_ref, step_ref):
    tr, ti = turn_ref[:, :LANES], turn_ref[:, LANES:]
    sr, si = step_ref[:, :LANES], step_ref[:, LANES:]
    turn_ref[:, :LANES] = tr * sr - ti * si
    turn_ref[:, LANES:] = tr * si + ti * sr


def filter_kernel(dev_count, x_ref, first_ref, step_ref, lane_ref, table_ref, h_ref, e_ref, turn_ref):
    coarse_forward(dev_count, x_ref, lane_ref, e_ref)
    turn_ref[...] = first_ref[...]
    points = 4 * dev_count * FINE

    def body(k, carry):
        re, im = fine_forward(e_ref[k], turn_ref[:, :LANES], turn_ref[:, LANES:], table_ref[...])
        scale = jnp.where((k == 0) | (k == dev_count), 1.0 / points, 2.0 / points).astype(f32)
        h_ref[k, :, :LANES] = re * scale
        h_ref[k, :, LANES:] = im * scale
        next_turn(turn_ref, step_ref)
        return carry

    lax.fori_loop(0, dev_count + 1, body, 0, unroll=dev_count <= 8)


def conv_kernel(dev_count, x_ref, h_hbm, first_ref, step_ref, lane_ref, table_ref, y_ref, h_ref, e_ref, turn_ref, sem):
    copy = pltpu.make_async_copy(h_hbm, h_ref, sem)
    copy.start()
    coarse_forward(dev_count, x_ref, lane_ref, e_ref)
    turn_ref[...] = first_ref[...]
    sgn = jnp.where(lane_mask(), 1.0, -1.0).astype(f32)
    copy.wait()

    def body(k, carry):
        tr, ti = turn_ref[:, :LANES], turn_ref[:, LANES:]
        re, im = fine_forward(e_ref[k], tr, ti, table_ref[...])
        hr, hi = h_ref[k, :, :LANES], h_ref[k, :, LANES:]
        prod = jnp.concatenate([re * hr - im * hi, re * hi + im * hr], axis=1).astype(bf16)
        both = jnp.dot(table_ref[...], prod, preferred_element_type=f32)
        re = both[:FINE, :LANES] + both[FINE:, LANES:]
        im = both[:FINE, LANES:] - both[FINE:, :LANES]
        re, im = re * tr + im * ti, (im * tr - re * ti) * sgn
        re, im = pltpu.roll(re, HALF, 1) + sgn * re, pltpu.roll(im, HALF, 1) + sgn * im
        c, d = lane_ref[k, 0:1, :], lane_ref[k, 1:2, :]
        e_ref[k, :, :LANES] = re * c - im * d
        e_ref[k, :, LANES:] = re * d + im * c
        next_turn(turn_ref, step_ref)
        return carry

    lax.fori_loop(0, dev_count + 1, body, 0, unroll=dev_count <= 8)
    coarse_inverse(dev_count, e_ref, y_ref)


def tables(dev_count):
    points = 4 * dev_count * FINE
    fine = np.arange(FINE)
    first = np.exp(-2j * np.pi * fine * (2 * dev_count) / points)[:, None] * np.ones(HALF)
    ones = np.ones((FINE, HALF))
    step = np.exp(-2j * np.pi * fine / points)[:, None] * ones
    first = np.concatenate([ones, first.real, 0 * ones, first.imag], axis=1)
    step = np.concatenate([step.real, step.real, step.imag, -step.imag], axis=1)
    turn = 2 * np.pi * np.arange(dev_count + 1)[:, None] * np.ones(HALF) / (4 * dev_count)
    lane = np.stack(
        [
            np.concatenate([np.ones_like(turn), np.cos(turn)], axis=1),
            np.concatenate([np.zeros_like(turn), np.sin(turn)], axis=1),
        ],
        axis=1,
    )
    angle = -2 * np.pi * (fine[:, None] * fine[None, :] % FINE) / FINE
    table = np.concatenate([np.cos(angle), np.sin(angle)], axis=0)
    return (
        jnp.asarray(first, f32),
        jnp.asarray(step, f32),
        jnp.asarray(lane, f32),
        jnp.asarray(table, bf16),
    )


VMEM_SPEC = pl.BlockSpec(memory_space=pltpu.VMEM)


def filter_spectrum(x, consts):
    dev_count = x.shape[0]
    return pl.pallas_call(
        functools.partial(filter_kernel, dev_count),
        in_specs=[VMEM_SPEC] * 5,
        out_specs=VMEM_SPEC,
        out_shape=jax.ShapeDtypeStruct((dev_count + 1, FINE, 2 * LANES), f32),
        scratch_shapes=[
            pltpu.VMEM((dev_count + 1, FINE, 2 * LANES), f32),
            pltpu.VMEM((FINE, 2 * LANES), f32),
        ],
        compiler_params=pltpu.CompilerParams(vmem_limit_bytes=BIG),
        name="filter_spectrum",
    )(x, *consts)


def convolve(x, spectrum, consts):
    dev_count = x.shape[0]
    return pl.pallas_call(
        functools.partial(conv_kernel, dev_count),
        in_specs=[VMEM_SPEC, pl.BlockSpec(memory_space=pl.ANY)] + [VMEM_SPEC] * 4,
        out_specs=VMEM_SPEC,
        out_shape=jax.ShapeDtypeStruct((dev_count, FINE, LANES), bf16),
        scratch_shapes=[
            pltpu.VMEM((dev_count + 1, FINE, 2 * LANES), f32),
            pltpu.VMEM((dev_count + 1, FINE, 2 * LANES), f32),
            pltpu.VMEM((FINE, 2 * LANES), f32),
            pltpu.SemaphoreType.DMA,
        ],
        compiler_params=pltpu.CompilerParams(vmem_limit_bytes=BIG),
        name="convolve",
    )(x, spectrum, *consts)


def finish_kernel(c_ref, q_ref, g_ref, skip_ref, out_ref):
    top, bot = unpack_pair(c_ref[0].astype(f32), c_ref[1].astype(f32))
    for i, conv in enumerate((top, bot)):
        rows = slice(i * FINE, (i + 1) * FINE)
        out_ref[rows, :] = (q_ref[rows, :] * (conv + skip_ref[...] * g_ref[rows, :])).astype(bf16)


def finish(conv, query, gated, skip_gain):
    length, channels = query.shape
    tile = pl.BlockSpec((length, LANES), lambda i: (0, i))
    return pl.pallas_call(
        finish_kernel,
        grid=(channels // LANES,),
        in_specs=[
            pl.BlockSpec((2, FINE, LANES), lambda i: (i, 0, 0)),
            tile,
            tile,
            pl.BlockSpec((1, LANES), lambda i: (0, i)),
        ],
        out_specs=tile,
        out_shape=jax.ShapeDtypeStruct((length, channels), bf16),
        name="finish",
    )(conv, query, gated, skip_gain.reshape(1, channels))


def local(tokens, norm_gain, in_weight, short_weight, long_filter, skip_gain):
    dev_count = lax.axis_size("context")
    tensor_count = lax.axis_size("tensor")
    channels = in_weight.shape[2]
    packed = channels // dev_count == HALF
    consts = tables(dev_count)

    values = tokens.astype(f32)
    inv_rms = lax.rsqrt(jnp.mean(values * values, axis=1, keepdims=True) + eps)
    normed = (values * inv_rms * norm_gain).astype(bf16)

    blocks = {0: normed}
    bit = tensor_count // 2
    while bit:
        pairs = [(i, i ^ bit) for i in range(tensor_count)]
        for mask in list(blocks):
            blocks[mask | bit] = lax.ppermute(blocks[mask], "tensor", pairs)
        bit //= 2
    blocks = [blocks[mask] for mask in range(tensor_count)]

    tail = normed[-8:]
    halo = jnp.zeros_like(tail)
    last = tensor_count - 1
    for t in range(tensor_count):
        pairs = [(c * tensor_count + last, (c + 1) * tensor_count + t) for c in range(dev_count - 1)]
        halo = halo + lax.ppermute(tail, ("context", "tensor"), pairs)
    halo = jnp.concatenate([jnp.zeros((PAD - 8, halo.shape[1]), bf16), halo], axis=0)

    exchange = functools.partial(
        lax.all_to_all, axis_name="context", split_axis=0, concat_axis=0, tiled=True
    )
    filt = exchange(pack_filter(long_filter) if packed else pack_any(long_filter, dev_count))
    spectrum = filter_spectrum(filt, consts)

    me = lax.axis_index("tensor").astype(jnp.int32).reshape(1)
    query, gated, sent = project(me, halo, blocks, jnp.transpose(in_weight, (1, 0, 2)), short_weight)
    if not packed:
        sent = pack_any(gated, dev_count)
    conv = exchange(convolve(exchange(sent), spectrum, consts))
    if packed:
        return finish(conv, query, gated, skip_gain)
    each = channels // dev_count
    conv = conv.reshape(dev_count, FINE, 2, HALF)[..., :each]
    conv = jnp.transpose(conv, (2, 1, 0, 3)).reshape(2 * FINE, channels).astype(f32)
    return (query * (conv + skip_gain * gated)).astype(bf16)


def solution(mesh):
    return jax.shard_map(
        local,
        mesh=mesh,
        in_specs=(
            P(("context", "tensor"), None),
            P(),
            P(None, None, "tensor"),
            P(None, None, "tensor"),
            P("context", "tensor"),
            P("tensor"),
        ),
        out_specs=P("context", "tensor"),
        check_vma=False,
    )
```

time: 865 us -> 109 us (0.13)
  the two profiles are of different devices: /device:TPU:0 before, /device:TPU:3 now
where the time goes in v1:
time: 109 us; the launch traced here: 108 us
  Pallas kernels  33.1 us (30%)
  waiting for transfers between devices  29.3 us (27%)
  starting transfers between devices  21.1 us (19%)
  blocking collectives  18.6 us (17%)
  other arithmetic  3.1 us (3%)
  local copies, waits for them, and re-layouts  2.75 us (3%)
    ppermute x3, waiting for transfers between devices, local(): blocks[mask | bit] = lax.ppermute(blocks[mask], 'tensor', pairs)  23.3 us
    all_to_all x1, blocking collectives, local(): conv = exchange(convolve(exchange(sent), spectrum, consts))  18.6 us
    pallas_call x1, Pallas kernels, project(): pl.pallas_call(functools.partial(project_kernel, len(blocks)), grid_spec=...  13.5 us
    ppermute x4, starting transfers between devices, local(): halo = halo + lax.ppermute(tail, ('context', 'tensor'), pairs)  8.74 us
    pallas_call x1, Pallas kernels, convolve(): pl.pallas_call(functools.partial(conv_kernel, dev_count), in_specs=[VMEM_...  6.74 us
    all_to_all x1, waiting for transfers between devices, local(): conv = exchange(convolve(exchange(sent), spectrum, consts))  6.06 us
    pallas_call x1, Pallas kernels, filter_spectrum(): pl.pallas_call(functools.partial(filter_kernel, dev_count), in_specs=[VME...  5.61 us
    all_to_all x1, starting transfers between devices, local(): conv = exchange(convolve(exchange(sent), spectrum, consts))  5.43 us
  transfers between devices with their start and end apart: 9, of which 2 were waited for; matrix products, arithmetic and copies ran while one was open for 0% of the time, Pallas kernels for 21%

profile of v1, /device:TPU:3, one launch (start us, length us, event | category | flops | bytes accessed | tf_op | source)
XLA Modules:
  0.0 108.1 jit_solution(3001337433441663423)
XLA Ops:
  0.0 1.5 %fusion = f32[128]{0:T(128)S(1)} fusion(bf16[128,4096]{1,0:T(8,128)(2,1)} %param.10), kind=kLoop, calls=%fused_computation.2 | loop fusion | flops 1572736 | bytes 1049088 | tf_op jit(solution)/shard_map/reduce_sum | solution.py:398
  1.5 1.6 %fusion.2.refs_0_ = bf16[128,4096]{1,0:T(8,128)(2,1)S(1)} fusion(bf16[128,4096]{1,0:T(8,128)(2,1)} %param.10, f32[4096]{0:T(1024)} %param.11, f32[128]{0:T(128)S(1)} %add_rsqrt_fusion), kind=kLoop, calls=%fused_computation.4 | loop fusion | flops 2097152 | bytes 2114048 | tf_op jit(solution)/shard_map/convert_element_type | solution.py:399
  3.1 0.0 copy-start.2
  3.1 0.1 collective-permute-start.5
  3.2 0.7 collective-permute-start.4
  3.9 23.3 %collective-permute-done.5.refs_2_ = bf16[128,4096]{1,0:T(8,128)(2,1)S(1)} collective-permute-done((bf16[128,4096]{1,0:T(8,128)(2,1)S(1)}, bf16[128,4096]{1,0:T(8,128)(2,1)S(1)}, u32[]{:S(2)}, u32[]{:S(2)}) %collective-permute-start.5) | collective-permute-done | bytes 1048608 | tf_op jit(solution)/shard_map/ppermute | solution.py:406
  27.2 1.5 %collective-permute-start.6 = (bf16[128,4096]{1,0:T(8,128)(2,1)S(1)}, bf16[128,4096]{1,0:T(8,128)(2,1)}, u32[]{:S(2)}, u32[]{:S(2)}) collective-permute-start(bf16[128,4096]{1,0:T(8,128)(2,1)S(1)} %collective-permute-done.5.refs_2_), channel_id=1, source_target_pairs={{0,1},{1,0},{2,3},{3,2},{4,5},{5,4},{6,7},{7,6},{8,9},{9,8},{10,11... | collective-permute-start | bytes 3145736 | tf_op jit(solution)/shard_map/ppermute | solution.py:406
  28.7 3.0 %collective-permute-start = (bf16[8,4096]{1,0:T(8,128)(2,1)S(1)}, bf16[8,4096]{1,0:T(8,128)(2,1)S(1)}, u32[]{:S(2)}, u32[]{:S(2)}) collective-permute-start(bf16[8,4096]{1,0:T(8,128)(2,1)S(1)} %slice.4), channel_id=1, source_target_pairs={{3,4},{7,8},{11,12},{15,16},{19,20},{23,24},{27,28}} | collective-permute-start | bytes 196616 | tf_op jit(solution)/shard_map/ppermute | solution.py:415
  31.8 1.3 %collective-permute-start.1 = (bf16[8,4096]{1,0:T(8,128)(2,1)S(1)}, bf16[8,4096]{1,0:T(8,128)(2,1)S(1)}, u32[]{:S(2)}, u32[]{:S(2)}) collective-permute-start(bf16[8,4096]{1,0:T(8,128)(2,1)S(1)} %slice.4), channel_id=1, source_target_pairs={{3,5},{7,9},{11,13},{15,17},{19,21},{23,25},{27,29}} | collective-permute-start | bytes 196616 | tf_op jit(solution)/shard_map/ppermute | solution.py:415
  33.1 1.3 %collective-permute-start.2 = (bf16[8,4096]{1,0:T(8,128)(2,1)S(1)}, bf16[8,4096]{1,0:T(8,128)(2,1)S(1)}, u32[]{:S(2)}, u32[]{:S(2)}) collective-permute-start(bf16[8,4096]{1,0:T(8,128)(2,1)S(1)} %slice.4), channel_id=1, source_target_pairs={{3,6},{7,10},{11,14},{15,18},{19,22},{23,26},{27,30}} | collective-permute-start | bytes 196616 | tf_op jit(solution)/shard_map/ppermute | solution.py:415
  34.4 0.0 collective-permute-done
  34.4 3.1 %collective-permute-start.3 = (bf16[8,4096]{1,0:T(8,128)(2,1)S(1)}, bf16[8,4096]{1,0:T(8,128)(2,1)S(1)}, u32[]{:S(2)}, u32[]{:S(2)}) collective-permute-start(bf16[8,4096]{1,0:T(8,128)(2,1)S(1)} %slice.4), channel_id=1, source_target_pairs={{3,7},{7,11},{11,15},{15,19},{19,23},{23,27},{27,31}} | collective-permute-start | bytes 196616 | tf_op jit(solution)/shard_map/ppermute | solution.py:415
  37.5 3.4 %pack_filter.1 = bf16[8,256,128]{2,1,0:T(8,128)(2,1)} custom-call(f32[512,512]{1,0:T(8,128)} %in_ref.1), custom_call_target="tpu_custom_call" | custom-call | tf_op jit(solution)/shard_map/pack_filter/pallas_call | solution.py:53
  41.0 4.5 %all-to-all-start.1 = ((bf16[8,256,128]{2,1,0:T(8,128)(2,1)}), bf16[8,256,128]{2,1,0:T(8,128)(2,1)}, u32[]{:S(2)}, u32[]{:S(2)}) async-start(bf16[8,256,128]{2,1,0:T(8,128)(2,1)} %pack_filter.1), calls=%async_computation.1 | async-start | bytes 1048576 | tf_op jit(solution)/shard_map/all_to_all | solution.py:421
  45.5 0.0 collective-permute-done.1
  45.5 0.0 collective-permute-done.2
  45.5 0.0 collective-permute-done.3
  45.6 0.0 collective-permute-done.4.refs_1_
  45.6 0.0 collective-permute-done.6.refs_3_
  45.6 0.0 copy-done.2
  45.6 13.5 %project.1 = (f32[512,512]{1,0:T(8,128)S(1)}, f32[512,512]{1,0:T(8,128)S(1)}, bf16[8,256,128]{2,1,0:T(8,128)(2,1)}) custom-call(s32[1]{0:T(128)} %bitcast.me_ref, bf16[16,4096]{1,0:T(8,128)(2,1)S(1)} %concatenate.3.halo_hbm, bf16[128,4096]{1,0:T(8,128)(2,1)S(1)} %fusion.2.refs_0_, bf16[128,4096]{1,0:T(8,128)(2,1)S(1)} %collective-permute-done.4.refs_1_, ...), custom_call_target="tpu_custom_call" | custom-call | flops 6643777536 | bytes 14680064 | tf_op jit(solution)/shard_map/project/pallas_call | solution.py:123
  59.1 0.0 copy-start
  59.2 1.0 copy-done
  60.1 0.0 copy-start.1
  60.1 1.0 copy-done.1
  61.1 0.0 all-to-all-done.1.x_ref
  61.1 5.4 %all-to-all-start = ((bf16[8,256,128]{2,1,0:T(8,128)(2,1)}), bf16[8,256,128]{2,1,0:T(8,128)(2,1)S(1)}, u32[]{:S(2)}, u32[]{:S(2)}) async-start(bf16[8,256,128]{2,1,0:T(8,128)(2,1)} %get-tuple-element.8), calls=%async_computation | async-start | bytes 1048576 | tf_op jit(solution)/shard_map/all_to_all | solution.py:428
  66.5 5.6 %filter_spectrum.1.h_hbm = f32[9,256,256]{2,1,0:T(8,128)} custom-call(bf16[8,256,128]{2,1,0:T(8,128)(2,1)} %all-to-all-done.1.x_ref, f32[256,256]{1,0:T(8,128)} %constant.21.clone.first_ref, f32[256,256]{1,0:T(8,128)} %constant.22.clone.step_ref, f32[9,2,128]{2,1,0:T(2,128)} %constant.23.clone.lane_ref, bf16[512,256]{1,0:T(8,128)(2,1)} %constant.24.clone.table_ref), custom_call_target="tpu_custom_call" | custom-call | tf_op jit(solution)/shard_map/filter_spectrum/pallas_call | solution.py:333
  72.1 6.1 %all-to-all-done.x_ref = bf16[8,256,128]{2,1,0:T(8,128)(2,1)S(1)} async-done(((bf16[8,256,128]{2,1,0:T(8,128)(2,1)}), bf16[8,256,128]{2,1,0:T(8,128)(2,1)S(1)}, u32[]{:S(2)}, u32[]{:S(2)}) %all-to-all-start) | async-done | bytes 524320 | tf_op jit(solution)/shard_map/all_to_all | solution.py:428
  78.2 0.0 copy-start.3
  78.2 0.8 copy-done.3
  79.0 6.7 %convolve.1 = bf16[8,256,128]{2,1,0:T(8,128)(2,1)} custom-call(bf16[8,256,128]{2,1,0:T(8,128)(2,1)} %copy-done.3, f32[9,256,256]{2,1,0:T(8,128)} %filter_spectrum.1.h_hbm, f32[256,256]{1,0:T(8,128)} %constant.21.clone.first_ref, f32[256,256]{1,0:T(8,128)} %constant.22.clone.step_ref, f32[9,2,128]{2,1,0:T(2,128)} %constant.23.clone.lane_ref, ...), custom_call_target="tpu_custom_call" | custom-call | tf_op jit(solution)/shard_map/convolve/pallas_call | solution.py:349
  85.7 18.6 %all_to_all.15.c_ref = bf16[8,256,128]{2,1,0:T(8,128)(2,1)} all-to-all(bf16[8,256,128]{2,1,0:T(8,128)(2,1)} %convolve.1), channel_id=1, replica_groups=mesh['context'=8,'tensor'=4] {'context'}, dimensions={0} | all-to-all | bytes 1048576 | tf_op jit(solution)/shard_map/all_to_all | solution.py:428
  104.3 3.8 %finish.1 = bf16[512,512]{1,0:T(8,128)(2,1)} custom-call(bf16[8,256,128]{2,1,0:T(8,128)(2,1)} %all_to_all.15.c_ref, f32[512,512]{1,0:T(8,128)} %copy-done, f32[512,512]{1,0:T(8,128)} %copy-done.1, f32[1,512]{1,0:T(1,128)} %bitcast.3), custom_call_target="tpu_custom_call" | custom-call | tf_op jit(solution)/shard_map/finish/pallas_call | solution.py:375
  (4 shorter events, 0.0 us)
Async XLA Ops:
  3.1 42.5 %copy-start.2 = (f32[3,3,512]{2,1,0:T(4,128)S(1)}, f32[3,3,512]{2,1,0:T(4,128)}, u32[]{:S(2)}) copy-start(f32[3,3,512]{2,1,0:T(4,128)} %refs_5_.1) | copy-start | bytes 55300
  3.1 24.1 %collective-permute-start.5 = (bf16[128,4096]{1,0:T(8,128)(2,1)S(1)}, bf16[128,4096]{1,0:T(8,128)(2,1)S(1)}, u32[]{:S(2)}, u32[]{:S(2)}) collective-permute-start(bf16[128,4096]{1,0:T(8,128)(2,1)S(1)} %fusion.2.refs_0_), channel_id=1, source_target_pairs={{0,2},{1,3},{2,0},{3,1},{4,6},{5,7},{6,4},{7,5},{8,10},{9,11},{10,... | collective-permute-start | bytes 3145736 | tf_op jit(solution)/shard_map/ppermute | solution.py:406
  3.2 42.4 %collective-permute-start.4 = (bf16[128,4096]{1,0:T(8,128)(2,1)S(1)}, bf16[128,4096]{1,0:T(8,128)(2,1)S(1)}, u32[]{:S(2)}, u32[]{:S(2)}) collective-permute-start(bf16[128,4096]{1,0:T(8,128)(2,1)S(1)} %fusion.2.refs_0_), channel_id=1, source_target_pairs={{0,1},{1,0},{2,3},{3,2},{4,5},{5,4},{6,7},{7,6},{8,9},{9,8},{10,11... | collective-permute-start | bytes 3145736 | tf_op jit(solution)/shard_map/ppermute | solution.py:406
  27.2 18.4 %collective-permute-start.6 = (bf16[128,4096]{1,0:T(8,128)(2,1)S(1)}, bf16[128,4096]{1,0:T(8,128)(2,1)}, u32[]{:S(2)}, u32[]{:S(2)}) collective-permute-start(bf16[128,4096]{1,0:T(8,128)(2,1)S(1)} %collective-permute-done.5.refs_2_), channel_id=1, source_target_pairs={{0,1},{1,0},{2,3},{3,2},{4,5},{5,4},{6,7},{7,6},{8,9},{9,8},{10,11... | collective-permute-start | bytes 3145736 | tf_op jit(solution)/shard_map/ppermute | solution.py:406
  28.7 5.6 %collective-permute-start = (bf16[8,4096]{1,0:T(8,128)(2,1)S(1)}, bf16[8,4096]{1,0:T(8,128)(2,1)S(1)}, u32[]{:S(2)}, u32[]{:S(2)}) collective-permute-start(bf16[8,4096]{1,0:T(8,128)(2,1)S(1)} %slice.4), channel_id=1, source_target_pairs={{3,4},{7,8},{11,12},{15,16},{19,20},{23,24},{27,28}} | collective-permute-start | bytes 196616 | tf_op jit(solution)/shard_map/ppermute | solution.py:415
  31.8 13.7 %collective-permute-start.1 = (bf16[8,4096]{1,0:T(8,128)(2,1)S(1)}, bf16[8,4096]{1,0:T(8,128)(2,1)S(1)}, u32[]{:S(2)}, u32[]{:S(2)}) collective-permute-start(bf16[8,4096]{1,0:T(8,128)(2,1)S(1)} %slice.4), channel_id=1, source_target_pairs={{3,5},{7,9},{11,13},{15,17},{19,21},{23,25},{27,29}} | collective-permute-start | bytes 196616 | tf_op jit(solution)/shard_map/ppermute | solution.py:415
  33.1 12.4 %collective-permute-start.2 = (bf16[8,4096]{1,0:T(8,128)(2,1)S(1)}, bf16[8,4096]{1,0:T(8,128)(2,1)S(1)}, u32[]{:S(2)}, u32[]{:S(2)}) collective-permute-start(bf16[8,4096]{1,0:T(8,128)(2,1)S(1)} %slice.4), channel_id=1, source_target_pairs={{3,6},{7,10},{11,14},{15,18},{19,22},{23,26},{27,30}} | collective-permute-start | bytes 196616 | tf_op jit(solution)/shard_map/ppermute | solution.py:415
  34.4 11.1 %collective-permute-start.3 = (bf16[8,4096]{1,0:T(8,128)(2,1)S(1)}, bf16[8,4096]{1,0:T(8,128)(2,1)S(1)}, u32[]{:S(2)}, u32[]{:S(2)}) collective-permute-start(bf16[8,4096]{1,0:T(8,128)(2,1)S(1)} %slice.4), channel_id=1, source_target_pairs={{3,7},{7,11},{11,15},{15,19},{19,23},{23,27},{27,31}} | collective-permute-start | bytes 196616 | tf_op jit(solution)/shard_map/ppermute | solution.py:415
  41.0 20.1 %all-to-all-start.1 = ((bf16[8,256,128]{2,1,0:T(8,128)(2,1)}), bf16[8,256,128]{2,1,0:T(8,128)(2,1)}, u32[]{:S(2)}, u32[]{:S(2)}) async-start(bf16[8,256,128]{2,1,0:T(8,128)(2,1)} %pack_filter.1), calls=%async_computation.1 | async-start | bytes 1048576 | tf_op jit(solution)/shard_map/all_to_all | solution.py:421
  59.1 1.0 copy-start
  60.1 1.0 copy-start.1
  61.1 17.1 %all-to-all-start = ((bf16[8,256,128]{2,1,0:T(8,128)(2,1)}), bf16[8,256,128]{2,1,0:T(8,128)(2,1)S(1)}, u32[]{:S(2)}, u32[]{:S(2)}) async-start(bf16[8,256,128]{2,1,0:T(8,128)(2,1)} %get-tuple-element.8), calls=%async_computation | async-start | bytes 1048576 | tf_op jit(solution)/shard_map/all_to_all | solution.py:428
  78.2 0.8 copy-start.3

commit v2 on v1

v2 whole, which is shorter than its diff:
```python
import functools
import math

import jax
import jax.numpy as jnp
import numpy as np
from jax import lax
from jax.experimental import pallas as pl
from jax.experimental.pallas import tpu as pltpu
from jax.sharding import PartitionSpec as P

eps = 1e-06

FINE = 256
HALF = 64
LANES = 2 * HALF
TAIL = 8
PAD = 16
BIG = 60 * 1024 * 1024
COST = (10**8, 10**8, 10**8)

VMEM_SPEC = pl.BlockSpec(memory_space=pltpu.VMEM)
HBM_SPEC = pl.BlockSpec(memory_space=pltpu.HBM)
ANY_SPEC = pl.BlockSpec(memory_space=pl.ANY)

f32 = jnp.float32
bf16 = jnp.bfloat16


def lane_mask():
    return lax.broadcasted_iota(jnp.int32, (1, LANES), 1) < HALF


def pack_pair(tile):
    low = lane_mask()
    rows = tile.shape[0] // 2
    top, bot = tile[:rows], tile[rows:]
    return (
        jnp.where(low, top, pltpu.roll(bot, HALF, 1)),
        jnp.where(low, pltpu.roll(top, HALF, 1), bot),
    )


def unpack_pair(first, second):
    low = lane_mask()
    return (
        jnp.where(low, first, pltpu.roll(second, HALF, 1)),
        jnp.where(low, pltpu.roll(first, HALF, 1), second),
    )


def start_all(copies):
    copies = [pltpu.make_async_copy(*copy) for copy in copies]
    for copy in copies:
        copy.start()
    return copies


def pack_any(rows, dev_count):
    length, channels = rows.shape
    each = channels // dev_count
    blocks = rows.astype(bf16).reshape(2, length // 2, dev_count, each)
    blocks = jnp.transpose(blocks, (2, 1, 0, 3))
    blocks = jnp.pad(blocks, ((0, 0), (0, 0), (0, 0), (0, HALF - each)))
    return blocks.reshape(dev_count, length // 2, LANES)


def norm_rows(tokens, gain):
    rows, width = tokens.shape
    step = min(32, rows)

    def kernel(tok_hbm, gain_hbm, out_ref, tail_ref, tok_ref, gain_ref, sem):
        parts = [pl.ds(i * step, step) for i in range(rows // step)]
        copies = start_all(
            [(gain_hbm, gain_ref, sem.at[len(parts)])]
            + [(tok_hbm.at[part], tok_ref.at[part], sem.at[i]) for i, part in enumerate(parts)]
        )
        copies[0].wait()
        for part, copy in zip(parts, copies[1:]):
            copy.wait()
            values = tok_ref[part, :].astype(f32)
            inv_rms = lax.rsqrt(jnp.mean(values * values, axis=1, keepdims=True) + eps)
            normed = (values * inv_rms * gain_ref[...]).astype(bf16)
            out_ref[part, :] = normed
            tail_ref[...] = normed[step - TAIL :]

    return pl.pallas_call(
        kernel,
        in_specs=[HBM_SPEC] * 2,
        out_specs=[VMEM_SPEC] * 2,
        out_shape=[jax.ShapeDtypeStruct((rows, width), bf16), jax.ShapeDtypeStruct((TAIL, width), bf16)],
        scratch_shapes=[
            pltpu.VMEM((rows, width), bf16),
            pltpu.VMEM((1, width), f32),
            pltpu.SemaphoreType.DMA((rows // step + 1,)),
        ],
        compiler_params=pltpu.CompilerParams(vmem_limit_bytes=BIG),
        name="norm_rows",
    )(tokens, gain.reshape(1, width))


def pack_into(p_ref, at, rows_ref):
    rows = pl.ds(at, rows_ref.shape[0] // 2)
    for i in range(p_ref.shape[0] // 2):
        first, second = pack_pair(rows_ref[:, i * LANES : (i + 1) * LANES])
        p_ref[2 * i, rows, :] = first.astype(bf16)
        p_ref[2 * i + 1, rows, :] = second.astype(bf16)


def project_kernel(count, parts, splits, with_filter, me_ref, halo_any, *refs):
    blocks = refs[:count]
    w_hbm, tap_hbm = refs[count : count + 2]
    outs = list(refs[count + 2 : -8])
    w_ref, tap_ref, x_ref, rows_ref, filt_ref, sem, w_sem, tap_sem = refs[-8:]
    each = blocks[0].shape[0]
    length = each * count
    width = x_ref.shape[1]
    depth = width // splits

    sources = [(halo_any, x_ref.at[pl.ds(0, PAD)], sem.at[count])]
    for mask, block in enumerate(blocks):
        first = pl.multiple_of(PAD + (me_ref[0] ^ mask) * each, 16)
        sources.append((block, x_ref.at[pl.ds(first, each)], sem.at[mask]))
    waits = start_all(sources + [(tap_hbm, tap_ref, tap_sem)])
    loads = {}
    for at, s in enumerate(parts):
        for i in range(splits):
            chunk = pl.ds(i * depth, depth)
            loads[s, i] = start_all([(w_hbm.at[s, chunk], w_ref.at[at, chunk], w_sem.at[at, i])])[0]
    if with_filter:
        filt_hbm, outs = outs[0], outs[1:]
        filt_load = start_all([(filt_hbm, filt_ref, sem.at[count + 1])])[0]
    for wait in waits:
        wait.wait()

    def mixed(s):
        at = parts.index(s)
        total = None
        for i in range(splits):
            loads[s, i].wait()
            chunk = slice(i * depth, (i + 1) * depth)
            term = jnp.dot(x_ref[:, chunk], w_ref[at, chunk], preferred_element_type=f32)
            total = term if total is None else total + term
        rows_ref[...] = total
        total = tap_ref[0, s : s + 1] * rows_ref[PAD : PAD + length]
        for lag in (1, 2):
            total += tap_ref[lag, s : s + 1] * rows_ref[PAD - lag : PAD - lag + length]
        return total

    if 1 in parts:
        g_ref, p_ref = outs[:2]
        g_ref[...] = mixed(1)
        g_ref[...] *= mixed(2)
        pack_into(p_ref, 0, g_ref)
    if 0 in parts:
        outs[-1][...] = mixed(0)
    if with_filter:
        filt_load.wait()
        pack_into(p_ref, length // 2, filt_ref)


def project(parts, me, halo, blocks, weight, taps, cost, filt=None):
    _, width, channels = weight.shape
    length = blocks[0].shape[0] * len(blocks)
    splits = 2
    shapes = []
    if 1 in parts:
        rows = length // 2 if filt is None else length // 2 + filt.shape[0] // 2
        shapes += [
            jax.ShapeDtypeStruct((length, channels), f32),
            jax.ShapeDtypeStruct((max(channels // HALF, 2), rows, LANES), bf16),
        ]
    if 0 in parts:
        shapes.append(jax.ShapeDtypeStruct((length, channels), f32))
    extra = [] if filt is None else [filt]
    return pl.pallas_call(
        functools.partial(project_kernel, len(blocks), parts, splits, filt is not None),
        in_specs=[pl.BlockSpec(memory_space=pltpu.SMEM)]
        + [ANY_SPEC] * (1 + len(blocks))
        + [HBM_SPEC] * (2 + len(extra)),
        out_specs=[VMEM_SPEC] * len(shapes),
        out_shape=shapes,
        scratch_shapes=[
            pltpu.VMEM((len(parts), width, channels), bf16),
            pltpu.VMEM(taps.shape, f32),
            pltpu.VMEM((PAD + length, width), bf16),
            pltpu.VMEM((PAD + length, channels), f32),
            pltpu.VMEM((8, LANES) if filt is None else filt.shape, f32),
            pltpu.SemaphoreType.DMA((len(blocks) + 2,)),
            pltpu.SemaphoreType.DMA((len(parts), splits)),
            pltpu.SemaphoreType.DMA,
        ],
        compiler_params=pltpu.CompilerParams(vmem_limit_bytes=BIG),
        cost_estimate=pl.CostEstimate(flops=cost, bytes_accessed=10**5, transcendentals=0),
        name="project",
    )(me, halo, *blocks, weight, taps, *extra)


def coarse_forward(dev_count, x_ref, lane_ref, e_ref, step=16):
    count = dev_count
    half = count // 2
    low = lane_mask()
    sgn = jnp.where(low, 1.0, -1.0).astype(f32)

    def body(i, carry):
        rows = pl.ds(pl.multiple_of(i * step, step), step)
        x = [x_ref[s, rows, :].astype(f32) for s in range(count)]
        plus = [x[s] + x[count - s] for s in range(1, half)]
        minus = [x[s] - x[count - s] for s in range(1, half)]
        for k in range(count + 1):
            even = k % 2 == 0
            re = x[0]
            im = None
            mid = round(math.cos(math.pi * half * k / count))
            if mid:
                re = re + x[half] if mid > 0 else re - x[half]
            mid = round(math.sin(math.pi * half * k / count))
            if mid:
                im = -x[half] if mid > 0 else x[half]
            for s in range(1, half):
                c, d = math.cos(math.pi * s * k / count), math.sin(math.pi * s * k / count)
                if abs(c) > 1e-9:
                    re = re + c * (plus if even else minus)[s - 1]
                if abs(d) > 1e-9:
                    term = (-d) * (minus if even else plus)[s - 1]
                    im = term if im is None else im + term
            c, d = lane_ref[k, 0:1, :], lane_ref[k, 1:2, :]
            if im is None:
                re, im = re * c, re * (-d)
            else:
                re, im = re * c + im * d, im * c - re * d
            e_ref[k, rows, :LANES] = pltpu.roll(re, HALF, 1) + sgn * re
            e_ref[k, rows, LANES:] = sgn * pltpu.roll(im, HALF, 1) + im
        return carry

    lax.fori_loop(0, FINE // step, body, 0)


def coarse_inverse(dev_count, g_ref, y_ref, step=16):
    count = dev_count
    half = count // 2

    def body(i, carry):
        rows = pl.ds(pl.multiple_of(i * step, step), step)
        acc = {}

        def add(name, s, term):
            acc[name, s] = term if (name, s) not in acc else acc[name, s] + term

        for k in range(count + 1):
            even = k % 2 == 0
            re, im = g_ref[k, rows, :LANES], g_ref[k, rows, LANES:]
            add("first", 0, re)
            mid = round(math.cos(math.pi * half * k / count))
            if mid:
                add("mid", 0, re if mid > 0 else -re)
            mid = round(math.sin(math.pi * half * k / count))
            if mid:
                add("mid", 0, -im if mid > 0 else im)
            for s in range(1, half):
                c, d = math.cos(math.pi * s * k / count), math.sin(math.pi * s * k / count)
                if abs(c) > 1e-9:
                    add("a" if even else "b", s, c * re)
                if abs(d) > 1e-9:
                    add("b" if even else "a", -s, (-d) * im)
        y_ref[0, rows, :] = acc["first", 0].astype(bf16)
        y_ref[half, rows, :] = acc["mid", 0].astype(bf16)
        zero = jnp.zeros((step, LANES), f32)
        for s in range(1, half):
            same = acc.get(("a", s), zero)
            flip = acc.get(("b", s), zero)
            same_sin = acc.get(("a", -s), zero)
            flip_sin = acc.get(("b", -s), zero)
            total, diff = same + same_sin, flip + flip_sin
            y_ref[s, rows, :] = (total + diff).astype(bf16)
            y_ref[count - s, rows, :] = (total - diff).astype(bf16)
        return carry

    lax.fori_loop(0, FINE // step, body, 0)


def fine_forward(e, tr, ti, table):
    re, im = e[:, :LANES], e[:, LANES:]
    turned = jnp.concatenate([re * tr - im * ti, re * ti + im * tr], axis=1).astype(bf16)
    both = jnp.dot(table, turned, preferred_element_type=f32)
    return (
        both[:FINE, :LANES] - both[FINE:, LANES:],
        both[:FINE, LANES:] + both[FINE:, :LANES],
    )


def next_turn(turn_ref, step_ref):
    tr, ti = turn_ref[:, :LANES], turn_ref[:, LANES:]
    sr, si = step_ref[:, :LANES], step_ref[:, LANES:]
    turn_ref[:, :LANES] = tr * sr - ti * si
    turn_ref[:, LANES:] = tr * si + ti * sr


def filter_kernel(dev_count, x_any, *refs):
    const_hbm, h_ref = refs[:4], refs[4]
    x_ref, first_ref, step_ref, lane_ref, table_ref, e_ref, sem = refs[5:]
    turn_ref = first_ref
    rows = pl.ds(x_any.shape[1] - FINE, FINE)
    pairs = [(x_any.at[:, rows], x_ref)] + list(zip(const_hbm, (first_ref, step_ref, lane_ref, table_ref)))
    for copy in start_all((*pair, sem.at[i]) for i, pair in enumerate(pairs)):
        copy.wait()
    coarse_forward(dev_count, x_ref, lane_ref, e_ref)
    points = 4 * dev_count * FINE

    def body(k, carry):
        re, im = fine_forward(e_ref[k], turn_ref[:, :LANES], turn_ref[:, LANES:], table_ref[...])
        scale = jnp.where((k == 0) | (k == dev_count), 1.0 / points, 2.0 / points).astype(f32)
        h_ref[k, :, :LANES] = re * scale
        h_ref[k, :, LANES:] = im * scale
        next_turn(turn_ref, step_ref)
        return carry

    lax.fori_loop(0, dev_count + 1, body, 0, unroll=dev_count <= 8)


def merge_halves(dev_count, late_first, early_ref, late_ref, x_ref):
    pick = late_first == 1
    for s in range(dev_count):
        early, late = early_ref[s].astype(f32), late_ref[s].astype(f32)
        first, second = jnp.where(pick, late, early), jnp.where(pick, early, late)
        top, bot = pack_pair(jnp.concatenate([first, second], axis=0))
        x_ref[s, : FINE // 2] = top
        x_ref[s, FINE // 2 :] = bot


def conv_kernel(dev_count, half_ref, early_any, late_any, h_hbm, *refs):
    const_hbm, y_ref = refs[:4], refs[4]
    early_ref, late_ref, x_ref, h_ref, first_ref, step_ref, lane_ref, table_ref, e_ref, sem = refs[5:]
    turn_ref = first_ref
    pairs = [(early_any.at[:, pl.ds(0, FINE // 2)], early_ref), (late_any, late_ref)]
    pairs += list(zip(const_hbm, (first_ref, step_ref, lane_ref, table_ref))) + [(h_hbm, h_ref)]
    copies = start_all((*pair, sem.at[i]) for i, pair in enumerate(pairs))
    for copy in copies[:-1]:
        copy.wait()
    merge_halves(dev_count, half_ref[0], early_ref, late_ref, x_ref)
    coarse_forward(dev_count, x_ref, lane_ref, e_ref)
    copies[-1].wait()
    sgn = jnp.where(lane_mask(), 1.0, -1.0).astype(f32)

    def body(k, carry):
        tr, ti = turn_ref[:, :LANES], turn_ref[:, LANES:]
        re, im = fine_forward(e_ref[k], tr, ti, table_ref[...])
        hr, hi = h_ref[k, :, :LANES], h_ref[k, :, LANES:]
        prod = jnp.concatenate([re * hr - im * hi, re * hi + im * hr], axis=1).astype(bf16)
        both = jnp.dot(table_ref[...], prod, preferred_element_type=f32)
        re = both[:FINE, :LANES] + both[FINE:, LANES:]
        im = both[:FINE, LANES:] - both[FINE:, :LANES]
        re, im = re * tr + im * ti, (im * tr - re * ti) * sgn
        re, im = pltpu.roll(re, HALF, 1) + sgn * re, pltpu.roll(im, HALF, 1) + sgn * im
        c, d = lane_ref[k, 0:1, :], lane_ref[k, 1:2, :]
        e_ref[k, :, :LANES] = re * c - im * d
        e_ref[k, :, LANES:] = re * d + im * c
        next_turn(turn_ref, step_ref)
        return carry

    lax.fori_loop(0, dev_count + 1, body, 0, unroll=dev_count <= 8)
    coarse_inverse(dev_count, e_ref, y_ref)


def tables(dev_count):
    points = 4 * dev_count * FINE
    fine = np.arange(FINE)
    first = np.exp(-2j * np.pi * fine * (2 * dev_count) / points)[:, None] * np.ones(HALF)
    ones = np.ones((FINE, HALF))
    step = np.exp(-2j * np.pi * fine / points)[:, None] * ones
    first = np.concatenate([ones, first.real, 0 * ones, first.imag], axis=1)
    step = np.concatenate([step.real, step.real, step.imag, -step.imag], axis=1)
    turn = 2 * np.pi * np.arange(dev_count + 1)[:, None] * np.ones(HALF) / (4 * dev_count)
    lane = np.stack(
        [
            np.concatenate([np.ones_like(turn), np.cos(turn)], axis=1),
            np.concatenate([np.zeros_like(turn), np.sin(turn)], axis=1),
        ],
        axis=1,
    )
    angle = -2 * np.pi * (fine[:, None] * fine[None, :] % FINE) / FINE
    table = np.concatenate([np.cos(angle), np.sin(angle)], axis=0)
    return (
        jnp.asarray(first, f32),
        jnp.asarray(step, f32),
        jnp.asarray(lane, f32),
        jnp.asarray(table, bf16),
    )


def const_scratch(consts):
    return [pltpu.VMEM(const.shape, const.dtype) for const in consts]


def filter_spectrum(x, consts):
    dev_count = x.shape[0]
    return pl.pallas_call(
        functools.partial(filter_kernel, dev_count),
        in_specs=[ANY_SPEC] + [HBM_SPEC] * 4,
        out_specs=VMEM_SPEC,
        out_shape=jax.ShapeDtypeStruct((dev_count + 1, FINE, 2 * LANES), f32),
        scratch_shapes=[pltpu.VMEM((dev_count, FINE, LANES), bf16)]
        + const_scratch(consts)
        + [pltpu.VMEM((dev_count + 1, FINE, 2 * LANES), f32), pltpu.SemaphoreType.DMA((5,))],
        compiler_params=pltpu.CompilerParams(vmem_limit_bytes=BIG),
        name="filter_spectrum",
    )(x, *consts)


def convolve(half, early, late, spectrum, consts):
    dev_count = early.shape[0]
    return pl.pallas_call(
        functools.partial(conv_kernel, dev_count),
        in_specs=[pl.BlockSpec(memory_space=pltpu.SMEM)] + [ANY_SPEC] * 2 + [HBM_SPEC] * 5,
        out_specs=VMEM_SPEC,
        out_shape=jax.ShapeDtypeStruct((dev_count, FINE, LANES), bf16),
        scratch_shapes=[
            pltpu.VMEM(late.shape, bf16),
            pltpu.VMEM(late.shape, bf16),
            pltpu.VMEM((dev_count, FINE, LANES), f32),
            pltpu.VMEM(spectrum.shape, f32),
        ]
        + const_scratch(consts)
        + [pltpu.VMEM((dev_count + 1, FINE, 2 * LANES), f32), pltpu.SemaphoreType.DMA((7,))],
        compiler_params=pltpu.CompilerParams(vmem_limit_bytes=BIG),
        name="convolve",
    )(half, early, late, spectrum, *consts)


def finish(half, conv, early, late, skip_gain):
    rows, channels = early[0].shape
    tiles = channels // LANES

    def kernel(half_ref, c_any, ge_hbm, qe_hbm, gl_hbm, ql_hbm, skip_hbm, out_ref, c_ref, row_ref, skip_ref, sem, c_sem, s_sem):
        early_at = half_ref[0]
        cols = [pl.ds(i * LANES, LANES) for i in range(tiles)]
        skip_copy = start_all([(skip_hbm, skip_ref, s_sem)])[0]
        copies = []
        for i in range(tiles):
            pair = pl.ds(2 * i, 2)
            copies.append(
                start_all(
                    [(c_any.at[pair], c_ref.at[pair], c_sem.at[i])]
                    + [
                        (src.at[:, cols[i]], row_ref.at[i, j], sem.at[i, j])
                        for j, src in enumerate((ge_hbm, qe_hbm, gl_hbm, ql_hbm))
                    ]
                )
            )
        skip_copy.wait()
        for i in range(tiles):
            for copy in copies[i]:
                copy.wait()
            top, bot = unpack_pair(c_ref[2 * i].astype(f32), c_ref[2 * i + 1].astype(f32))
            skip = skip_ref[:, cols[i]]
            for at, j in ((early_at, 0), (1 - early_at, 2)):
                conv = jnp.where(at == 0, top, bot)
                value = row_ref[i, j + 1] * (conv + skip * row_ref[i, j])
                out_ref[pl.ds(pl.multiple_of(at * FINE, FINE), FINE), cols[i]] = value.astype(bf16)

    return pl.pallas_call(
        kernel,
        in_specs=[pl.BlockSpec(memory_space=pltpu.SMEM), ANY_SPEC] + [HBM_SPEC] * 5,
        out_specs=VMEM_SPEC,
        out_shape=jax.ShapeDtypeStruct((2 * rows, channels), bf16),
        scratch_shapes=[
            pltpu.VMEM(conv.shape, bf16),
            pltpu.VMEM((tiles, 4, rows, LANES), f32),
            pltpu.VMEM((1, channels), f32),
            pltpu.SemaphoreType.DMA((tiles, 4)),
            pltpu.SemaphoreType.DMA((tiles,)),
            pltpu.SemaphoreType.DMA,
        ],
        compiler_params=pltpu.CompilerParams(vmem_limit_bytes=BIG),
        name="finish",
    )(half, conv, *early, *late, skip_gain.reshape(1, channels))


def local(tokens, norm_gain, in_weight, short_weight, long_filter, skip_gain):
    dev_count = lax.axis_size("context")
    tensor_count = lax.axis_size("tensor")
    channels = in_weight.shape[2]
    packed = channels // dev_count == HALF
    consts = tables(dev_count)
    weight = jnp.transpose(in_weight, (1, 0, 2))
    exchange = functools.partial(
        lax.all_to_all, axis_name="context", split_axis=0, concat_axis=0, tiled=True
    )

    me = lax.axis_index("tensor").astype(jnp.int32)
    mid = tensor_count // 2
    half = (me // mid).reshape(1)
    place = (me % mid).reshape(1)

    def swap(x, bit):
        return lax.ppermute(x, "tensor", [(i, i ^ bit) for i in range(tensor_count)])

    def gathered(block):
        blocks = {0: block}
        bit = mid // 2
        while bit:
            for mask in list(blocks):
                blocks[mask | bit] = swap(blocks[mask], bit)
            bit //= 2
        return [blocks[mask] for mask in range(mid)]

    start = [(c * tensor_count - 1, c * tensor_count) for c in range(1, dev_count)]
    inner = [(c * tensor_count + mid - 1, c * tensor_count) for c in range(dev_count)]

    def halo(tail, first, second):
        total = jnp.zeros_like(tail)
        for j in range(mid):
            pairs = [(a, b + first + j) for a, b in start] + [(a, b + second + j) for a, b in inner]
            total = total + lax.ppermute(tail, ("context", "tensor"), pairs)
        return jnp.concatenate([jnp.zeros((PAD - TAIL, tail.shape[1]), bf16), total], axis=0)

    normed, tail = norm_rows(tokens, norm_gain)
    normed, early_halo = lax.optimization_barrier((normed, halo(tail, 0, mid)))
    crossed = swap(normed, mid)
    early_blocks = gathered(normed)
    early_halo, late_halo = lax.optimization_barrier((early_halo, halo(tail, mid, 0)))

    if packed:
        early_gated, packs = project(
            (1, 2), place, early_halo, early_blocks, weight, short_weight, COST[0], long_filter
        )
    else:
        early_gated, _ = project((1, 2), place, early_halo, early_blocks, weight, short_weight, COST[0])
        packs = [pack_any(rows, dev_count) for rows in (early_gated, long_filter)]
        packs = jnp.concatenate(packs, axis=1)
    early_sent = exchange(packs)
    crossed, _ = lax.optimization_barrier((crossed, packs))
    late_blocks = gathered(crossed)
    late_gated, packs = project((1, 2), place, late_halo, late_blocks, weight, short_weight, COST[1])
    late_sent = exchange(packs if packed else pack_any(late_gated, dev_count))
    spectrum = filter_spectrum(early_sent, consts)
    (late_query,) = project((0,), place, late_halo, late_blocks, weight, short_weight, COST[2])
    (early_query,) = project((0,), place, early_halo, early_blocks, weight, short_weight, COST[2])
    conv = exchange(convolve(half, early_sent, late_sent, spectrum, consts))
    early, late = (early_gated, early_query), (late_gated, late_query)
    if packed:
        return finish(half, conv, early, late, skip_gain)
    each = channels // dev_count
    conv = conv.reshape(dev_count, FINE, 2, HALF)[..., :each]
    conv = jnp.transpose(conv, (2, 1, 0, 3)).reshape(2 * FINE, channels).astype(f32)
    first, second = (
        [jnp.where(half == swapped, a, b) for a, b in zip(early, late)] for swapped in (0, 1)
    )
    gated, query = (jnp.concatenate([a, b], axis=0) for a, b in zip(first, second))
    return (query * (conv + skip_gain * gated)).astype(bf16)


def solution(mesh):
    return jax.shard_map(
        local,
        mesh=mesh,
        in_specs=(
            P(("context", "tensor"), None),
            P(),
            P(None, None, "tensor"),
            P(None, None, "tensor"),
            P("context", "tensor"),
            P("tensor"),
        ),
        out_specs=P("context", "tensor"),
        check_vma=False,
    )
```

time: 109 us -> 95.6 us (0.88)
  the two profiles are of different devices: /device:TPU:3 before, /device:TPU:0 now
where the time goes in v2:
time: 95.6 us; the launch traced here: 95 us
  Pallas kernels  44.5 us (47%)
  starting transfers between devices  24.5 us (26%)
  waiting for transfers between devices  20.8 us (22%)
  local copies, waits for them, and re-layouts  4.87 us (5%)
    pallas_call x4, Pallas kernels, project(): pl.pallas_call(functools.partial(project_kernel, len(blocks), parts, spli...  26 us
    ppermute x3, starting transfers between devices, swap(): lax.ppermute(x, 'tensor', [(i, i ^ bit) for i in range(tensor_count)])  8.11 us
    ppermute x3, waiting for transfers between devices, swap(): lax.ppermute(x, 'tensor', [(i, i ^ bit) for i in range(tensor_count)])  7.28 us
    pallas_call x1, Pallas kernels, convolve(): pl.pallas_call(functools.partial(conv_kernel, dev_count), in_specs=[pl.Bl...  7.04 us
    all_to_all x1, starting transfers between devices, local(): early_sent = exchange(packs)  5.85 us
    pallas_call x1, Pallas kernels, filter_spectrum(): pl.pallas_call(functools.partial(filter_kernel, dev_count), in_specs=[ANY...  5.69 us
    all_to_all x1, waiting for transfers between devices, local(): early_sent = exchange(packs)  4.45 us
    all_to_all x1, starting transfers between devices, local(): conv = exchange(convolve(half, early_sent, late_sent, spectrum, consts))  3.69 us
  transfers between devices with their start and end apart: 10, of which 6 were waited for; matrix products, arithmetic and copies ran while one was open for 1% of the time, Pallas kernels for 33%

profile of v2, /device:TPU:0, one launch (start us, length us, event | category | flops | bytes accessed | tf_op | source)
XLA Modules:
  0.0 95.0 jit_solution(7899923442289892762)
XLA Ops:
  0.0 2.7 %norm_rows.1 = (bf16[128,4096]{1,0:T(8,128)(2,1)}, bf16[8,4096]{1,0:T(8,128)(2,1)}) custom-call(bf16[128,4096]{1,0:T(8,128)(2,1)} %tok_hbm.1, f32[1,4096]{1,0:T(1,128)} %bitcast.9), custom_call_target="tpu_custom_call" | custom-call | tf_op jit(solution)/shard_map/norm_rows/pallas_call | solution.py:87
  2.7 0.7 collective-permute-start.1
  3.4 0.7 collective-permute-start
  4.1 0.0 collective-permute-done.1
  4.1 0.0 collective-permute-done
  4.1 0.7 concatenate.6.halo_any
  4.8 6.0 %collective-permute-start.4 = (bf16[128,4096]{1,0:T(8,128)(2,1)}, bf16[128,4096]{1,0:T(8,128)(2,1)S(1)}, u32[]{:S(2)}, u32[]{:S(2)}) collective-permute-start(bf16[128,4096]{1,0:T(8,128)(2,1)} %get-tuple-element.20.refs_0_), channel_id=1, source_target_pairs={{0,1},{1,0},{2,3},{3,2},{4,5},{5,4},{6,7},{7,6},{8,9},{9,8},{10,11... | collective-permute-start | bytes 3145736 | tf_op jit(solution)/shard_map/ppermute | solution.py:496
  10.7 2.1 %collective-permute-start.5 = (bf16[128,4096]{1,0:T(8,128)(2,1)}, bf16[128,4096]{1,0:T(8,128)(2,1)S(1)}, u32[]{:S(2)}, u32[]{:S(2)}) collective-permute-start(bf16[128,4096]{1,0:T(8,128)(2,1)} %get-tuple-element.20.refs_0_), channel_id=1, source_target_pairs={{0,2},{1,3},{2,0},{3,1},{4,6},{5,7},{6,4},{7,5},{8,10},{9,11},{10,... | collective-permute-start | bytes 3145736 | tf_op jit(solution)/shard_map/ppermute | solution.py:496
  12.9 0.7 collective-permute-start.3
  13.5 1.3 %collective-permute-start.2 = (bf16[8,4096]{1,0:T(8,128)(2,1)}, bf16[8,4096]{1,0:T(8,128)(2,1)S(1)}, u32[]{:S(2)}, u32[]{:S(2)}) collective-permute-start(bf16[8,4096]{1,0:T(8,128)(2,1)} %get-tuple-element.17), channel_id=1, source_target_pairs={{3,6},{7,10},{11,14},{15,18},{19,22},{23,26},{27,30},{1,0},{5,4},{... | collective-permute-start | bytes 196616 | tf_op jit(solution)/shard_map/ppermute | solution.py:514
  14.9 0.0 collective-permute-done.3
  14.9 2.0 %collective-permute-done.2 = bf16[8,4096]{1,0:T(8,128)(2,1)S(1)} collective-permute-done((bf16[8,4096]{1,0:T(8,128)(2,1)}, bf16[8,4096]{1,0:T(8,128)(2,1)S(1)}, u32[]{:S(2)}, u32[]{:S(2)}) %collective-permute-start.2) | collective-permute-done | bytes 65568 | tf_op jit(solution)/shard_map/ppermute | solution.py:514
  16.9 0.7 concatenate.7.halo_any
  17.6 0.0 collective-permute-done.4.refs_1_
  17.6 0.0 copy-start.1
  17.6 1.0 %copy-done.1 = bf16[128,4096]{1,0:T(8,128)(2,1)} copy-done((bf16[128,4096]{1,0:T(8,128)(2,1)}, bf16[128,4096]{1,0:T(8,128)(2,1)S(1)}, u32[]{:S(2)}) %copy-start.1) | copy-done | bytes 1048600
  18.6 7.9 %project.4 = (f32[256,512]{1,0:T(8,128)}, bf16[8,384,128]{2,1,0:T(8,128)(2,1)}) custom-call(s32[1]{0:T(128)} %bitcast.1.me_ref, bf16[16,4096]{1,0:T(8,128)(2,1)} %concatenate.6.halo_any, bf16[128,4096]{1,0:T(8,128)(2,1)} %get-tuple-element.20.refs_0_, bf16[128,4096]{1,0:T(8,128)(2,1)} %copy-done.1, bf16[3,4096,512]{2,1,0:T(8,128)(2,1)} %bitcast.5, ...), custom_call_target="tpu_custom_call" | custom-call | flops 100000000 | bytes 100000 | tf_op jit(solution)/shard_map/project/pallas_call | solution.py:176
  26.5 5.8 %all-to-all-start = ((bf16[8,384,128]{2,1,0:T(8,128)(2,1)}), bf16[8,384,128]{2,1,0:T(8,128)(2,1)S(1)}, u32[]{:S(2)}, u32[]{:S(2)}) async-start(bf16[8,384,128]{2,1,0:T(8,128)(2,1)} %get-tuple-element.21), calls=%async_computation | async-start | bytes 1572864 | tf_op jit(solution)/shard_map/all_to_all | solution.py:531
  32.3 4.6 %collective-permute-done.5.refs_0_ = bf16[128,4096]{1,0:T(8,128)(2,1)S(1)} collective-permute-done((bf16[128,4096]{1,0:T(8,128)(2,1)}, bf16[128,4096]{1,0:T(8,128)(2,1)S(1)}, u32[]{:S(2)}, u32[]{:S(2)}) %collective-permute-start.5) | collective-permute-done | bytes 1048608 | tf_op jit(solution)/shard_map/ppermute | solution.py:496
  36.9 0.0 copy-start.2
  36.9 0.0 collective-permute-start.6
  36.9 2.7 %collective-permute-done.6.refs_1_ = bf16[128,4096]{1,0:T(8,128)(2,1)S(1)} collective-permute-done((bf16[128,4096]{1,0:T(8,128)(2,1)S(1)}, bf16[128,4096]{1,0:T(8,128)(2,1)S(1)}, u32[]{:S(2)}, u32[]{:S(2)}) %collective-permute-start.6) | collective-permute-done | bytes 1048608 | tf_op jit(solution)/shard_map/ppermute | solution.py:496
  39.6 0.0 copy-done.2
  39.6 0.0 copy-start.3
  39.6 1.0 %copy-done.3 = bf16[128,4096]{1,0:T(8,128)(2,1)} copy-done((bf16[128,4096]{1,0:T(8,128)(2,1)}, bf16[128,4096]{1,0:T(8,128)(2,1)S(1)}, u32[]{:S(2)}) %copy-start.3) | copy-done | bytes 1048600
  40.6 7.7 %project.5 = (f32[256,512]{1,0:T(8,128)}, bf16[8,128,128]{2,1,0:T(8,128)(2,1)}) custom-call(s32[1]{0:T(128)} %bitcast.1.me_ref, bf16[16,4096]{1,0:T(8,128)(2,1)} %concatenate.7.halo_any, bf16[128,4096]{1,0:T(8,128)(2,1)} %copy-done.2, bf16[128,4096]{1,0:T(8,128)(2,1)} %copy-done.3, bf16[3,4096,512]{2,1,0:T(8,128)(2,1)} %bitcast.6, f32[3,3,512]{2,1,0:T(4,128)} %refs_3_.9), custom_call_target="tpu_custom_call" | custom-call | flops 100000000 | bytes 100000 | tf_op jit(solution)/shard_map/project/pallas_call | solution.py:176
  48.3 4.4 %all-to-all-done.x_any.early_any = bf16[8,384,128]{2,1,0:T(8,128)(2,1)S(1)} async-done(((bf16[8,384,128]{2,1,0:T(8,128)(2,1)}), bf16[8,384,128]{2,1,0:T(8,128)(2,1)S(1)}, u32[]{:S(2)}, u32[]{:S(2)}) %all-to-all-start) | async-done | bytes 786464 | tf_op jit(solution)/shard_map/all_to_all | solution.py:531
  52.8 0.0 copy-start
  52.8 3.6 %all-to-all-start.1 = ((bf16[8,128,128]{2,1,0:T(8,128)(2,1)}), bf16[8,128,128]{2,1,0:T(8,128)(2,1)S(1)}, u32[]{:S(2)}, u32[]{:S(2)}) async-start(bf16[8,128,128]{2,1,0:T(8,128)(2,1)} %get-tuple-element.24), calls=%async_computation.1 | async-start | bytes 524288 | tf_op jit(solution)/shard_map/all_to_all | solution.py:535
  56.4 0.0 copy-done
  56.4 5.7 %filter_spectrum.1.h_hbm = f32[9,256,256]{2,1,0:T(8,128)} custom-call(bf16[8,384,128]{2,1,0:T(8,128)(2,1)} %copy-done, f32[256,256]{1,0:T(8,128)} %constant.38.clone.refs_0_, f32[256,256]{1,0:T(8,128)} %constant.39.clone.refs_1_, f32[9,2,128]{2,1,0:T(2,128)} %constant.40.clone.refs_2_, bf16[512,256]{1,0:T(8,128)(2,1)} %constant.41.clone.refs_3_), custom_call_target="tpu_custom_call" | custom-call | tf_op jit(solution)/shard_map/filter_spectrum/pallas_call | solution.py:397
  62.1 3.4 %all-to-all-done.1.late_any = bf16[8,128,128]{2,1,0:T(8,128)(2,1)S(1)} async-done(((bf16[8,128,128]{2,1,0:T(8,128)(2,1)}), bf16[8,128,128]{2,1,0:T(8,128)(2,1)S(1)}, u32[]{:S(2)}, u32[]{:S(2)}) %all-to-all-start.1) | async-done | bytes 262176 | tf_op jit(solution)/shard_map/all_to_all | solution.py:535
  65.5 0.0 copy-start.5
  65.5 0.7 copy-done.5
  66.2 7.0 %convolve.1 = bf16[8,256,128]{2,1,0:T(8,128)(2,1)} custom-call(s32[1]{0:T(128)} %bitcast.half_ref, bf16[8,384,128]{2,1,0:T(8,128)(2,1)} %copy-done, bf16[8,128,128]{2,1,0:T(8,128)(2,1)} %copy-done.5, f32[9,256,256]{2,1,0:T(8,128)} %filter_spectrum.1.h_hbm, f32[256,256]{1,0:T(8,128)} %constant.38.clone.refs_0_, f32[256,256]{1,0:T(8,128)} %constant.39.clone.refs_1_, ...), custom_call_target="tpu_custom_call" | custom-call | tf_op jit(solution)/shard_map/convolve/pallas_call | solution.py:412
  73.2 3.7 %all-to-all-start.2 = ((bf16[8,256,128]{2,1,0:T(8,128)(2,1)}), bf16[8,256,128]{2,1,0:T(8,128)(2,1)S(1)}, u32[]{:S(2)}, u32[]{:S(2)}) async-start(bf16[8,256,128]{2,1,0:T(8,128)(2,1)} %convolve.1), calls=%async_computation.2 | async-start | bytes 1048576 | tf_op jit(solution)/shard_map/all_to_all | solution.py:539
  76.9 5.2 %project.6.qe_hbm = f32[256,512]{1,0:T(8,128)} custom-call(s32[1]{0:T(128)} %bitcast.1.me_ref, bf16[16,4096]{1,0:T(8,128)(2,1)} %concatenate.6.halo_any, bf16[128,4096]{1,0:T(8,128)(2,1)} %get-tuple-element.20.refs_0_, bf16[128,4096]{1,0:T(8,128)(2,1)} %copy-done.1, bf16[3,4096,512]{2,1,0:T(8,128)(2,1)} %bitcast.7, f32[3,3,512]{2,1,0:T(4,128)} %refs_3_.9), custom_call_target="tpu_custom_call" | custom-call | flops 100000000 | bytes 100000 | tf_op jit(solution)/shard_map/project/pallas_call | solution.py:176
  82.2 5.2 %project.7.ql_hbm = f32[256,512]{1,0:T(8,128)} custom-call(s32[1]{0:T(128)} %bitcast.1.me_ref, bf16[16,4096]{1,0:T(8,128)(2,1)} %concatenate.7.halo_any, bf16[128,4096]{1,0:T(8,128)(2,1)} %copy-done.2, bf16[128,4096]{1,0:T(8,128)(2,1)} %copy-done.3, bf16[3,4096,512]{2,1,0:T(8,128)(2,1)} %bitcast.8, f32[3,3,512]{2,1,0:T(4,128)} %refs_3_.9), custom_call_target="tpu_custom_call" | custom-call | flops 100000000 | bytes 100000 | tf_op jit(solution)/shard_map/project/pallas_call | solution.py:176
  87.4 3.6 %all-to-all-done.2.c_any = bf16[8,256,128]{2,1,0:T(8,128)(2,1)S(1)} async-done(((bf16[8,256,128]{2,1,0:T(8,128)(2,1)}), bf16[8,256,128]{2,1,0:T(8,128)(2,1)S(1)}, u32[]{:S(2)}, u32[]{:S(2)}) %all-to-all-start.2) | async-done | bytes 524320 | tf_op jit(solution)/shard_map/all_to_all | solution.py:539
  91.0 0.0 copy-start.4
  91.0 0.8 copy-done.4
  91.8 3.1 %finish.1 = bf16[512,512]{1,0:T(8,128)(2,1)} custom-call(s32[1]{0:T(128)} %bitcast.half_ref, bf16[8,256,128]{2,1,0:T(8,128)(2,1)} %copy-done.4, f32[256,512]{1,0:T(8,128)} %get-tuple-element.25.ge_hbm, f32[256,512]{1,0:T(8,128)} %project.6.qe_hbm, f32[256,512]{1,0:T(8,128)} %get-tuple-element.26.gl_hbm, f32[256,512]{1,0:T(8,128)} %project.7.ql_hbm, ...), custom_call_target="tpu_custom_call" | custom-call | tf_op jit(solution)/shard_map/finish/pallas_call | solution.py:461
  (2 shorter events, 0.0 us)
Async XLA Ops:
  2.7 1.3 %collective-permute-start.1 = (bf16[8,4096]{1,0:T(8,128)(2,1)}, bf16[8,4096]{1,0:T(8,128)(2,1)S(1)}, u32[]{:S(2)}, u32[]{:S(2)}) collective-permute-start(bf16[8,4096]{1,0:T(8,128)(2,1)} %get-tuple-element.17), channel_id=1, source_target_pairs={{3,5},{7,9},{11,13},{15,17},{19,21},{23,25},{27,29},{1,3},{5,7},{9... | collective-permute-start | bytes 196616 | tf_op jit(solution)/shard_map/ppermute | solution.py:514
  3.4 0.7 collective-permute-start
  4.8 12.8 %collective-permute-start.4 = (bf16[128,4096]{1,0:T(8,128)(2,1)}, bf16[128,4096]{1,0:T(8,128)(2,1)S(1)}, u32[]{:S(2)}, u32[]{:S(2)}) collective-permute-start(bf16[128,4096]{1,0:T(8,128)(2,1)} %get-tuple-element.20.refs_0_), channel_id=1, source_target_pairs={{0,1},{1,0},{2,3},{3,2},{4,5},{5,4},{6,7},{7,6},{8,9},{9,8},{10,11... | collective-permute-start | bytes 3145736 | tf_op jit(solution)/shard_map/ppermute | solution.py:496
  10.7 26.2 %collective-permute-start.5 = (bf16[128,4096]{1,0:T(8,128)(2,1)}, bf16[128,4096]{1,0:T(8,128)(2,1)S(1)}, u32[]{:S(2)}, u32[]{:S(2)}) collective-permute-start(bf16[128,4096]{1,0:T(8,128)(2,1)} %get-tuple-element.20.refs_0_), channel_id=1, source_target_pairs={{0,2},{1,3},{2,0},{3,1},{4,6},{5,7},{6,4},{7,5},{8,10},{9,11},{10,... | collective-permute-start | bytes 3145736 | tf_op jit(solution)/shard_map/ppermute | solution.py:496
  12.9 2.0 %collective-permute-start.3 = (bf16[8,4096]{1,0:T(8,128)(2,1)}, bf16[8,4096]{1,0:T(8,128)(2,1)S(1)}, u32[]{:S(2)}, u32[]{:S(2)}) collective-permute-start(bf16[8,4096]{1,0:T(8,128)(2,1)} %get-tuple-element.17), channel_id=1, source_target_pairs={{3,7},{7,11},{11,15},{15,19},{19,23},{23,27},{27,31},{1,1},{5,5},{... | collective-permute-start | bytes 196616 | tf_op jit(solution)/shard_map/ppermute | solution.py:514
  13.5 3.4 %collective-permute-start.2 = (bf16[8,4096]{1,0:T(8,128)(2,1)}, bf16[8,4096]{1,0:T(8,128)(2,1)S(1)}, u32[]{:S(2)}, u32[]{:S(2)}) collective-permute-start(bf16[8,4096]{1,0:T(8,128)(2,1)} %get-tuple-element.17), channel_id=1, source_target_pairs={{3,6},{7,10},{11,14},{15,18},{19,22},{23,26},{27,30},{1,0},{5,4},{... | collective-permute-start | bytes 196616 | tf_op jit(solution)/shard_map/ppermute | solution.py:514
  17.6 1.0 %copy-start.1 = (bf16[128,4096]{1,0:T(8,128)(2,1)}, bf16[128,4096]{1,0:T(8,128)(2,1)S(1)}, u32[]{:S(2)}) copy-start(bf16[128,4096]{1,0:T(8,128)(2,1)S(1)} %collective-permute-done.4.refs_1_) | copy-start | bytes 3145732
  26.5 26.3 %all-to-all-start = ((bf16[8,384,128]{2,1,0:T(8,128)(2,1)}), bf16[8,384,128]{2,1,0:T(8,128)(2,1)S(1)}, u32[]{:S(2)}, u32[]{:S(2)}) async-start(bf16[8,384,128]{2,1,0:T(8,128)(2,1)} %get-tuple-element.21), calls=%async_computation | async-start | bytes 1572864 | tf_op jit(solution)/shard_map/all_to_all | solution.py:531
  36.9 2.7 %copy-start.2 = (bf16[128,4096]{1,0:T(8,128)(2,1)}, bf16[128,4096]{1,0:T(8,128)(2,1)S(1)}, u32[]{:S(2)}) copy-start(bf16[128,4096]{1,0:T(8,128)(2,1)S(1)} %collective-permute-done.5.refs_0_) | copy-start | bytes 3145732
  36.9 2.7 %collective-permute-start.6 = (bf16[128,4096]{1,0:T(8,128)(2,1)S(1)}, bf16[128,4096]{1,0:T(8,128)(2,1)S(1)}, u32[]{:S(2)}, u32[]{:S(2)}) collective-permute-start(bf16[128,4096]{1,0:T(8,128)(2,1)S(1)} %collective-permute-done.5.refs_0_), channel_id=1, source_target_pairs={{0,1},{1,0},{2,3},{3,2},{4,5},{5,4},{6,7},{7,6},{8,9},{9,8},{10,11... | collective-permute-start | bytes 3145736 | tf_op jit(solution)/shard_map/ppermute | solution.py:496
  39.6 1.0 %copy-start.3 = (bf16[128,4096]{1,0:T(8,128)(2,1)}, bf16[128,4096]{1,0:T(8,128)(2,1)S(1)}, u32[]{:S(2)}) copy-start(bf16[128,4096]{1,0:T(8,128)(2,1)S(1)} %collective-permute-done.6.refs_1_) | copy-start | bytes 3145732
  52.8 3.6 %copy-start = (bf16[8,384,128]{2,1,0:T(8,128)(2,1)}, bf16[8,384,128]{2,1,0:T(8,128)(2,1)S(1)}, u32[]{:S(2)}) copy-start(bf16[8,384,128]{2,1,0:T(8,128)(2,1)S(1)} %all-to-all-done.x_any.early_any) | copy-start | bytes 2359300
  52.8 12.7 %all-to-all-start.1 = ((bf16[8,128,128]{2,1,0:T(8,128)(2,1)}), bf16[8,128,128]{2,1,0:T(8,128)(2,1)S(1)}, u32[]{:S(2)}, u32[]{:S(2)}) async-start(bf16[8,128,128]{2,1,0:T(8,128)(2,1)} %get-tuple-element.24), calls=%async_computation.1 | async-start | bytes 524288 | tf_op jit(solution)/shard_map/all_to_all | solution.py:535
  65.5 0.7 copy-start.5
  73.2 17.8 %all-to-all-start.2 = ((bf16[8,256,128]{2,1,0:T(8,128)(2,1)}), bf16[8,256,128]{2,1,0:T(8,128)(2,1)S(1)}, u32[]{:S(2)}, u32[]{:S(2)}) async-start(bf16[8,256,128]{2,1,0:T(8,128)(2,1)} %convolve.1), calls=%async_computation.2 | async-start | bytes 1048576 | tf_op jit(solution)/shard_map/all_to_all | solution.py:539
  91.0 0.8 copy-start.4

commit v3 on v2

--- a/solution.py
+++ b/solution.py
@@ -99,37 +99,44 @@
     )(tokens, gain.reshape(1, width))
 
 
-def pack_into(p_ref, at, rows_ref):
-    rows = pl.ds(at, rows_ref.shape[0] // 2)
+def pack_into(p_ref, at, rows_ref, first, length):
+    rows = pl.ds(at, length // 2)
     for i in range(p_ref.shape[0] // 2):
-        first, second = pack_pair(rows_ref[:, i * LANES : (i + 1) * LANES])
-        p_ref[2 * i, rows, :] = first.astype(bf16)
-        p_ref[2 * i + 1, rows, :] = second.astype(bf16)
-
-
-def project_kernel(count, parts, splits, with_filter, me_ref, halo_any, *refs):
-    blocks = refs[:count]
-    w_hbm, tap_hbm = refs[count : count + 2]
-    outs = list(refs[count + 2 : -8])
+        one, two = pack_pair(rows_ref[first : first + length, i * LANES : (i + 1) * LANES])
+        p_ref[2 * i, rows, :] = one.astype(bf16)
+        p_ref[2 * i + 1, rows, :] = two.astype(bf16)
+
+
+def project_kernel(count, parts, splits, ext_rows, with_filter, me_ref, *refs):
+    blocks, refs = refs[:count], refs[count:]
+    w_hbm, tap_hbm = refs[:2]
+    extra, outs = refs[2 : 2 + bool(ext_rows) + with_filter], refs[2 + bool(ext_rows) + with_filter : -8]
     w_ref, tap_ref, x_ref, rows_ref, filt_ref, sem, w_sem, tap_sem = refs[-8:]
     each = blocks[0].shape[0]
     length = each * count
+    end = PAD + length
     width = x_ref.shape[1]
     depth = width // splits
 
-    sources = [(halo_any, x_ref.at[pl.ds(0, PAD)], sem.at[count])]
+    sources = [(tap_hbm, tap_ref, tap_sem)]
     for mask, block in enumerate(blocks):
         first = pl.multiple_of(PAD + (me_ref[0] ^ mask) * each, 16)
         sources.append((block, x_ref.at[pl.ds(first, each)], sem.at[mask]))
-    waits = start_all(sources + [(tap_hbm, tap_ref, tap_sem)])
+    if ext_rows:
+        sources.append((extra[0].at[pl.ds(0, PAD)], x_ref.at[pl.ds(0, PAD)], sem.at[count]))
+    else:
+        x_ref[:PAD] = jnp.zeros((PAD, width), bf16)
+    if ext_rows > PAD:
+        rest = ext_rows - PAD
+        sources.append((extra[0].at[pl.ds(PAD, rest)], x_ref.at[pl.ds(end, rest)], sem.at[count + 1]))
+    waits = start_all(sources)
     loads = {}
     for at, s in enumerate(parts):
         for i in range(splits):
             chunk = pl.ds(i * depth, depth)
             loads[s, i] = start_all([(w_hbm.at[s, chunk], w_ref.at[at, chunk], w_sem.at[at, i])])[0]
     if with_filter:
-        filt_hbm, outs = outs[0], outs[1:]
-        filt_load = start_all([(filt_hbm, filt_ref, sem.at[count + 1])])[0]
+        filt_load = start_all([(extra[-1], filt_ref, sem.at[count + 2])])[0]
     for wait in waits:
         wait.wait()
 
@@ -142,58 +149,70 @@
             term = jnp.dot(x_ref[:, chunk], w_ref[at, chunk], preferred_element_type=f32)
             total = term if total is None else total + term
         rows_ref[...] = total
-        total = tap_ref[0, s : s + 1] * rows_ref[PAD : PAD + length]
-        for lag in (1, 2):
-            total += tap_ref[lag, s : s + 1] * rows_ref[PAD - lag : PAD - lag + length]
-        return total
+        spans = [(PAD, length)]
+        if ext_rows > PAD:
+            spans.append((end + PAD, PAD))
+        results = []
+        for first, size in spans:
+            total = tap_ref[0, s : s + 1] * rows_ref[first : first + size]
+            for lag in (1, 2):
+                total += tap_ref[lag, s : s + 1] * rows_ref[first - lag : first - lag + size]
+            results.append(total)
+        return results
 
     if 1 in parts:
         g_ref, p_ref = outs[:2]
-        g_ref[...] = mixed(1)
-        g_ref[...] *= mixed(2)
-        pack_into(p_ref, 0, g_ref)
+        spans = [slice(0, length), slice(length, length + PAD)]
+        for span, key in zip(spans, mixed(1)):
+            g_ref[span, :] = key
+        for span, value in zip(spans, mixed(2)):
+            g_ref[span, :] *= value
+        pack_into(p_ref, 0, g_ref, 0, length)
+        if ext_rows > PAD:
+            pack_into(p_ref, length // 2, g_ref, length, PAD)
     if 0 in parts:
-        outs[-1][...] = mixed(0)
+        outs[-1][...] = mixed(0)[0]
     if with_filter:
         filt_load.wait()
-        pack_into(p_ref, length // 2, filt_ref)
-
-
-def project(parts, me, halo, blocks, weight, taps, cost, filt=None):
+        pack_into(p_ref, length // 2, filt_ref, 0, filt_ref.shape[0])
+
+
+def project(parts, me, blocks, weight, taps, cost, ext=None, filt=None):
     _, width, channels = weight.shape
     length = blocks[0].shape[0] * len(blocks)
     splits = 2
+    ext_rows = 0 if ext is None else ext.shape[0]
+    more = PAD if ext_rows > PAD else 0
     shapes = []
     if 1 in parts:
-        rows = length // 2 if filt is None else length // 2 + filt.shape[0] // 2
+        rows = (length + more) // 2 + (0 if filt is None else filt.shape[0] // 2)
         shapes += [
-            jax.ShapeDtypeStruct((length, channels), f32),
+            jax.ShapeDtypeStruct((length + more, channels), f32),
             jax.ShapeDtypeStruct((max(channels // HALF, 2), rows, LANES), bf16),
         ]
     if 0 in parts:
         shapes.append(jax.ShapeDtypeStruct((length, channels), f32))
-    extra = [] if filt is None else [filt]
+    extra = [x for x in (ext, filt) if x is not None]
+    rows = PAD + length + (2 * PAD if more else 0)
     return pl.pallas_call(
-        functools.partial(project_kernel, len(blocks), parts, splits, filt is not None),
-        in_specs=[pl.BlockSpec(memory_space=pltpu.SMEM)]
-        + [ANY_SPEC] * (1 + len(blocks))
-        + [HBM_SPEC] * (2 + len(extra)),
+        functools.partial(project_kernel, len(blocks), parts, splits, ext_rows, filt is not None),
+        in_specs=[pl.BlockSpec(memory_space=pltpu.SMEM)] + [ANY_SPEC] * (len(blocks) + 2 + len(extra)),
         out_specs=[VMEM_SPEC] * len(shapes),
         out_shape=shapes,
         scratch_shapes=[
             pltpu.VMEM((len(parts), width, channels), bf16),
             pltpu.VMEM(taps.shape, f32),
-            pltpu.VMEM((PAD + length, width), bf16),
-            pltpu.VMEM((PAD + length, channels), f32),
+            pltpu.VMEM((rows, width), bf16),
+            pltpu.VMEM((rows, channels), f32),
             pltpu.VMEM((8, LANES) if filt is None else filt.shape, f32),
-            pltpu.SemaphoreType.DMA((len(blocks) + 2,)),
+            pltpu.SemaphoreType.DMA((len(blocks) + 3,)),
             pltpu.SemaphoreType.DMA((len(parts), splits)),
             pltpu.SemaphoreType.DMA,
         ],
         compiler_params=pltpu.CompilerParams(vmem_limit_bytes=BIG),
         cost_estimate=pl.CostEstimate(flops=cost, bytes_accessed=10**5, transcendentals=0),
         name="project",
-    )(me, halo, *blocks, weight, taps, *extra)
+    )(me, *blocks, weight, taps, *extra)
 
 
 def coarse_forward(dev_count, x_ref, lane_ref, e_ref, step=16):
@@ -320,12 +339,16 @@
 
 def merge_halves(dev_count, late_first, early_ref, late_ref, x_ref):
     pick = late_first == 1
+    low = lane_mask()
+    size = FINE // 2
     for s in range(dev_count):
         early, late = early_ref[s].astype(f32), late_ref[s].astype(f32)
+        fixed = jnp.where(low, late[size:], early[: PAD // 2])
+        early, late = jnp.concatenate([fixed, early[PAD // 2 :]], axis=0), late[:size]
         first, second = jnp.where(pick, late, early), jnp.where(pick, early, late)
         top, bot = pack_pair(jnp.concatenate([first, second], axis=0))
-        x_ref[s, : FINE // 2] = top
-        x_ref[s, FINE // 2 :] = bot
+        x_ref[s, :size] = top
+        x_ref[s, size:] = bot
 
 
 def conv_kernel(dev_count, half_ref, early_any, late_any, h_hbm, *refs):
@@ -415,7 +438,7 @@
         out_specs=VMEM_SPEC,
         out_shape=jax.ShapeDtypeStruct((dev_count, FINE, LANES), bf16),
         scratch_shapes=[
-            pltpu.VMEM(late.shape, bf16),
+            pltpu.VMEM((dev_count, FINE // 2, LANES), bf16),
             pltpu.VMEM(late.shape, bf16),
             pltpu.VMEM((dev_count, FINE, LANES), f32),
             pltpu.VMEM(spectrum.shape, f32),
@@ -442,7 +465,7 @@
                 start_all(
                     [(c_any.at[pair], c_ref.at[pair], c_sem.at[i])]
                     + [
-                        (src.at[:, cols[i]], row_ref.at[i, j], sem.at[i, j])
+                        (src.at[:, cols[i]], row_ref.at[i, j, pl.ds(0, src.shape[0])], sem.at[i, j])
                         for j, src in enumerate((ge_hbm, qe_hbm, gl_hbm, ql_hbm))
                     ]
                 )
@@ -453,9 +476,10 @@
                 copy.wait()
             top, bot = unpack_pair(c_ref[2 * i].astype(f32), c_ref[2 * i + 1].astype(f32))
             skip = skip_ref[:, cols[i]]
+            row_ref[i, 0, :PAD] = row_ref[i, 2, rows:]
             for at, j in ((early_at, 0), (1 - early_at, 2)):
                 conv = jnp.where(at == 0, top, bot)
-                value = row_ref[i, j + 1] * (conv + skip * row_ref[i, j])
+                value = row_ref[i, j + 1, :rows] * (conv + skip * row_ref[i, j, :rows])
                 out_ref[pl.ds(pl.multiple_of(at * FINE, FINE), FINE), cols[i]] = value.astype(bf16)
 
     return pl.pallas_call(
@@ -465,7 +489,7 @@
         out_shape=jax.ShapeDtypeStruct((2 * rows, channels), bf16),
         scratch_shapes=[
             pltpu.VMEM(conv.shape, bf16),
-            pltpu.VMEM((tiles, 4, rows, LANES), f32),
+            pltpu.VMEM((tiles, 4, rows + PAD, LANES), f32),
             pltpu.VMEM((1, channels), f32),
             pltpu.SemaphoreType.DMA((tiles, 4)),
             pltpu.SemaphoreType.DMA((tiles,)),
@@ -504,42 +528,49 @@
             bit //= 2
         return [blocks[mask] for mask in range(mid)]
 
-    start = [(c * tensor_count - 1, c * tensor_count) for c in range(1, dev_count)]
-    inner = [(c * tensor_count + mid - 1, c * tensor_count) for c in range(dev_count)]
-
-    def halo(tail, first, second):
-        total = jnp.zeros_like(tail)
-        for j in range(mid):
-            pairs = [(a, b + first + j) for a, b in start] + [(a, b + second + j) for a, b in inner]
-            total = total + lax.ppermute(tail, ("context", "tensor"), pairs)
-        return jnp.concatenate([jnp.zeros((PAD - TAIL, tail.shape[1]), bf16), total], axis=0)
-
     normed, tail = norm_rows(tokens, norm_gain)
-    normed, early_halo = lax.optimization_barrier((normed, halo(tail, 0, mid)))
     crossed = swap(normed, mid)
     early_blocks = gathered(normed)
-    early_halo, late_halo = lax.optimization_barrier((early_halo, halo(tail, mid, 0)))
-
+
+    late_halo = jnp.zeros_like(tail)
+    for j in range(mid):
+        pairs = [(c * tensor_count - 1, c * tensor_count + mid + j) for c in range(1, dev_count)]
+        pairs += [(c * tensor_count + mid - 1, c * tensor_count + j) for c in range(dev_count)]
+        late_halo = late_halo + lax.ppermute(tail, ("context", "tensor"), pairs)
+    head = sum(jnp.where(place == mask, block[:PAD], 0) for mask, block in enumerate(early_blocks))
+    early_blocks, late_halo = lax.optimization_barrier((early_blocks, late_halo))
+    early_halo = swap(late_halo, mid)
+
+    packs = None
     if packed:
         early_gated, packs = project(
-            (1, 2), place, early_halo, early_blocks, weight, short_weight, COST[0], long_filter
+            (1, 2), place, early_blocks, weight, short_weight, COST[0], filt=long_filter
         )
     else:
-        early_gated, _ = project((1, 2), place, early_halo, early_blocks, weight, short_weight, COST[0])
+        early_gated, _ = project((1, 2), place, early_blocks, weight, short_weight, COST[0])
         packs = [pack_any(rows, dev_count) for rows in (early_gated, long_filter)]
         packs = jnp.concatenate(packs, axis=1)
     early_sent = exchange(packs)
     crossed, _ = lax.optimization_barrier((crossed, packs))
     late_blocks = gathered(crossed)
-    late_gated, packs = project((1, 2), place, late_halo, late_blocks, weight, short_weight, COST[1])
-    late_sent = exchange(packs if packed else pack_any(late_gated, dev_count))
+    gap = jnp.zeros((PAD - TAIL, tail.shape[1]), bf16)
+    late_ext = jnp.concatenate([gap, late_halo, gap, early_halo, head], axis=0)
+    late_gated, packs = project((1, 2), place, late_blocks, weight, short_weight, COST[1], ext=late_ext)
+    if not packed:
+        rows = late_gated.shape[0] - PAD
+        packs = [pack_any(late_gated[:rows], dev_count), pack_any(late_gated[rows:], dev_count)]
+        packs = jnp.concatenate(packs, axis=1)
+    late_sent = exchange(packs)
     spectrum = filter_spectrum(early_sent, consts)
-    (late_query,) = project((0,), place, late_halo, late_blocks, weight, short_weight, COST[2])
-    (early_query,) = project((0,), place, early_halo, early_blocks, weight, short_weight, COST[2])
+    early_ext = jnp.concatenate([gap, early_halo], axis=0)
+    (early_query,) = project((0,), place, early_blocks, weight, short_weight, COST[2], ext=early_ext)
+    (late_query,) = project((0,), place, late_blocks, weight, short_weight, COST[2], ext=late_ext[:PAD])
     conv = exchange(convolve(half, early_sent, late_sent, spectrum, consts))
     early, late = (early_gated, early_query), (late_gated, late_query)
     if packed:
         return finish(half, conv, early, late, skip_gain)
+    early_gated = jnp.concatenate([late_gated[rows:], early_gated[PAD:]], axis=0)
+    early, late = (early_gated, early_query), (late_gated[:rows], late_query)
     each = channels // dev_count
     conv = conv.reshape(dev_count, FINE, 2, HALF)[..., :each]
     conv = jnp.transpose(conv, (2, 1, 0, 3)).reshape(2 * FINE, channels).astype(f32)

time: 95.6 us -> 90.8 us (0.950)
  waiting for transfers between devices: 20.8 us -> 12.2 us
  starting transfers between devices: 24.5 us -> 27.9 us
  other arithmetic: 0.04 us -> 1.04 us
  local copies, waits for them, and re-layouts: 4.87 us -> 3.87 us
    all_to_all x1, starting transfers between devices: 5.85 us -> 10.3 us  [local(): early_sent = exchange(packs)]
    ppermute x3 -> x4, waiting for transfers between devices: 7.28 us -> 3.02 us  [swap(): lax.ppermute(x, 'tensor', [(i, i ^ bit) for i in range(tensor_count)])]
    all_to_all x1, waiting for transfers between devices: 4.45 us -> 2.09 us  [local(): early_sent = exchange(packs)]
    ppermute x4 -> x2, waiting for transfers between devices: 2.04 us -> 0.1 us  [local(): late_halo = late_halo + lax.ppermute(tail, ('context', 'tensor'), pairs)]
    ppermute x4 -> x2, starting transfers between devices: 3.27 us -> 1.94 us  [local(): late_halo = late_halo + lax.ppermute(tail, ('context', 'tensor'), pairs)]
    concatenate x0 -> x1, other arithmetic: none -> 1.02 us  [local(): late_ext = jnp.concatenate([gap, late_halo, gap, early_halo, head], axis=0)]
    unnamed x12 -> x18, local copies, waits for them, and re-layouts: 3.54 us -> 2.56 us
    ppermute x3 -> x4, starting transfers between devices: 8.11 us -> 7.42 us  [swap(): lax.ppermute(x, 'tensor', [(i, i ^ bit) for i in range(tensor_count)])]
  transfers between devices with their start and end apart: 10 -> 9, of which waited for: 6 -> 6; matrix products, arithmetic and copies ran while one was open for 1% -> 3% of each run, Pallas kernels for 33% -> 36%
where the time goes in v3:
time: 90.8 us; the launch traced here: 90.3 us
  Pallas kernels  45 us (50%)
  starting transfers between devices  27.9 us (31%)
  waiting for transfers between devices  12.2 us (13%)
  local copies, waits for them, and re-layouts  3.87 us (4%)
  other arithmetic  1.04 us (1%)
    pallas_call x4, Pallas kernels, project(): pl.pallas_call(functools.partial(project_kernel, len(blocks), parts, spli...  26.5 us
    all_to_all x1, starting transfers between devices, local(): early_sent = exchange(packs)  10.3 us
    ppermute x4, starting transfers between devices, swap(): lax.ppermute(x, 'tensor', [(i, i ^ bit) for i in range(tensor_count)])  7.42 us
    pallas_call x1, Pallas kernels, convolve(): pl.pallas_call(functools.partial(conv_kernel, dev_count), in_specs=[pl.Bl...  7.03 us
    pallas_call x1, Pallas kernels, filter_spectrum(): pl.pallas_call(functools.partial(filter_kernel, dev_count), in_specs=[ANY...  5.68 us
    all_to_all x1, starting transfers between devices, local(): late_sent = exchange(packs)  4.53 us
    all_to_all x1, waiting for transfers between devices, local(): late_sent = exchange(packs)  4.14 us
    all_to_all x1, starting transfers between devices, local(): conv = exchange(convolve(half, early_sent, late_sent, spectrum, consts))  3.69 us
  transfers between devices with their start and end apart: 9, of which 6 were waited for; matrix products, arithmetic and copies ran while one was open for 3% of the time, Pallas kernels for 36%

profile of v3, /device:TPU:0, one launch (start us, length us, event | category | flops | bytes accessed | tf_op | source)
XLA Modules:
  0.0 90.3 jit_solution(14095447329597253380)
XLA Ops:
  0.0 2.7 %norm_rows.1 = (bf16[128,4096]{1,0:T(8,128)(2,1)}, bf16[8,4096]{1,0:T(8,128)(2,1)}) custom-call(bf16[128,4096]{1,0:T(8,128)(2,1)} %tok_hbm.1, f32[1,4096]{1,0:T(1,128)} %bitcast.11), custom_call_target="tpu_custom_call" | custom-call | tf_op jit(solution)/shard_map/norm_rows/pallas_call | solution.py:87
  2.7 0.5 collective-permute-start
  3.2 0.7 collective-permute-start.2
  3.9 1.3 %collective-permute-start.1 = (bf16[8,4096]{1,0:T(8,128)(2,1)}, bf16[8,4096]{1,0:T(8,128)(2,1)S(1)}, u32[]{:S(2)}, u32[]{:S(2)}) collective-permute-start(bf16[8,4096]{1,0:T(8,128)(2,1)} %get-tuple-element.16), channel_id=1, source_target_pairs={{3,6},{7,10},{11,14},{15,18},{19,22},{23,26},{27,30},{1,0},{5,4},{... | collective-permute-start | bytes 196616 | tf_op jit(solution)/shard_map/ppermute | solution.py:539
  5.2 1.9 %collective-permute-start.3 = (bf16[128,4096]{1,0:T(8,128)(2,1)}, bf16[128,4096]{1,0:T(8,128)(2,1)S(1)}, u32[]{:S(2)}, u32[]{:S(2)}) collective-permute-start(bf16[128,4096]{1,0:T(8,128)(2,1)} %get-tuple-element.17.refs_0_), channel_id=1, source_target_pairs={{0,2},{1,3},{2,0},{3,1},{4,6},{5,7},{6,4},{7,5},{8,10},{9,11},{10,... | collective-permute-start | bytes 3145736 | tf_op jit(solution)/shard_map/ppermute | solution.py:520
  7.2 0.0 collective-permute-done.2
  7.2 0.1 collective-permute-done.1
  7.3 0.0 collective-permute-done.refs_1_
  7.3 0.0 copy-start.1
  7.3 1.3 %collective-permute-start.5 = (bf16[8,4096]{1,0:T(8,128)(2,1)S(1)}, bf16[8,4096]{1,0:T(8,128)(2,1)S(1)}, u32[]{:S(2)}, u32[]{:S(2)}) collective-permute-start(bf16[8,4096]{1,0:T(8,128)(2,1)S(1)} %add.16), channel_id=1, source_target_pairs={{0,2},{1,3},{2,0},{3,1},{4,6},{5,7},{6,4},{7,5},{8,10},{9,11},{10,... | collective-permute-start | bytes 196616 | tf_op jit(solution)/shard_map/ppermute | solution.py:520
  8.6 0.0 copy-done.1
  8.6 8.0 %project.4 = (f32[256,512]{1,0:T(8,128)}, bf16[8,384,128]{2,1,0:T(8,128)(2,1)}) custom-call(s32[1]{0:T(128)} %bitcast.1.me_ref, bf16[128,4096]{1,0:T(8,128)(2,1)} %get-tuple-element.17.refs_0_, bf16[128,4096]{1,0:T(8,128)(2,1)} %copy-done.1, bf16[3,4096,512]{2,1,0:T(8,128)(2,1)} %bitcast.7, f32[3,3,512]{2,1,0:T(4,128)} %refs_3_.9, f32[512,512]{1,0:T(8,128)} %refs_4_.1), custom_call_target="tpu_custom_call" | custom-call | flops 100000000 | bytes 100000 | tf_op jit(solution)/shard_map/project/pallas_call | solution.py:197
  16.6 10.3 %all-to-all-start = ((bf16[8,384,128]{2,1,0:T(8,128)(2,1)}), bf16[8,384,128]{2,1,0:T(8,128)(2,1)S(1)}, u32[]{:S(2)}, u32[]{:S(2)}) async-start(bf16[8,384,128]{2,1,0:T(8,128)(2,1)} %get-tuple-element.19), calls=%async_computation | async-start | bytes 1572864 | tf_op jit(solution)/shard_map/all_to_all | solution.py:553
  26.9 1.8 %collective-permute-done.3.refs_0_ = bf16[128,4096]{1,0:T(8,128)(2,1)S(1)} collective-permute-done((bf16[128,4096]{1,0:T(8,128)(2,1)}, bf16[128,4096]{1,0:T(8,128)(2,1)S(1)}, u32[]{:S(2)}, u32[]{:S(2)}) %collective-permute-start.3) | collective-permute-done | bytes 1048608 | tf_op jit(solution)/shard_map/ppermute | solution.py:520
  28.7 0.0 copy-start.2
  28.7 3.7 %collective-permute-start.4 = (bf16[128,4096]{1,0:T(8,128)(2,1)S(1)}, bf16[128,4096]{1,0:T(8,128)(2,1)S(1)}, u32[]{:S(2)}, u32[]{:S(2)}) collective-permute-start(bf16[128,4096]{1,0:T(8,128)(2,1)S(1)} %collective-permute-done.3.refs_0_), channel_id=1, source_target_pairs={{0,1},{1,0},{2,3},{3,2},{4,5},{5,4},{6,7},{7,6},{8,9},{9,8},{10,11... | collective-permute-start | bytes 3145736 | tf_op jit(solution)/shard_map/ppermute | solution.py:520
  32.3 0.0 collective-permute-done.5
  32.3 1.0 %fusion.1.refs_4_ = bf16[48,4096]{1,0:T(8,128)(2,1)S(1)} fusion(bf16[48,4096]{1,0:T(8,128)(2,1)S(1)} %constant_dynamic-update-slice_fusion, bf16[128,4096]{1,0:T(8,128)(2,1)} %copy-done.1, bf16[128,4096]{1,0:T(8,128)(2,1)} %get-tuple-element.17.refs_0_, pred[]{:T(512)} %bitcast.5, pred[]{:T(512)} %bitcast.4), kind=kLoop, calls=%fused_computation.2 | loop fusion | flops 393216 | bytes 393218 | tf_op jit(solution)/shard_map/concatenate | solution.py:557
  33.4 0.0 copy-start.6
  33.4 1.2 %collective-permute-done.4.refs_1_ = bf16[128,4096]{1,0:T(8,128)(2,1)S(1)} collective-permute-done((bf16[128,4096]{1,0:T(8,128)(2,1)S(1)}, bf16[128,4096]{1,0:T(8,128)(2,1)S(1)}, u32[]{:S(2)}, u32[]{:S(2)}) %collective-permute-start.4) | collective-permute-done | bytes 1048608 | tf_op jit(solution)/shard_map/ppermute | solution.py:520
  34.6 0.0 copy-done.2
  34.6 0.0 copy-done.6
  34.6 0.0 copy-start.3
  34.6 1.0 %copy-done.3 = bf16[128,4096]{1,0:T(8,128)(2,1)} copy-done((bf16[128,4096]{1,0:T(8,128)(2,1)}, bf16[128,4096]{1,0:T(8,128)(2,1)S(1)}, u32[]{:S(2)}) %copy-start.3) | copy-done | bytes 1048600
  35.6 8.1 %project.5 = (f32[272,512]{1,0:T(8,128)}, bf16[8,136,128]{2,1,0:T(8,128)(2,1)}) custom-call(s32[1]{0:T(128)} %bitcast.1.me_ref, bf16[128,4096]{1,0:T(8,128)(2,1)} %copy-done.2, bf16[128,4096]{1,0:T(8,128)(2,1)} %copy-done.3, bf16[3,4096,512]{2,1,0:T(8,128)(2,1)} %bitcast.8, f32[3,3,512]{2,1,0:T(4,128)} %refs_3_.9, bf16[48,4096]{1,0:T(8,128)(2,1)} %copy-done.6), custom_call_target="tpu_custom_call" | custom-call | flops 100000000 | bytes 100000 | tf_op jit(solution)/shard_map/project/pallas_call | solution.py:197
  43.7 2.1 %all-to-all-done.x_any.early_any = bf16[8,384,128]{2,1,0:T(8,128)(2,1)S(1)} async-done(((bf16[8,384,128]{2,1,0:T(8,128)(2,1)}), bf16[8,384,128]{2,1,0:T(8,128)(2,1)S(1)}, u32[]{:S(2)}, u32[]{:S(2)}) %all-to-all-start) | async-done | bytes 786464 | tf_op jit(solution)/shard_map/all_to_all | solution.py:553
  45.8 0.0 copy-start
  45.8 4.5 %all-to-all-start.1 = ((bf16[8,136,128]{2,1,0:T(8,128)(2,1)}), bf16[8,136,128]{2,1,0:T(8,128)(2,1)S(1)}, u32[]{:S(2)}, u32[]{:S(2)}) async-start(bf16[8,136,128]{2,1,0:T(8,128)(2,1)} %get-tuple-element.22), calls=%async_computation.1 | async-start | bytes 557056 | tf_op jit(solution)/shard_map/all_to_all | solution.py:563
  50.4 0.0 copy-done
  50.4 5.7 %filter_spectrum.1.h_hbm = f32[9,256,256]{2,1,0:T(8,128)} custom-call(bf16[8,384,128]{2,1,0:T(8,128)(2,1)} %copy-done, f32[256,256]{1,0:T(8,128)} %constant.44.clone.refs_0_, f32[256,256]{1,0:T(8,128)} %constant.45.clone.refs_1_, f32[9,2,128]{2,1,0:T(2,128)} %constant.46.clone.refs_2_, bf16[512,256]{1,0:T(8,128)(2,1)} %constant.47.clone.refs_3_), custom_call_target="tpu_custom_call" | custom-call | tf_op jit(solution)/shard_map/filter_spectrum/pallas_call | solution.py:420
  56.0 4.1 %all-to-all-done.1.late_any = bf16[8,136,128]{2,1,0:T(8,128)(2,1)S(1)} async-done(((bf16[8,136,128]{2,1,0:T(8,128)(2,1)}), bf16[8,136,128]{2,1,0:T(8,128)(2,1)S(1)}, u32[]{:S(2)}, u32[]{:S(2)}) %all-to-all-start.1) | async-done | bytes 278560 | tf_op jit(solution)/shard_map/all_to_all | solution.py:563
  60.2 0.0 copy-start.5
  60.2 0.7 copy-done.5
  60.9 7.0 %convolve.1 = bf16[8,256,128]{2,1,0:T(8,128)(2,1)} custom-call(s32[1]{0:T(128)} %bitcast.half_ref, bf16[8,384,128]{2,1,0:T(8,128)(2,1)} %copy-done, bf16[8,136,128]{2,1,0:T(8,128)(2,1)} %copy-done.5, f32[9,256,256]{2,1,0:T(8,128)} %filter_spectrum.1.h_hbm, f32[256,256]{1,0:T(8,128)} %constant.44.clone.refs_0_, f32[256,256]{1,0:T(8,128)} %constant.45.clone.refs_1_, ...), custom_call_target="tpu_custom_call" | custom-call | tf_op jit(solution)/shard_map/convolve/pallas_call | solution.py:435
  67.9 3.7 %all-to-all-start.2 = ((bf16[8,256,128]{2,1,0:T(8,128)(2,1)}), bf16[8,256,128]{2,1,0:T(8,128)(2,1)S(1)}, u32[]{:S(2)}, u32[]{:S(2)}) async-start(bf16[8,256,128]{2,1,0:T(8,128)(2,1)} %convolve.1), calls=%async_computation.2 | async-start | bytes 1048576 | tf_op jit(solution)/shard_map/all_to_all | solution.py:568
  71.6 0.7 concatenate.11.refs_4_
  72.3 0.7 concatenate.10.refs_4_
  73.0 5.2 %project.6.qe_hbm = f32[256,512]{1,0:T(8,128)} custom-call(s32[1]{0:T(128)} %bitcast.1.me_ref, bf16[128,4096]{1,0:T(8,128)(2,1)} %get-tuple-element.17.refs_0_, bf16[128,4096]{1,0:T(8,128)(2,1)} %copy-done.1, bf16[3,4096,512]{2,1,0:T(8,128)(2,1)} %bitcast.9, f32[3,3,512]{2,1,0:T(4,128)} %refs_3_.9, bf16[16,4096]{1,0:T(8,128)(2,1)} %concatenate.10.refs_4_), custom_call_target="tpu_custom_call" | custom-call | flops 100000000 | bytes 100000 | tf_op jit(solution)/shard_map/project/pallas_call | solution.py:197
  78.2 5.2 %project.7.ql_hbm = f32[256,512]{1,0:T(8,128)} custom-call(s32[1]{0:T(128)} %bitcast.1.me_ref, bf16[128,4096]{1,0:T(8,128)(2,1)} %copy-done.2, bf16[128,4096]{1,0:T(8,128)(2,1)} %copy-done.3, bf16[3,4096,512]{2,1,0:T(8,128)(2,1)} %bitcast.10, f32[3,3,512]{2,1,0:T(4,128)} %refs_3_.9, bf16[16,4096]{1,0:T(8,128)(2,1)} %concatenate.11.refs_4_), custom_call_target="tpu_custom_call" | custom-call | flops 100000000 | bytes 100000 | tf_op jit(solution)/shard_map/project/pallas_call | solution.py:197
  83.4 2.9 %all-to-all-done.2.c_any = bf16[8,256,128]{2,1,0:T(8,128)(2,1)S(1)} async-done(((bf16[8,256,128]{2,1,0:T(8,128)(2,1)}), bf16[8,256,128]{2,1,0:T(8,128)(2,1)S(1)}, u32[]{:S(2)}, u32[]{:S(2)}) %all-to-all-start.2) | async-done | bytes 524320 | tf_op jit(solution)/shard_map/all_to_all | solution.py:568
  86.3 0.0 copy-start.4
  86.3 0.8 copy-done.4
  87.1 3.1 %finish.1 = bf16[512,512]{1,0:T(8,128)(2,1)} custom-call(s32[1]{0:T(128)} %bitcast.half_ref, bf16[8,256,128]{2,1,0:T(8,128)(2,1)} %copy-done.4, f32[256,512]{1,0:T(8,128)} %get-tuple-element.23.ge_hbm, f32[256,512]{1,0:T(8,128)} %project.6.qe_hbm, f32[272,512]{1,0:T(8,128)} %get-tuple-element.24.gl_hbm, f32[256,512]{1,0:T(8,128)} %project.7.ql_hbm, ...), custom_call_target="tpu_custom_call" | custom-call | tf_op jit(solution)/shard_map/finish/pallas_call | solution.py:485
  (5 shorter events, 0.0 us)
Async XLA Ops:
  2.7 4.6 %collective-permute-start = (bf16[128,4096]{1,0:T(8,128)(2,1)}, bf16[128,4096]{1,0:T(8,128)(2,1)S(1)}, u32[]{:S(2)}, u32[]{:S(2)}) collective-permute-start(bf16[128,4096]{1,0:T(8,128)(2,1)} %get-tuple-element.17.refs_0_), channel_id=1, source_target_pairs={{0,1},{1,0},{2,3},{3,2},{4,5},{5,4},{6,7},{7,6},{8,9},{9,8},{10,11... | collective-permute-start | bytes 3145736 | tf_op jit(solution)/shard_map/ppermute | solution.py:520
  3.2 3.9 %collective-permute-start.2 = (bf16[8,4096]{1,0:T(8,128)(2,1)}, bf16[8,4096]{1,0:T(8,128)(2,1)S(1)}, u32[]{:S(2)}, u32[]{:S(2)}) collective-permute-start(bf16[8,4096]{1,0:T(8,128)(2,1)} %get-tuple-element.16), channel_id=1, source_target_pairs={{3,7},{7,11},{11,15},{15,19},{19,23},{23,27},{27,31},{1,1},{5,5},{... | collective-permute-start | bytes 196616 | tf_op jit(solution)/shard_map/ppermute | solution.py:539
  3.9 3.4 %collective-permute-start.1 = (bf16[8,4096]{1,0:T(8,128)(2,1)}, bf16[8,4096]{1,0:T(8,128)(2,1)S(1)}, u32[]{:S(2)}, u32[]{:S(2)}) collective-permute-start(bf16[8,4096]{1,0:T(8,128)(2,1)} %get-tuple-element.16), channel_id=1, source_target_pairs={{3,6},{7,10},{11,14},{15,18},{19,22},{23,26},{27,30},{1,0},{5,4},{... | collective-permute-start | bytes 196616 | tf_op jit(solution)/shard_map/ppermute | solution.py:539
  5.2 23.5 %collective-permute-start.3 = (bf16[128,4096]{1,0:T(8,128)(2,1)}, bf16[128,4096]{1,0:T(8,128)(2,1)S(1)}, u32[]{:S(2)}, u32[]{:S(2)}) collective-permute-start(bf16[128,4096]{1,0:T(8,128)(2,1)} %get-tuple-element.17.refs_0_), channel_id=1, source_target_pairs={{0,2},{1,3},{2,0},{3,1},{4,6},{5,7},{6,4},{7,5},{8,10},{9,11},{10,... | collective-permute-start | bytes 3145736 | tf_op jit(solution)/shard_map/ppermute | solution.py:520
  7.3 1.3 %copy-start.1 = (bf16[128,4096]{1,0:T(8,128)(2,1)}, bf16[128,4096]{1,0:T(8,128)(2,1)S(1)}, u32[]{:S(2)}) copy-start(bf16[128,4096]{1,0:T(8,128)(2,1)S(1)} %collective-permute-done.refs_1_) | copy-start | bytes 3145732
  7.3 25.0 %collective-permute-start.5 = (bf16[8,4096]{1,0:T(8,128)(2,1)S(1)}, bf16[8,4096]{1,0:T(8,128)(2,1)S(1)}, u32[]{:S(2)}, u32[]{:S(2)}) collective-permute-start(bf16[8,4096]{1,0:T(8,128)(2,1)S(1)} %add.16), channel_id=1, source_target_pairs={{0,2},{1,3},{2,0},{3,1},{4,6},{5,7},{6,4},{7,5},{8,10},{9,11},{10,... | collective-permute-start | bytes 196616 | tf_op jit(solution)/shard_map/ppermute | solution.py:520
  16.6 29.2 %all-to-all-start = ((bf16[8,384,128]{2,1,0:T(8,128)(2,1)}), bf16[8,384,128]{2,1,0:T(8,128)(2,1)S(1)}, u32[]{:S(2)}, u32[]{:S(2)}) async-start(bf16[8,384,128]{2,1,0:T(8,128)(2,1)} %get-tuple-element.19), calls=%async_computation | async-start | bytes 1572864 | tf_op jit(solution)/shard_map/all_to_all | solution.py:553
  28.7 5.9 %copy-start.2 = (bf16[128,4096]{1,0:T(8,128)(2,1)}, bf16[128,4096]{1,0:T(8,128)(2,1)S(1)}, u32[]{:S(2)}) copy-start(bf16[128,4096]{1,0:T(8,128)(2,1)S(1)} %collective-permute-done.3.refs_0_) | copy-start | bytes 3145732
  28.7 5.9 %collective-permute-start.4 = (bf16[128,4096]{1,0:T(8,128)(2,1)S(1)}, bf16[128,4096]{1,0:T(8,128)(2,1)S(1)}, u32[]{:S(2)}, u32[]{:S(2)}) collective-permute-start(bf16[128,4096]{1,0:T(8,128)(2,1)S(1)} %collective-permute-done.3.refs_0_), channel_id=1, source_target_pairs={{0,1},{1,0},{2,3},{3,2},{4,5},{5,4},{6,7},{7,6},{8,9},{9,8},{10,11... | collective-permute-start | bytes 3145736 | tf_op jit(solution)/shard_map/ppermute | solution.py:520
  33.4 1.3 %copy-start.6 = (bf16[48,4096]{1,0:T(8,128)(2,1)}, bf16[48,4096]{1,0:T(8,128)(2,1)S(1)}, u32[]{:S(2)}) copy-start(bf16[48,4096]{1,0:T(8,128)(2,1)S(1)} %fusion.1.refs_4_) | copy-start | bytes 1179652
  34.6 1.0 %copy-start.3 = (bf16[128,4096]{1,0:T(8,128)(2,1)}, bf16[128,4096]{1,0:T(8,128)(2,1)S(1)}, u32[]{:S(2)}) copy-start(bf16[128,4096]{1,0:T(8,128)(2,1)S(1)} %collective-permute-done.4.refs_1_) | copy-start | bytes 3145732
  45.8 4.5 %copy-start = (bf16[8,384,128]{2,1,0:T(8,128)(2,1)}, bf16[8,384,128]{2,1,0:T(8,128)(2,1)S(1)}, u32[]{:S(2)}) copy-start(bf16[8,384,128]{2,1,0:T(8,128)(2,1)S(1)} %all-to-all-done.x_any.early_any) | copy-start | bytes 2359300
  45.8 14.4 %all-to-all-start.1 = ((bf16[8,136,128]{2,1,0:T(8,128)(2,1)}), bf16[8,136,128]{2,1,0:T(8,128)(2,1)S(1)}, u32[]{:S(2)}, u32[]{:S(2)}) async-start(bf16[8,136,128]{2,1,0:T(8,128)(2,1)} %get-tuple-element.22), calls=%async_computation.1 | async-start | bytes 557056 | tf_op jit(solution)/shard_map/all_to_all | solution.py:563
  60.2 0.7 copy-start.5
  67.9 18.3 %all-to-all-start.2 = ((bf16[8,256,128]{2,1,0:T(8,128)(2,1)}), bf16[8,256,128]{2,1,0:T(8,128)(2,1)S(1)}, u32[]{:S(2)}, u32[]{:S(2)}) async-start(bf16[8,256,128]{2,1,0:T(8,128)(2,1)} %convolve.1), calls=%async_computation.2 | async-start | bytes 1048576 | tf_op jit(solution)/shard_map/all_to_all | solution.py:568
  86.3 0.8 copy-start.4

commit v4 on v3

--- a/solution.py
+++ b/solution.py
@@ -69,29 +69,34 @@
     rows, width = tokens.shape
     step = min(32, rows)
 
-    def kernel(tok_hbm, gain_hbm, out_ref, tail_ref, tok_ref, gain_ref, sem):
+    def kernel(tok_hbm, gain_hbm, out_any, tail_any, tok_ref, gain_ref, out_ref, sem, out_sem):
         parts = [pl.ds(i * step, step) for i in range(rows // step)]
         copies = start_all(
             [(gain_hbm, gain_ref, sem.at[len(parts)])]
             + [(tok_hbm.at[part], tok_ref.at[part], sem.at[i]) for i, part in enumerate(parts)]
         )
         copies[0].wait()
-        for part, copy in zip(parts, copies[1:]):
-            copy.wait()
+        sends = []
+        for i, part in enumerate(parts):
+            copies[1 + i].wait()
             values = tok_ref[part, :].astype(f32)
             inv_rms = lax.rsqrt(jnp.mean(values * values, axis=1, keepdims=True) + eps)
-            normed = (values * inv_rms * gain_ref[...]).astype(bf16)
-            out_ref[part, :] = normed
-            tail_ref[...] = normed[step - TAIL :]
+            out_ref[part, :] = (values * inv_rms * gain_ref[...]).astype(bf16)
+            sends += start_all([(out_ref.at[part], out_any.at[part], out_sem.at[i])])
+        sends += start_all([(out_ref.at[pl.ds(rows - TAIL, TAIL)], tail_any, out_sem.at[len(parts)])])
+        for send in sends:
+            send.wait()
 
     return pl.pallas_call(
         kernel,
         in_specs=[HBM_SPEC] * 2,
-        out_specs=[VMEM_SPEC] * 2,
+        out_specs=[ANY_SPEC] * 2,
         out_shape=[jax.ShapeDtypeStruct((rows, width), bf16), jax.ShapeDtypeStruct((TAIL, width), bf16)],
         scratch_shapes=[
             pltpu.VMEM((rows, width), bf16),
             pltpu.VMEM((1, width), f32),
+            pltpu.VMEM((rows, width), bf16),
+            pltpu.SemaphoreType.DMA((rows // step + 1,)),
             pltpu.SemaphoreType.DMA((rows // step + 1,)),
         ],
         compiler_params=pltpu.CompilerParams(vmem_limit_bytes=BIG),
@@ -110,8 +115,14 @@
 def project_kernel(count, parts, splits, ext_rows, with_filter, me_ref, *refs):
     blocks, refs = refs[:count], refs[count:]
     w_hbm, tap_hbm = refs[:2]
-    extra, outs = refs[2 : 2 + bool(ext_rows) + with_filter], refs[2 + bool(ext_rows) + with_filter : -8]
-    w_ref, tap_ref, x_ref, rows_ref, filt_ref, sem, w_sem, tap_sem = refs[-8:]
+    extra, refs = refs[2 : 2 + bool(ext_rows) + with_filter], refs[2 + bool(ext_rows) + with_filter :]
+    number = 2 * (1 in parts) + (0 in parts)
+    out_any, outs, refs = refs[:number], refs[number : 2 * number], refs[2 * number :]
+    w_ref, tap_ref, x_ref, rows_ref, filt_ref, sem, w_sem, tap_sem, out_sem = refs
+
+    def send(i):
+        return start_all([(outs[i], out_any[i], out_sem.at[i])])
+
     each = blocks[0].shape[0]
     length = each * count
     end = PAD + length
@@ -167,14 +178,19 @@
             g_ref[span, :] = key
         for span, value in zip(spans, mixed(2)):
             g_ref[span, :] *= value
+        sends = send(0)
         pack_into(p_ref, 0, g_ref, 0, length)
         if ext_rows > PAD:
             pack_into(p_ref, length // 2, g_ref, length, PAD)
+        if with_filter:
+            filt_load.wait()
+            pack_into(p_ref, length // 2, filt_ref, 0, filt_ref.shape[0])
+        sends += send(1)
     if 0 in parts:
         outs[-1][...] = mixed(0)[0]
-    if with_filter:
-        filt_load.wait()
-        pack_into(p_ref, length // 2, filt_ref, 0, filt_ref.shape[0])
+        sends = (sends if 1 in parts else []) + send(number - 1)
+    for copy in sends:
+        copy.wait()
 
 
 def project(parts, me, blocks, weight, taps, cost, ext=None, filt=None):
@@ -197,9 +213,10 @@
     return pl.pallas_call(
         functools.partial(project_kernel, len(blocks), parts, splits, ext_rows, filt is not None),
         in_specs=[pl.BlockSpec(memory_space=pltpu.SMEM)] + [ANY_SPEC] * (len(blocks) + 2 + len(extra)),
-        out_specs=[VMEM_SPEC] * len(shapes),
+        out_specs=[ANY_SPEC] * len(shapes),
         out_shape=shapes,
-        scratch_shapes=[
+        scratch_shapes=[pltpu.VMEM(x.shape, x.dtype) for x in shapes]
+        + [
             pltpu.VMEM((len(parts), width, channels), bf16),
             pltpu.VMEM(taps.shape, f32),
             pltpu.VMEM((rows, width), bf16),
@@ -208,6 +225,7 @@
             pltpu.SemaphoreType.DMA((len(blocks) + 3,)),
             pltpu.SemaphoreType.DMA((len(parts), splits)),
             pltpu.SemaphoreType.DMA,
+            pltpu.SemaphoreType.DMA((len(shapes),)),
         ],
         compiler_params=pltpu.CompilerParams(vmem_limit_bytes=BIG),
         cost_estimate=pl.CostEstimate(flops=cost, bytes_accessed=10**5, transcendentals=0),
@@ -215,7 +233,7 @@
     )(me, *blocks, weight, taps, *extra)
 
 
-def coarse_forward(dev_count, x_ref, lane_ref, e_ref, step=16):
+def coarse_forward(dev_count, x_ref, lane_ref, e_ref, step=32):
     count = dev_count
     half = count // 2
     low = lane_mask()
@@ -255,7 +273,7 @@
     lax.fori_loop(0, FINE // step, body, 0)
 
 
-def coarse_inverse(dev_count, g_ref, y_ref, step=16):
+def coarse_inverse(dev_count, g_ref, y_ref, first, length, step=32):
     count = dev_count
     half = count // 2
 
@@ -295,7 +313,7 @@
             y_ref[count - s, rows, :] = (total - diff).astype(bf16)
         return carry
 
-    lax.fori_loop(0, FINE // step, body, 0)
+    lax.fori_loop(first // step, (first + length) // step, body, 0)
 
 
 def fine_forward(e, tr, ti, table):
@@ -352,17 +370,18 @@
 
 
 def conv_kernel(dev_count, half_ref, early_any, late_any, h_hbm, *refs):
-    const_hbm, y_ref = refs[:4], refs[4]
-    early_ref, late_ref, x_ref, h_ref, first_ref, step_ref, lane_ref, table_ref, e_ref, sem = refs[5:]
+    const_hbm, y_any = refs[:4], refs[4]
+    early_ref, late_ref, x_ref, h_ref, first_ref, step_ref, lane_ref, table_ref, e_ref, y_ref, sem, y_sem = refs[5:]
     turn_ref = first_ref
-    pairs = [(early_any.at[:, pl.ds(0, FINE // 2)], early_ref), (late_any, late_ref)]
-    pairs += list(zip(const_hbm, (first_ref, step_ref, lane_ref, table_ref))) + [(h_hbm, h_ref)]
+    pairs = [(early_any.at[:, pl.ds(0, FINE // 2)], early_ref), (late_any, late_ref), (const_hbm[2], lane_ref)]
+    pairs += [(const_hbm[0], first_ref), (const_hbm[1], step_ref), (const_hbm[3], table_ref), (h_hbm, h_ref)]
     copies = start_all((*pair, sem.at[i]) for i, pair in enumerate(pairs))
-    for copy in copies[:-1]:
+    for copy in copies[:3]:
         copy.wait()
     merge_halves(dev_count, half_ref[0], early_ref, late_ref, x_ref)
     coarse_forward(dev_count, x_ref, lane_ref, e_ref)
-    copies[-1].wait()
+    for copy in copies[3:]:
+        copy.wait()
     sgn = jnp.where(lane_mask(), 1.0, -1.0).astype(f32)
 
     def body(k, carry):
@@ -382,7 +401,13 @@
         return carry
 
     lax.fori_loop(0, dev_count + 1, body, 0, unroll=dev_count <= 8)
-    coarse_inverse(dev_count, e_ref, y_ref)
+    sends = []
+    for i in range(2):
+        rows = pl.ds(i * FINE // 2, FINE // 2)
+        coarse_inverse(dev_count, e_ref, y_ref, i * FINE // 2, FINE // 2)
+        sends += start_all([(y_ref.at[:, rows], y_any.at[:, rows], y_sem.at[i])])
+    for send in sends:
+        send.wait()
 
 
 def tables(dev_count):
@@ -435,7 +460,7 @@
     return pl.pallas_call(
         functools.partial(conv_kernel, dev_count),
         in_specs=[pl.BlockSpec(memory_space=pltpu.SMEM)] + [ANY_SPEC] * 2 + [HBM_SPEC] * 5,
-        out_specs=VMEM_SPEC,
+        out_specs=ANY_SPEC,
         out_shape=jax.ShapeDtypeStruct((dev_count, FINE, LANES), bf16),
         scratch_shapes=[
             pltpu.VMEM((dev_count, FINE // 2, LANES), bf16),
@@ -444,7 +469,12 @@
             pltpu.VMEM(spectrum.shape, f32),
         ]
         + const_scratch(consts)
-        + [pltpu.VMEM((dev_count + 1, FINE, 2 * LANES), f32), pltpu.SemaphoreType.DMA((7,))],
+        + [
+            pltpu.VMEM((dev_count + 1, FINE, 2 * LANES), f32),
+            pltpu.VMEM((dev_count, FINE, LANES), bf16),
+            pltpu.SemaphoreType.DMA((7,)),
+            pltpu.SemaphoreType.DMA((2,)),
+        ],
         compiler_params=pltpu.CompilerParams(vmem_limit_bytes=BIG),
         name="convolve",
     )(half, early, late, spectrum, *consts)
@@ -454,7 +484,9 @@
     rows, channels = early[0].shape
     tiles = channels // LANES
 
-    def kernel(half_ref, c_any, ge_hbm, qe_hbm, gl_hbm, ql_hbm, skip_hbm, out_ref, c_ref, row_ref, skip_ref, sem, c_sem, s_sem):
+    def kernel(half_ref, c_any, *refs):
+        src_hbm, skip_hbm, out_any = refs[:4], refs[4], refs[5]
+        c_ref, row_ref, skip_ref, out_ref, sem, c_sem, s_sem, out_sem = refs[6:]
         early_at = half_ref[0]
         cols = [pl.ds(i * LANES, LANES) for i in range(tiles)]
         skip_copy = start_all([(skip_hbm, skip_ref, s_sem)])[0]
@@ -466,11 +498,12 @@
                     [(c_any.at[pair], c_ref.at[pair], c_sem.at[i])]
                     + [
                         (src.at[:, cols[i]], row_ref.at[i, j, pl.ds(0, src.shape[0])], sem.at[i, j])
-                        for j, src in enumerate((ge_hbm, qe_hbm, gl_hbm, ql_hbm))
+                        for j, src in enumerate(src_hbm)
                     ]
                 )
             )
         skip_copy.wait()
+        sends = []
         for i in range(tiles):
             for copy in copies[i]:
                 copy.wait()
@@ -480,20 +513,25 @@
             for at, j in ((early_at, 0), (1 - early_at, 2)):
                 conv = jnp.where(at == 0, top, bot)
                 value = row_ref[i, j + 1, :rows] * (conv + skip * row_ref[i, j, :rows])
-                out_ref[pl.ds(pl.multiple_of(at * FINE, FINE), FINE), cols[i]] = value.astype(bf16)
+                out_ref[i, pl.ds(pl.multiple_of(at * FINE, FINE), FINE), :] = value.astype(bf16)
+            sends += start_all([(out_ref.at[i], out_any.at[:, cols[i]], out_sem.at[i])])
+        for send in sends:
+            send.wait()
 
     return pl.pallas_call(
         kernel,
         in_specs=[pl.BlockSpec(memory_space=pltpu.SMEM), ANY_SPEC] + [HBM_SPEC] * 5,
-        out_specs=VMEM_SPEC,
+        out_specs=ANY_SPEC,
         out_shape=jax.ShapeDtypeStruct((2 * rows, channels), bf16),
         scratch_shapes=[
             pltpu.VMEM(conv.shape, bf16),
             pltpu.VMEM((tiles, 4, rows + PAD, LANES), f32),
             pltpu.VMEM((1, channels), f32),
+            pltpu.VMEM((tiles, 2 * rows, LANES), bf16),
             pltpu.SemaphoreType.DMA((tiles, 4)),
             pltpu.SemaphoreType.DMA((tiles,)),
             pltpu.SemaphoreType.DMA,
+            pltpu.SemaphoreType.DMA((tiles,)),
         ],
         compiler_params=pltpu.CompilerParams(vmem_limit_bytes=BIG),
         name="finish",
@@ -532,15 +570,13 @@
     crossed = swap(normed, mid)
     early_blocks = gathered(normed)
 
+    early_blocks, tail = lax.optimization_barrier((early_blocks, tail))
     late_halo = jnp.zeros_like(tail)
     for j in range(mid):
         pairs = [(c * tensor_count - 1, c * tensor_count + mid + j) for c in range(1, dev_count)]
         pairs += [(c * tensor_count + mid - 1, c * tensor_count + j) for c in range(dev_count)]
         late_halo = late_halo + lax.ppermute(tail, ("context", "tensor"), pairs)
     head = sum(jnp.where(place == mask, block[:PAD], 0) for mask, block in enumerate(early_blocks))
-    early_blocks, late_halo = lax.optimization_barrier((early_blocks, late_halo))
-    early_halo = swap(late_halo, mid)
-
     packs = None
     if packed:
         early_gated, packs = project(
@@ -550,6 +586,8 @@
         early_gated, _ = project((1, 2), place, early_blocks, weight, short_weight, COST[0])
         packs = [pack_any(rows, dev_count) for rows in (early_gated, long_filter)]
         packs = jnp.concatenate(packs, axis=1)
+    packs, late_halo = lax.optimization_barrier((packs, late_halo))
+    early_halo = swap(late_halo, mid)
     early_sent = exchange(packs)
     crossed, _ = lax.optimization_barrier((crossed, packs))
     late_blocks = gathered(crossed)

time: 90.8 us -> 86.5 us (0.953)
  starting transfers between devices: 27.9 us -> 20.8 us
  waiting for transfers between devices: 12.2 us -> 16.7 us
  Pallas kernels: 45 us -> 43 us
    ppermute x4, waiting for transfers between devices: 3.02 us -> 7.13 us  [swap(): lax.ppermute(x, 'tensor', [(i, i ^ bit) for i in range(tensor_count)])]
    all_to_all x1, starting transfers between devices: 10.3 us -> 7.14 us  [local(): early_sent = exchange(packs)]
    ppermute x4, starting transfers between devices: 7.42 us -> 4.58 us  [swap(): lax.ppermute(x, 'tensor', [(i, i ^ bit) for i in range(tensor_count)])]
    all_to_all x1, starting transfers between devices: 4.53 us -> 3.46 us  [local(): late_sent = exchange(packs)]
    pallas_call x1, Pallas kernels: 7.03 us -> 6.03 us  [convolve(): pl.pallas_call(functools.partial(conv_kernel, dev_count), in_specs=[pl.Bl...]
  transfers between devices with their start and end apart: 9 -> 9, of which waited for: 6 -> 6; matrix products, arithmetic and copies ran while one was open for 3% -> 3% of each run, Pallas kernels for 36% -> 37%
where the time goes in v4:
time: 86.5 us; the launch traced here: 86 us
  Pallas kernels  43 us (50%)
  starting transfers between devices  20.8 us (24%)
  waiting for transfers between devices  16.7 us (19%)
  local copies, waits for them, and re-layouts  4.1 us (5%)
  other arithmetic  1.04 us (1%)
    pallas_call x4, Pallas kernels, project(): pl.pallas_call(functools.partial(project_kernel, len(blocks), parts, spli...  26.6 us
    all_to_all x1, starting transfers between devices, local(): early_sent = exchange(packs)  7.14 us
    ppermute x4, waiting for transfers between devices, swap(): lax.ppermute(x, 'tensor', [(i, i ^ bit) for i in range(tensor_count)])  7.13 us
    pallas_call x1, Pallas kernels, convolve(): pl.pallas_call(functools.partial(conv_kernel, dev_count), in_specs=[pl.Bl...  6.03 us
    pallas_call x1, Pallas kernels, filter_spectrum(): pl.pallas_call(functools.partial(filter_kernel, dev_count), in_specs=[ANY...  5.02 us
    ppermute x4, starting transfers between devices, swap(): lax.ppermute(x, 'tensor', [(i, i ^ bit) for i in range(tensor_count)])  4.58 us
    all_to_all x1, waiting for transfers between devices, local(): late_sent = exchange(packs)  4.5 us
    all_to_all x1, starting transfers between devices, local(): conv = exchange(convolve(half, early_sent, late_sent, spectrum, consts))  3.69 us
  transfers between devices with their start and end apart: 9, of which 6 were waited for; matrix products, arithmetic and copies ran while one was open for 3% of the time, Pallas kernels for 37%

profile of v4, /device:TPU:0, one launch (start us, length us, event | category | flops | bytes accessed | tf_op | source)
XLA Modules:
  0.0 86.0 jit_solution(16271304977755292384)
XLA Ops:
  0.0 2.5 %norm_rows.1 = (bf16[128,4096]{1,0:T(8,128)(2,1)}, bf16[8,4096]{1,0:T(8,128)(2,1)}) custom-call(bf16[128,4096]{1,0:T(8,128)(2,1)} %tok_hbm.1, f32[1,4096]{1,0:T(1,128)} %bitcast.11), custom_call_target="tpu_custom_call" | custom-call | tf_op jit(solution)/shard_map/norm_rows/pallas_call | solution.py:90
  2.5 0.5 collective-permute-start
  3.0 2.6 %collective-permute-start.3 = (bf16[128,4096]{1,0:T(8,128)(2,1)}, bf16[128,4096]{1,0:T(8,128)(2,1)S(1)}, u32[]{:S(2)}, u32[]{:S(2)}) collective-permute-start(bf16[128,4096]{1,0:T(8,128)(2,1)} %get-tuple-element.19.refs_0_), channel_id=1, source_target_pairs={{0,2},{1,3},{2,0},{3,1},{4,6},{5,7},{6,4},{7,5},{8,10},{9,11},{10,... | collective-permute-start | bytes 3145736 | tf_op jit(solution)/shard_map/ppermute | solution.py:558
  5.5 0.0 collective-permute-done.refs_1_
  5.6 0.0 copy-start.1
  5.6 0.7 collective-permute-start.2
  6.2 1.3 %collective-permute-start.1 = (bf16[8,4096]{1,0:T(8,128)(2,1)}, bf16[8,4096]{1,0:T(8,128)(2,1)S(1)}, u32[]{:S(2)}, u32[]{:S(2)}) collective-permute-start(bf16[8,4096]{1,0:T(8,128)(2,1)} %get-tuple-element.22), channel_id=1, source_target_pairs={{3,6},{7,10},{11,14},{15,18},{19,22},{23,26},{27,30},{1,0},{5,4},{... | collective-permute-start | bytes 196616 | tf_op jit(solution)/shard_map/ppermute | solution.py:578
  7.5 0.0 copy-done.1
  7.6 8.0 %project.4 = (f32[256,512]{1,0:T(8,128)}, bf16[8,384,128]{2,1,0:T(8,128)(2,1)}) custom-call(s32[1]{0:T(128)} %bitcast.1.me_ref, bf16[128,4096]{1,0:T(8,128)(2,1)} %get-tuple-element.19.refs_0_, bf16[128,4096]{1,0:T(8,128)(2,1)} %copy-done.1, bf16[3,4096,512]{2,1,0:T(8,128)(2,1)} %bitcast.7, f32[3,3,512]{2,1,0:T(4,128)} %refs_3_.9, f32[512,512]{1,0:T(8,128)} %refs_4_.1), custom_call_target="tpu_custom_call" | custom-call | flops 100000000 | bytes 100000 | tf_op jit(solution)/shard_map/project/pallas_call | solution.py:213
  15.6 0.0 collective-permute-done.2
  15.6 0.0 collective-permute-done.1
  15.6 7.1 %all-to-all-start = ((bf16[8,384,128]{2,1,0:T(8,128)(2,1)}), bf16[8,384,128]{2,1,0:T(8,128)(2,1)S(1)}, u32[]{:S(2)}, u32[]{:S(2)}) async-start(bf16[8,384,128]{2,1,0:T(8,128)(2,1)} %get-tuple-element.23), calls=%async_computation | async-start | bytes 1572864 | tf_op jit(solution)/shard_map/all_to_all | solution.py:591
  22.8 1.5 %collective-permute-start.5 = (bf16[8,4096]{1,0:T(8,128)(2,1)S(1)}, bf16[8,4096]{1,0:T(8,128)(2,1)S(1)}, u32[]{:S(2)}, u32[]{:S(2)}) collective-permute-start(bf16[8,4096]{1,0:T(8,128)(2,1)S(1)} %add.16), channel_id=1, source_target_pairs={{0,2},{1,3},{2,0},{3,1},{4,6},{5,7},{6,4},{7,5},{8,10},{9,11},{10,... | collective-permute-start | bytes 196616 | tf_op jit(solution)/shard_map/ppermute | solution.py:558
  24.3 5.5 %collective-permute-done.3.refs_0_ = bf16[128,4096]{1,0:T(8,128)(2,1)S(1)} collective-permute-done((bf16[128,4096]{1,0:T(8,128)(2,1)}, bf16[128,4096]{1,0:T(8,128)(2,1)S(1)}, u32[]{:S(2)}, u32[]{:S(2)}) %collective-permute-start.3) | collective-permute-done | bytes 1048608 | tf_op jit(solution)/shard_map/ppermute | solution.py:558
  29.8 0.0 copy-start.2
  29.8 0.0 collective-permute-start.4
  29.8 1.1 %collective-permute-done.5 = bf16[8,4096]{1,0:T(8,128)(2,1)S(1)} collective-permute-done((bf16[8,4096]{1,0:T(8,128)(2,1)S(1)}, bf16[8,4096]{1,0:T(8,128)(2,1)S(1)}, u32[]{:S(2)}, u32[]{:S(2)}) %collective-permute-start.5) | collective-permute-done | bytes 65568 | tf_op jit(solution)/shard_map/ppermute | solution.py:558
  30.9 1.0 %add_dynamic-update-slice_fusion.refs_4_ = bf16[48,4096]{1,0:T(8,128)(2,1)S(1)} fusion(bf16[48,4096]{1,0:T(8,128)(2,1)S(1)} %constant_dynamic-update-slice_fusion, bf16[128,4096]{1,0:T(8,128)(2,1)} %copy-done.1, bf16[128,4096]{1,0:T(8,128)(2,1)} %get-tuple-element.19.refs_0_, pred[]{:T(512)} %bitcast.5, pred[]{:T(512)} %bitcast.4), kind=kLoop, calls=%fused_computation | loop fusion | flops 393216 | bytes 393218 | tf_op jit(solution)/shard_map/concatenate | solution.py:595
  31.9 0.0 copy-start.6
  32.0 0.5 collective-permute-done.4.refs_1_
  32.4 0.0 copy-done.2
  32.4 0.3 copy-done.6
  32.7 0.0 copy-start.3
  32.7 1.0 %copy-done.3 = bf16[128,4096]{1,0:T(8,128)(2,1)} copy-done((bf16[128,4096]{1,0:T(8,128)(2,1)}, bf16[128,4096]{1,0:T(8,128)(2,1)S(1)}, u32[]{:S(2)}) %copy-start.3) | copy-done | bytes 1048600
  33.7 8.1 %project.5 = (f32[272,512]{1,0:T(8,128)}, bf16[8,136,128]{2,1,0:T(8,128)(2,1)}) custom-call(s32[1]{0:T(128)} %bitcast.1.me_ref, bf16[128,4096]{1,0:T(8,128)(2,1)} %copy-done.2, bf16[128,4096]{1,0:T(8,128)(2,1)} %copy-done.3, bf16[3,4096,512]{2,1,0:T(8,128)(2,1)} %bitcast.8, f32[3,3,512]{2,1,0:T(4,128)} %refs_3_.9, bf16[48,4096]{1,0:T(8,128)(2,1)} %copy-done.6), custom_call_target="tpu_custom_call" | custom-call | flops 100000000 | bytes 100000 | tf_op jit(solution)/shard_map/project/pallas_call | solution.py:213
  41.8 2.7 %all-to-all-done.x_any.early_any = bf16[8,384,128]{2,1,0:T(8,128)(2,1)S(1)} async-done(((bf16[8,384,128]{2,1,0:T(8,128)(2,1)}), bf16[8,384,128]{2,1,0:T(8,128)(2,1)S(1)}, u32[]{:S(2)}, u32[]{:S(2)}) %all-to-all-start) | async-done | bytes 786464 | tf_op jit(solution)/shard_map/all_to_all | solution.py:591
  44.5 0.0 copy-start
  44.5 3.5 %all-to-all-start.1 = ((bf16[8,136,128]{2,1,0:T(8,128)(2,1)}), bf16[8,136,128]{2,1,0:T(8,128)(2,1)S(1)}, u32[]{:S(2)}, u32[]{:S(2)}) async-start(bf16[8,136,128]{2,1,0:T(8,128)(2,1)} %get-tuple-element.26), calls=%async_computation.1 | async-start | bytes 557056 | tf_op jit(solution)/shard_map/all_to_all | solution.py:601
  47.9 0.0 copy-done
  48.0 5.0 %filter_spectrum.1.h_hbm = f32[9,256,256]{2,1,0:T(8,128)} custom-call(bf16[8,384,128]{2,1,0:T(8,128)(2,1)} %copy-done, f32[256,256]{1,0:T(8,128)} %constant.44.clone.refs_0_, f32[256,256]{1,0:T(8,128)} %constant.45.clone.refs_1_, f32[9,2,128]{2,1,0:T(2,128)} %constant.46.clone.refs_2_, bf16[512,256]{1,0:T(8,128)(2,1)} %constant.47.clone.refs_3_), custom_call_target="tpu_custom_call" | custom-call | tf_op jit(solution)/shard_map/filter_spectrum/pallas_call | solution.py:445
  53.0 4.5 %all-to-all-done.1.late_any = bf16[8,136,128]{2,1,0:T(8,128)(2,1)S(1)} async-done(((bf16[8,136,128]{2,1,0:T(8,128)(2,1)}), bf16[8,136,128]{2,1,0:T(8,128)(2,1)S(1)}, u32[]{:S(2)}, u32[]{:S(2)}) %all-to-all-start.1) | async-done | bytes 278560 | tf_op jit(solution)/shard_map/all_to_all | solution.py:601
  57.5 0.0 copy-start.5
  57.5 0.7 copy-done.5
  58.2 6.0 %convolve.1 = bf16[8,256,128]{2,1,0:T(8,128)(2,1)} custom-call(s32[1]{0:T(128)} %bitcast.half_ref, bf16[8,384,128]{2,1,0:T(8,128)(2,1)} %copy-done, bf16[8,136,128]{2,1,0:T(8,128)(2,1)} %copy-done.5, f32[9,256,256]{2,1,0:T(8,128)} %filter_spectrum.1.h_hbm, f32[256,256]{1,0:T(8,128)} %constant.44.clone.refs_0_, f32[256,256]{1,0:T(8,128)} %constant.45.clone.refs_1_, ...), custom_call_target="tpu_custom_call" | custom-call | tf_op jit(solution)/shard_map/convolve/pallas_call | solution.py:460
  64.2 3.7 %all-to-all-start.2 = ((bf16[8,256,128]{2,1,0:T(8,128)(2,1)}), bf16[8,256,128]{2,1,0:T(8,128)(2,1)S(1)}, u32[]{:S(2)}, u32[]{:S(2)}) async-start(bf16[8,256,128]{2,1,0:T(8,128)(2,1)} %convolve.1), calls=%async_computation.2 | async-start | bytes 1048576 | tf_op jit(solution)/shard_map/all_to_all | solution.py:606
  67.9 0.7 concatenate.11.refs_4_
  68.6 0.7 concatenate.10.refs_4_
  69.2 5.2 %project.6.refs_1_ = f32[256,512]{1,0:T(8,128)} custom-call(s32[1]{0:T(128)} %bitcast.1.me_ref, bf16[128,4096]{1,0:T(8,128)(2,1)} %get-tuple-element.19.refs_0_, bf16[128,4096]{1,0:T(8,128)(2,1)} %copy-done.1, bf16[3,4096,512]{2,1,0:T(8,128)(2,1)} %bitcast.9, f32[3,3,512]{2,1,0:T(4,128)} %refs_3_.9, bf16[16,4096]{1,0:T(8,128)(2,1)} %concatenate.10.refs_4_), custom_call_target="tpu_custom_call" | custom-call | flops 100000000 | bytes 100000 | tf_op jit(solution)/shard_map/project/pallas_call | solution.py:213
  74.5 5.2 %project.7.refs_3_ = f32[256,512]{1,0:T(8,128)} custom-call(s32[1]{0:T(128)} %bitcast.1.me_ref, bf16[128,4096]{1,0:T(8,128)(2,1)} %copy-done.2, bf16[128,4096]{1,0:T(8,128)(2,1)} %copy-done.3, bf16[3,4096,512]{2,1,0:T(8,128)(2,1)} %bitcast.10, f32[3,3,512]{2,1,0:T(4,128)} %refs_3_.9, bf16[16,4096]{1,0:T(8,128)(2,1)} %concatenate.11.refs_4_), custom_call_target="tpu_custom_call" | custom-call | flops 100000000 | bytes 100000 | tf_op jit(solution)/shard_map/project/pallas_call | solution.py:213
  79.7 2.4 %all-to-all-done.2.c_any = bf16[8,256,128]{2,1,0:T(8,128)(2,1)S(1)} async-done(((bf16[8,256,128]{2,1,0:T(8,128)(2,1)}), bf16[8,256,128]{2,1,0:T(8,128)(2,1)S(1)}, u32[]{:S(2)}, u32[]{:S(2)}) %all-to-all-start.2) | async-done | bytes 524320 | tf_op jit(solution)/shard_map/all_to_all | solution.py:606
  82.1 0.0 copy-start.4
  82.1 0.8 copy-done.4
  82.9 3.0 %finish.1 = bf16[512,512]{1,0:T(8,128)(2,1)} custom-call(s32[1]{0:T(128)} %bitcast.half_ref, bf16[8,256,128]{2,1,0:T(8,128)(2,1)} %copy-done.4, f32[256,512]{1,0:T(8,128)} %get-tuple-element.27.refs_0_, f32[256,512]{1,0:T(8,128)} %project.6.refs_1_, f32[272,512]{1,0:T(8,128)} %get-tuple-element.28.refs_2_, f32[256,512]{1,0:T(8,128)} %project.7.refs_3_, ...), custom_call_target="tpu_custom_call" | custom-call | tf_op jit(solution)/shard_map/finish/pallas_call | solution.py:521
  (5 shorter events, 0.0 us)
Async XLA Ops:
  2.5 3.1 %collective-permute-start = (bf16[128,4096]{1,0:T(8,128)(2,1)}, bf16[128,4096]{1,0:T(8,128)(2,1)S(1)}, u32[]{:S(2)}, u32[]{:S(2)}) collective-permute-start(bf16[128,4096]{1,0:T(8,128)(2,1)} %get-tuple-element.19.refs_0_), channel_id=1, source_target_pairs={{0,1},{1,0},{2,3},{3,2},{4,5},{5,4},{6,7},{7,6},{8,9},{9,8},{10,11... | collective-permute-start | bytes 3145736 | tf_op jit(solution)/shard_map/ppermute | solution.py:558
  3.0 26.8 %collective-permute-start.3 = (bf16[128,4096]{1,0:T(8,128)(2,1)}, bf16[128,4096]{1,0:T(8,128)(2,1)S(1)}, u32[]{:S(2)}, u32[]{:S(2)}) collective-permute-start(bf16[128,4096]{1,0:T(8,128)(2,1)} %get-tuple-element.19.refs_0_), channel_id=1, source_target_pairs={{0,2},{1,3},{2,0},{3,1},{4,6},{5,7},{6,4},{7,5},{8,10},{9,11},{10,... | collective-permute-start | bytes 3145736 | tf_op jit(solution)/shard_map/ppermute | solution.py:558
  5.6 2.0 %copy-start.1 = (bf16[128,4096]{1,0:T(8,128)(2,1)}, bf16[128,4096]{1,0:T(8,128)(2,1)S(1)}, u32[]{:S(2)}) copy-start(bf16[128,4096]{1,0:T(8,128)(2,1)S(1)} %collective-permute-done.refs_1_) | copy-start | bytes 3145732
  5.6 10.0 %collective-permute-start.2 = (bf16[8,4096]{1,0:T(8,128)(2,1)}, bf16[8,4096]{1,0:T(8,128)(2,1)S(1)}, u32[]{:S(2)}, u32[]{:S(2)}) collective-permute-start(bf16[8,4096]{1,0:T(8,128)(2,1)} %get-tuple-element.22), channel_id=1, source_target_pairs={{3,7},{7,11},{11,15},{15,19},{19,23},{23,27},{27,31},{1,1},{5,5},{... | collective-permute-start | bytes 196616 | tf_op jit(solution)/shard_map/ppermute | solution.py:578
  6.2 9.4 %collective-permute-start.1 = (bf16[8,4096]{1,0:T(8,128)(2,1)}, bf16[8,4096]{1,0:T(8,128)(2,1)S(1)}, u32[]{:S(2)}, u32[]{:S(2)}) collective-permute-start(bf16[8,4096]{1,0:T(8,128)(2,1)} %get-tuple-element.22), channel_id=1, source_target_pairs={{3,6},{7,10},{11,14},{15,18},{19,22},{23,26},{27,30},{1,0},{5,4},{... | collective-permute-start | bytes 196616 | tf_op jit(solution)/shard_map/ppermute | solution.py:578
  15.6 28.9 %all-to-all-start = ((bf16[8,384,128]{2,1,0:T(8,128)(2,1)}), bf16[8,384,128]{2,1,0:T(8,128)(2,1)S(1)}, u32[]{:S(2)}, u32[]{:S(2)}) async-start(bf16[8,384,128]{2,1,0:T(8,128)(2,1)} %get-tuple-element.23), calls=%async_computation | async-start | bytes 1572864 | tf_op jit(solution)/shard_map/all_to_all | solution.py:591
  22.8 8.2 %collective-permute-start.5 = (bf16[8,4096]{1,0:T(8,128)(2,1)S(1)}, bf16[8,4096]{1,0:T(8,128)(2,1)S(1)}, u32[]{:S(2)}, u32[]{:S(2)}) collective-permute-start(bf16[8,4096]{1,0:T(8,128)(2,1)S(1)} %add.16), channel_id=1, source_target_pairs={{0,2},{1,3},{2,0},{3,1},{4,6},{5,7},{6,4},{7,5},{8,10},{9,11},{10,... | collective-permute-start | bytes 196616 | tf_op jit(solution)/shard_map/ppermute | solution.py:558
  29.8 2.7 %copy-start.2 = (bf16[128,4096]{1,0:T(8,128)(2,1)}, bf16[128,4096]{1,0:T(8,128)(2,1)S(1)}, u32[]{:S(2)}) copy-start(bf16[128,4096]{1,0:T(8,128)(2,1)S(1)} %collective-permute-done.3.refs_0_) | copy-start | bytes 3145732
  29.8 2.7 %collective-permute-start.4 = (bf16[128,4096]{1,0:T(8,128)(2,1)S(1)}, bf16[128,4096]{1,0:T(8,128)(2,1)S(1)}, u32[]{:S(2)}, u32[]{:S(2)}) collective-permute-start(bf16[128,4096]{1,0:T(8,128)(2,1)S(1)} %collective-permute-done.3.refs_0_), channel_id=1, source_target_pairs={{0,1},{1,0},{2,3},{3,2},{4,5},{5,4},{6,7},{7,6},{8,9},{9,8},{10,11... | collective-permute-start | bytes 3145736 | tf_op jit(solution)/shard_map/ppermute | solution.py:558
  31.9 0.7 copy-start.6
  32.7 1.0 %copy-start.3 = (bf16[128,4096]{1,0:T(8,128)(2,1)}, bf16[128,4096]{1,0:T(8,128)(2,1)S(1)}, u32[]{:S(2)}) copy-start(bf16[128,4096]{1,0:T(8,128)(2,1)S(1)} %collective-permute-done.4.refs_1_) | copy-start | bytes 3145732
  44.5 3.5 %copy-start = (bf16[8,384,128]{2,1,0:T(8,128)(2,1)}, bf16[8,384,128]{2,1,0:T(8,128)(2,1)S(1)}, u32[]{:S(2)}) copy-start(bf16[8,384,128]{2,1,0:T(8,128)(2,1)S(1)} %all-to-all-done.x_any.early_any) | copy-start | bytes 2359300
  44.5 13.0 %all-to-all-start.1 = ((bf16[8,136,128]{2,1,0:T(8,128)(2,1)}), bf16[8,136,128]{2,1,0:T(8,128)(2,1)S(1)}, u32[]{:S(2)}, u32[]{:S(2)}) async-start(bf16[8,136,128]{2,1,0:T(8,128)(2,1)} %get-tuple-element.26), calls=%async_computation.1 | async-start | bytes 557056 | tf_op jit(solution)/shard_map/all_to_all | solution.py:601
  57.5 0.7 copy-start.5
  64.2 17.8 %all-to-all-start.2 = ((bf16[8,256,128]{2,1,0:T(8,128)(2,1)}), bf16[8,256,128]{2,1,0:T(8,128)(2,1)S(1)}, u32[]{:S(2)}, u32[]{:S(2)}) async-start(bf16[8,256,128]{2,1,0:T(8,128)(2,1)} %convolve.1), calls=%async_computation.2 | async-start | bytes 1048576 | tf_op jit(solution)/shard_map/all_to_all | solution.py:606
  82.1 0.8 copy-start.4

commit v5 on v4

--- a/solution.py
+++ b/solution.py
@@ -17,6 +17,7 @@
 TAIL = 8
 PAD = 16
 BIG = 60 * 1024 * 1024
+FINISH_LIMIT = 50
 COST = (10**8, 10**8, 10**8)
 
 VMEM_SPEC = pl.BlockSpec(memory_space=pltpu.VMEM)
@@ -126,8 +127,8 @@
     each = blocks[0].shape[0]
     length = each * count
     end = PAD + length
-    width = x_ref.shape[1]
-    depth = width // splits
+    width, channels = x_ref.shape[1], rows_ref.shape[1]
+    each_cols = channels // splits
 
     sources = [(tap_hbm, tap_ref, tap_sem)]
     for mask, block in enumerate(blocks):
@@ -144,8 +145,8 @@
     loads = {}
     for at, s in enumerate(parts):
         for i in range(splits):
-            chunk = pl.ds(i * depth, depth)
-            loads[s, i] = start_all([(w_hbm.at[s, chunk], w_ref.at[at, chunk], w_sem.at[at, i])])[0]
+            cols = pl.ds(i * each_cols, each_cols)
+            loads[s, i] = start_all([(w_hbm.at[s, :, cols], w_ref.at[at, i], w_sem.at[at, i])])[0]
     if with_filter:
         filt_load = start_all([(extra[-1], filt_ref, sem.at[count + 2])])[0]
     for wait in waits:
@@ -153,13 +154,10 @@
 
     def mixed(s):
         at = parts.index(s)
-        total = None
         for i in range(splits):
             loads[s, i].wait()
-            chunk = slice(i * depth, (i + 1) * depth)
-            term = jnp.dot(x_ref[:, chunk], w_ref[at, chunk], preferred_element_type=f32)
-            total = term if total is None else total + term
-        rows_ref[...] = total
+            cols = slice(i * each_cols, (i + 1) * each_cols)
+            rows_ref[:, cols] = jnp.dot(x_ref[...], w_ref[at, i], preferred_element_type=f32)
         spans = [(PAD, length)]
         if ext_rows > PAD:
             spans.append((end + PAD, PAD))
@@ -196,7 +194,7 @@
 def project(parts, me, blocks, weight, taps, cost, ext=None, filt=None):
     _, width, channels = weight.shape
     length = blocks[0].shape[0] * len(blocks)
-    splits = 2
+    splits = 1
     ext_rows = 0 if ext is None else ext.shape[0]
     more = PAD if ext_rows > PAD else 0
     shapes = []
@@ -217,7 +215,7 @@
         out_shape=shapes,
         scratch_shapes=[pltpu.VMEM(x.shape, x.dtype) for x in shapes]
         + [
-            pltpu.VMEM((len(parts), width, channels), bf16),
+            pltpu.VMEM((len(parts), splits, width, channels // splits), bf16),
             pltpu.VMEM(taps.shape, f32),
             pltpu.VMEM((rows, width), bf16),
             pltpu.VMEM((rows, channels), f32),
@@ -233,7 +231,7 @@
     )(me, *blocks, weight, taps, *extra)
 
 
-def coarse_forward(dev_count, x_ref, lane_ref, e_ref, step=32):
+def coarse_forward(dev_count, x_ref, lane_ref, e_ref, step=64):
     count = dev_count
     half = count // 2
     low = lane_mask()
@@ -273,7 +271,7 @@
     lax.fori_loop(0, FINE // step, body, 0)
 
 
-def coarse_inverse(dev_count, g_ref, y_ref, first, length, step=32):
+def coarse_inverse(dev_count, g_ref, y_ref, first, length, step=64):
     count = dev_count
     half = count // 2
 
@@ -480,62 +478,88 @@
     )(half, early, late, spectrum, *consts)
 
 
-def finish(half, conv, early, late, skip_gain):
-    rows, channels = early[0].shape
+def query_kernel(count, me_ref, *refs):
+    blocks, refs = refs[:count], refs[count:]
+    halo_any, w_hbm, tap_hbm, early_any, late_any, skip_hbm, out_any = refs[:7]
+    x_ref, w_ref, tap_ref, early_ref, late_ref, skip_ref, rows_ref, out_ref, sem, out_sem = refs[7:]
+    each = blocks[0].shape[0]
+    length = each * count
+    half = length // 2
+    early_at = me_ref[1]
+
+    ahead = pl.ds(pl.multiple_of((1 - early_at) * PAD, PAD), PAD)
+    pairs = [(halo_any.at[ahead], x_ref.at[pl.ds(0, PAD)])]
+    for mask, block in enumerate(blocks):
+        first = pl.multiple_of(PAD + (me_ref[0] ^ mask) * each, 16)
+        pairs.append((block, x_ref.at[pl.ds(first, each)]))
+    pairs += [(w_hbm.at[0], w_ref), (tap_hbm, tap_ref), (skip_hbm, skip_ref)]
+    pairs += [(early_any, early_ref), (late_any, late_ref)]
+    for copy in start_all((*pair, sem.at[i]) for i, pair in enumerate(pairs)):
+        copy.wait()
+    rows_ref[...] = jnp.dot(x_ref[...], w_ref[...], preferred_element_type=f32)
+    total = tap_ref[0, 0:1] * rows_ref[PAD:]
+    for lag in (1, 2):
+        total += tap_ref[lag, 0:1] * rows_ref[PAD - lag : PAD - lag + length]
+    out_ref[0] = total
+    early_ref[:PAD] = late_ref[half:]
+    for at, g_ref in ((early_at, early_ref), (1 - early_at, late_ref)):
+        rows = pl.ds(pl.multiple_of(at * half, half), half)
+        out_ref[1, rows, :] = out_ref[0, rows, :] * (skip_ref[...] * g_ref[:half])
+    start_all([(out_ref, out_any, out_sem)])[0].wait()
+
+
+def query_terms(me, blocks, halo, weight, taps, early, late, skip):
+    _, width, channels = weight.shape
+    length = blocks[0].shape[0] * len(blocks)
+    skip = skip.reshape(1, channels)
+    return pl.pallas_call(
+        functools.partial(query_kernel, len(blocks)),
+        in_specs=[pl.BlockSpec(memory_space=pltpu.SMEM)] + [ANY_SPEC] * (len(blocks) + 6),
+        out_specs=ANY_SPEC,
+        out_shape=jax.ShapeDtypeStruct((2, length, channels), f32),
+        scratch_shapes=[
+            pltpu.VMEM((PAD + length, width), bf16),
+            pltpu.VMEM((width, channels), bf16),
+            pltpu.VMEM(taps.shape, f32),
+            pltpu.VMEM(early.shape, f32),
+            pltpu.VMEM(late.shape, f32),
+            pltpu.VMEM(skip.shape, f32),
+            pltpu.VMEM((PAD + length, channels), f32),
+            pltpu.VMEM((2, length, channels), f32),
+            pltpu.SemaphoreType.DMA((len(blocks) + 6,)),
+            pltpu.SemaphoreType.DMA,
+        ],
+        compiler_params=pltpu.CompilerParams(vmem_limit_bytes=BIG),
+        cost_estimate=pl.CostEstimate(flops=COST[2], bytes_accessed=10**5, transcendentals=0),
+        name="query_terms",
+    )(me, *blocks, halo, weight, taps, early, late, skip)
+
+
+def finish(conv, terms):
+    _, length, channels = terms.shape
     tiles = channels // LANES
 
-    def kernel(half_ref, c_any, *refs):
-        src_hbm, skip_hbm, out_any = refs[:4], refs[4], refs[5]
-        c_ref, row_ref, skip_ref, out_ref, sem, c_sem, s_sem, out_sem = refs[6:]
-        early_at = half_ref[0]
-        cols = [pl.ds(i * LANES, LANES) for i in range(tiles)]
-        skip_copy = start_all([(skip_hbm, skip_ref, s_sem)])[0]
-        copies = []
-        for i in range(tiles):
-            pair = pl.ds(2 * i, 2)
-            copies.append(
-                start_all(
-                    [(c_any.at[pair], c_ref.at[pair], c_sem.at[i])]
-                    + [
-                        (src.at[:, cols[i]], row_ref.at[i, j, pl.ds(0, src.shape[0])], sem.at[i, j])
-                        for j, src in enumerate(src_hbm)
-                    ]
-                )
-            )
-        skip_copy.wait()
+    def kernel(c_ref, term_ref, out_any, out_ref, sem):
         sends = []
         for i in range(tiles):
-            for copy in copies[i]:
-                copy.wait()
+            cols = slice(i * LANES, (i + 1) * LANES)
             top, bot = unpack_pair(c_ref[2 * i].astype(f32), c_ref[2 * i + 1].astype(f32))
-            skip = skip_ref[:, cols[i]]
-            row_ref[i, 0, :PAD] = row_ref[i, 2, rows:]
-            for at, j in ((early_at, 0), (1 - early_at, 2)):
-                conv = jnp.where(at == 0, top, bot)
-                value = row_ref[i, j + 1, :rows] * (conv + skip * row_ref[i, j, :rows])
-                out_ref[i, pl.ds(pl.multiple_of(at * FINE, FINE), FINE), :] = value.astype(bf16)
-            sends += start_all([(out_ref.at[i], out_any.at[:, cols[i]], out_sem.at[i])])
+            for j, part in enumerate((top, bot)):
+                rows = slice(j * FINE, (j + 1) * FINE)
+                out_ref[i, rows] = (term_ref[0, rows, cols] * part + term_ref[1, rows, cols]).astype(bf16)
+            sends += start_all([(out_ref.at[i], out_any.at[:, pl.ds(i * LANES, LANES)], sem.at[i])])
         for send in sends:
             send.wait()
 
     return pl.pallas_call(
         kernel,
-        in_specs=[pl.BlockSpec(memory_space=pltpu.SMEM), ANY_SPEC] + [HBM_SPEC] * 5,
+        in_specs=[VMEM_SPEC] * 2,
         out_specs=ANY_SPEC,
-        out_shape=jax.ShapeDtypeStruct((2 * rows, channels), bf16),
-        scratch_shapes=[
-            pltpu.VMEM(conv.shape, bf16),
-            pltpu.VMEM((tiles, 4, rows + PAD, LANES), f32),
-            pltpu.VMEM((1, channels), f32),
-            pltpu.VMEM((tiles, 2 * rows, LANES), bf16),
-            pltpu.SemaphoreType.DMA((tiles, 4)),
-            pltpu.SemaphoreType.DMA((tiles,)),
-            pltpu.SemaphoreType.DMA,
-            pltpu.SemaphoreType.DMA((tiles,)),
-        ],
-        compiler_params=pltpu.CompilerParams(vmem_limit_bytes=BIG),
+        out_shape=jax.ShapeDtypeStruct((length, channels), bf16),
+        scratch_shapes=[pltpu.VMEM((tiles, length, LANES), bf16), pltpu.SemaphoreType.DMA((tiles,))],
+        compiler_params=pltpu.CompilerParams(vmem_limit_bytes=FINISH_LIMIT * 1024 * 1024),
         name="finish",
-    )(half, conv, *early, *late, skip_gain.reshape(1, channels))
+    )(conv, terms)
 
 
 def local(tokens, norm_gain, in_weight, short_weight, long_filter, skip_gain):
@@ -600,23 +624,23 @@
         packs = jnp.concatenate(packs, axis=1)
     late_sent = exchange(packs)
     spectrum = filter_spectrum(early_sent, consts)
-    early_ext = jnp.concatenate([gap, early_halo], axis=0)
-    (early_query,) = project((0,), place, early_blocks, weight, short_weight, COST[2], ext=early_ext)
-    (late_query,) = project((0,), place, late_blocks, weight, short_weight, COST[2], ext=late_ext[:PAD])
     conv = exchange(convolve(half, early_sent, late_sent, spectrum, consts))
-    early, late = (early_gated, early_query), (late_gated, late_query)
+    terms = query_terms(
+        jnp.concatenate([me.reshape(1), half]),
+        early_blocks + late_blocks,
+        late_ext,
+        weight,
+        short_weight,
+        early_gated,
+        late_gated,
+        skip_gain,
+    )
     if packed:
-        return finish(half, conv, early, late, skip_gain)
-    early_gated = jnp.concatenate([late_gated[rows:], early_gated[PAD:]], axis=0)
-    early, late = (early_gated, early_query), (late_gated[:rows], late_query)
+        return finish(conv, terms)
     each = channels // dev_count
     conv = conv.reshape(dev_count, FINE, 2, HALF)[..., :each]
     conv = jnp.transpose(conv, (2, 1, 0, 3)).reshape(2 * FINE, channels).astype(f32)
-    first, second = (
-        [jnp.where(half == swapped, a, b) for a, b in zip(early, late)] for swapped in (0, 1)
-    )
-    gated, query = (jnp.concatenate([a, b], axis=0) for a, b in zip(first, second))
-    return (query * (conv + skip_gain * gated)).astype(bf16)
+    return (terms[0] * conv + terms[1]).astype(bf16)
 
 
 def solution(mesh):

time: 86.5 us -> 85.4 us (0.987)
  Pallas kernels: 43 us -> 37.9 us
  waiting for transfers between devices: 16.7 us -> 20.8 us
    pallas_call x4 -> x2, Pallas kernels: 26.6 us -> 15.2 us  [project(): pl.pallas_call(functools.partial(project_kernel, len(blocks), parts, spli...]
    pallas_call x1 -> x2, Pallas kernels: 2.96 us -> 9.64 us  [the longest x1 8.61 us: query_terms(): pl.pallas_call(functools.partial(query_kernel, len(blocks)), in_specs=[pl...]
    all_to_all x1, waiting for transfers between devices: 2.36 us -> 5.24 us  [local(): conv = exchange(convolve(half, early_sent, late_sent, spectrum, consts))]
    concatenate x2 -> x0, local copies, waits for them, and re-layouts: 1.32 us -> none  [the longest x1 0.66 us: local(): early_ext = jnp.concatenate([gap, early_halo], axis=0)]
    all_to_all x1, waiting for transfers between devices: 2.67 us -> 3.83 us  [local(): early_sent = exchange(packs)]
  transfers between devices with their start and end apart: 9 -> 9, of which waited for: 6 -> 6; matrix products, arithmetic and copies ran while one was open for 3% -> 2% of each run, Pallas kernels for 37% -> 34%
where the time goes in v5:
time: 85.4 us; the launch traced here: 84.9 us
  Pallas kernels  37.9 us (44%)
  waiting for transfers between devices  20.8 us (24%)
  starting transfers between devices  20.7 us (24%)
  local copies, waits for them, and re-layouts  3.64 us (4%)
  other arithmetic  1.69 us (2%)
    pallas_call x2, Pallas kernels, project(): pl.pallas_call(functools.partial(project_kernel, len(blocks), parts, spli...  15.2 us
    pallas_call x1, Pallas kernels, query_terms(): pl.pallas_call(functools.partial(query_kernel, len(blocks)), in_specs=[pl...  8.61 us
    all_to_all x1, starting transfers between devices, local(): early_sent = exchange(packs)  7.14 us
    ppermute x4, waiting for transfers between devices, swap(): lax.ppermute(x, 'tensor', [(i, i ^ bit) for i in range(tensor_count)])  7 us
    pallas_call x1, Pallas kernels, convolve(): pl.pallas_call(functools.partial(conv_kernel, dev_count), in_specs=[pl.Bl...  5.81 us
    all_to_all x1, waiting for transfers between devices, local(): conv = exchange(convolve(half, early_sent, late_sent, spectrum, consts))  5.24 us
    pallas_call x1, Pallas kernels, filter_spectrum(): pl.pallas_call(functools.partial(filter_kernel, dev_count), in_specs=[ANY...  4.81 us
    all_to_all x1, waiting for transfers between devices, local(): late_sent = exchange(packs)  4.73 us
  transfers between devices with their start and end apart: 9, of which 6 were waited for; matrix products, arithmetic and copies ran while one was open for 2% of the time, Pallas kernels for 34%

profile of v5, /device:TPU:0, one launch (start us, length us, event | category | flops | bytes accessed | tf_op | source)
XLA Modules:
  0.0 84.9 jit_solution(12231438979247757664)
XLA Ops:
  0.0 2.5 %norm_rows.1 = (bf16[128,4096]{1,0:T(8,128)(2,1)}, bf16[8,4096]{1,0:T(8,128)(2,1)}) custom-call(bf16[128,4096]{1,0:T(8,128)(2,1)} %tok_hbm.1, f32[1,4096]{1,0:T(1,128)} %bitcast.11), custom_call_target="tpu_custom_call" | custom-call | tf_op jit(solution)/shard_map/norm_rows/pallas_call | solution.py:91
  2.5 0.5 collective-permute-start
  3.0 2.6 %collective-permute-start.3 = (bf16[128,4096]{1,0:T(8,128)(2,1)}, bf16[128,4096]{1,0:T(8,128)(2,1)S(1)}, u32[]{:S(2)}, u32[]{:S(2)}) collective-permute-start(bf16[128,4096]{1,0:T(8,128)(2,1)} %get-tuple-element.19.refs_0_), channel_id=1, source_target_pairs={{0,2},{1,3},{2,0},{3,1},{4,6},{5,7},{6,4},{7,5},{8,10},{9,11},{10,... | collective-permute-start | bytes 3145736 | tf_op jit(solution)/shard_map/ppermute | solution.py:582
  5.5 0.0 collective-permute-done.refs_1_
  5.5 0.0 copy-start.2
  5.5 0.7 collective-permute-start.2
  6.2 1.3 %collective-permute-start.1 = (bf16[8,4096]{1,0:T(8,128)(2,1)}, bf16[8,4096]{1,0:T(8,128)(2,1)S(1)}, u32[]{:S(2)}, u32[]{:S(2)}) collective-permute-start(bf16[8,4096]{1,0:T(8,128)(2,1)} %get-tuple-element.22), channel_id=1, source_target_pairs={{3,6},{7,10},{11,14},{15,18},{19,22},{23,26},{27,30},{1,0},{5,4},{... | collective-permute-start | bytes 196616 | tf_op jit(solution)/shard_map/ppermute | solution.py:602
  7.5 0.0 copy-done.2
  7.5 8.1 %project.2 = (f32[256,512]{1,0:T(8,128)}, bf16[8,384,128]{2,1,0:T(8,128)(2,1)}) custom-call(s32[1]{0:T(128)} %bitcast.1.me_ref, bf16[128,4096]{1,0:T(8,128)(2,1)} %get-tuple-element.19.refs_0_, bf16[128,4096]{1,0:T(8,128)(2,1)} %copy-done.2, bf16[3,4096,512]{2,1,0:T(8,128)(2,1)} %bitcast.8, f32[3,3,512]{2,1,0:T(4,128)} %refs_6_.1, f32[512,512]{1,0:T(8,128)} %refs_4_.1), custom_call_target="tpu_custom_call" | custom-call | flops 100000000 | bytes 100000 | tf_op jit(solution)/shard_map/project/pallas_call | solution.py:211
  15.7 0.0 collective-permute-done.2
  15.7 0.0 collective-permute-done.1
  15.7 7.1 %all-to-all-start = ((bf16[8,384,128]{2,1,0:T(8,128)(2,1)}), bf16[8,384,128]{2,1,0:T(8,128)(2,1)S(1)}, u32[]{:S(2)}, u32[]{:S(2)}) async-start(bf16[8,384,128]{2,1,0:T(8,128)(2,1)} %get-tuple-element.23), calls=%async_computation | async-start | bytes 1572864 | tf_op jit(solution)/shard_map/all_to_all | solution.py:615
  22.9 1.5 %collective-permute-start.5 = (bf16[8,4096]{1,0:T(8,128)(2,1)S(1)}, bf16[8,4096]{1,0:T(8,128)(2,1)S(1)}, u32[]{:S(2)}, u32[]{:S(2)}) collective-permute-start(bf16[8,4096]{1,0:T(8,128)(2,1)S(1)} %add.12), channel_id=1, source_target_pairs={{0,2},{1,3},{2,0},{3,1},{4,6},{5,7},{6,4},{7,5},{8,10},{9,11},{10,... | collective-permute-start | bytes 196616 | tf_op jit(solution)/shard_map/ppermute | solution.py:582
  24.4 5.4 %collective-permute-done.3.refs_0_.refs_2_ = bf16[128,4096]{1,0:T(8,128)(2,1)S(1)} collective-permute-done((bf16[128,4096]{1,0:T(8,128)(2,1)}, bf16[128,4096]{1,0:T(8,128)(2,1)S(1)}, u32[]{:S(2)}, u32[]{:S(2)}) %collective-permute-start.3) | collective-permute-done | bytes 1048608 | tf_op jit(solution)/shard_map/ppermute | solution.py:582
  29.8 0.0 copy-start.3
  29.8 0.0 collective-permute-start.4
  29.8 1.1 %collective-permute-done.5 = bf16[8,4096]{1,0:T(8,128)(2,1)S(1)} collective-permute-done((bf16[8,4096]{1,0:T(8,128)(2,1)S(1)}, bf16[8,4096]{1,0:T(8,128)(2,1)S(1)}, u32[]{:S(2)}, u32[]{:S(2)}) %collective-permute-start.5) | collective-permute-done | bytes 65568 | tf_op jit(solution)/shard_map/ppermute | solution.py:582
  30.9 1.0 %add_dynamic-update-slice_fusion.refs_4_ = bf16[48,4096]{1,0:T(8,128)(2,1)S(1)} fusion(bf16[48,4096]{1,0:T(8,128)(2,1)S(1)} %constant_dynamic-update-slice_fusion, bf16[128,4096]{1,0:T(8,128)(2,1)} %copy-done.2, bf16[128,4096]{1,0:T(8,128)(2,1)} %get-tuple-element.19.refs_0_, pred[]{:T(512)} %bitcast.5, pred[]{:T(512)} %bitcast.4), kind=kLoop, calls=%fused_computation | loop fusion | flops 393216 | bytes 393218 | tf_op jit(solution)/shard_map/concatenate | solution.py:619
  31.9 0.0 copy-start.5
  31.9 0.5 collective-permute-done.4.refs_1_.refs_3_
  32.4 0.0 copy-done.3
  32.4 0.3 copy-done.5
  32.7 0.0 copy-start.4
  32.7 1.0 %copy-done.4 = bf16[128,4096]{1,0:T(8,128)(2,1)} copy-done((bf16[128,4096]{1,0:T(8,128)(2,1)}, bf16[128,4096]{1,0:T(8,128)(2,1)S(1)}, u32[]{:S(2)}) %copy-start.4) | copy-done | bytes 1048600
  33.7 7.1 %project.3 = (f32[272,512]{1,0:T(8,128)}, bf16[8,136,128]{2,1,0:T(8,128)(2,1)}) custom-call(s32[1]{0:T(128)} %bitcast.1.me_ref, bf16[128,4096]{1,0:T(8,128)(2,1)} %copy-done.3, bf16[128,4096]{1,0:T(8,128)(2,1)} %copy-done.4, bf16[3,4096,512]{2,1,0:T(8,128)(2,1)} %bitcast.9, f32[3,3,512]{2,1,0:T(4,128)} %refs_6_.1, bf16[48,4096]{1,0:T(8,128)(2,1)} %copy-done.5), custom_call_target="tpu_custom_call" | custom-call | flops 100000000 | bytes 100000 | tf_op jit(solution)/shard_map/project/pallas_call | solution.py:211
  40.8 3.8 %all-to-all-done.x_any.early_any = bf16[8,384,128]{2,1,0:T(8,128)(2,1)S(1)} async-done(((bf16[8,384,128]{2,1,0:T(8,128)(2,1)}), bf16[8,384,128]{2,1,0:T(8,128)(2,1)S(1)}, u32[]{:S(2)}, u32[]{:S(2)}) %all-to-all-start) | async-done | bytes 786464 | tf_op jit(solution)/shard_map/all_to_all | solution.py:615
  44.6 0.0 copy-start.1
  44.6 3.4 %all-to-all-start.1 = ((bf16[8,136,128]{2,1,0:T(8,128)(2,1)}), bf16[8,136,128]{2,1,0:T(8,128)(2,1)S(1)}, u32[]{:S(2)}, u32[]{:S(2)}) async-start(bf16[8,136,128]{2,1,0:T(8,128)(2,1)} %get-tuple-element.26), calls=%async_computation.1 | async-start | bytes 557056 | tf_op jit(solution)/shard_map/all_to_all | solution.py:625
  48.1 0.0 copy-done.1
  48.1 4.8 %filter_spectrum.1.h_hbm = f32[9,256,256]{2,1,0:T(8,128)} custom-call(bf16[8,384,128]{2,1,0:T(8,128)(2,1)} %copy-done.1, f32[256,256]{1,0:T(8,128)} %constant.44.clone.refs_0_, f32[256,256]{1,0:T(8,128)} %constant.45.clone.refs_1_, f32[9,2,128]{2,1,0:T(2,128)} %constant.46.clone.refs_2_, bf16[512,256]{1,0:T(8,128)(2,1)} %constant.47.clone.refs_3_), custom_call_target="tpu_custom_call" | custom-call | tf_op jit(solution)/shard_map/filter_spectrum/pallas_call | solution.py:443
  52.9 4.7 %all-to-all-done.1.late_any = bf16[8,136,128]{2,1,0:T(8,128)(2,1)S(1)} async-done(((bf16[8,136,128]{2,1,0:T(8,128)(2,1)}), bf16[8,136,128]{2,1,0:T(8,128)(2,1)S(1)}, u32[]{:S(2)}, u32[]{:S(2)}) %all-to-all-start.1) | async-done | bytes 278560 | tf_op jit(solution)/shard_map/all_to_all | solution.py:625
  57.6 0.0 copy-start.6
  57.6 0.7 copy-done.6
  58.3 5.8 %convolve.1 = bf16[8,256,128]{2,1,0:T(8,128)(2,1)} custom-call(s32[1]{0:T(128)} %bitcast.half_ref, bf16[8,384,128]{2,1,0:T(8,128)(2,1)} %copy-done.1, bf16[8,136,128]{2,1,0:T(8,128)(2,1)} %copy-done.6, f32[9,256,256]{2,1,0:T(8,128)} %filter_spectrum.1.h_hbm, f32[256,256]{1,0:T(8,128)} %constant.44.clone.refs_0_, f32[256,256]{1,0:T(8,128)} %constant.45.clone.refs_1_, ...), custom_call_target="tpu_custom_call" | custom-call | tf_op jit(solution)/shard_map/convolve/pallas_call | solution.py:458
  64.2 3.6 %all-to-all-start.2 = ((bf16[8,256,128]{2,1,0:T(8,128)(2,1)}), bf16[8,256,128]{2,1,0:T(8,128)(2,1)S(1)}, u32[]{:S(2)}, u32[]{:S(2)}) async-start(bf16[8,256,128]{2,1,0:T(8,128)(2,1)} %convolve.1), calls=%async_computation.2 | async-start | bytes 1048576 | tf_op jit(solution)/shard_map/all_to_all | solution.py:627
  67.8 0.6 pad_add_fusion.me_ref
  68.4 8.6 %query_terms.1.term_ref = f32[2,512,512]{2,1,0:T(8,128)} custom-call(s32[2]{0:T(128)} %pad_add_fusion.me_ref, bf16[128,4096]{1,0:T(8,128)(2,1)} %get-tuple-element.19.refs_0_, bf16[128,4096]{1,0:T(8,128)(2,1)} %copy-done.2, bf16[128,4096]{1,0:T(8,128)(2,1)} %copy-done.3, bf16[128,4096]{1,0:T(8,128)(2,1)} %copy-done.4, bf16[48,4096]{1,0:T(8,128)(2,1)} %copy-done.5, ...), custom_call_target="tpu_custom_call" | custom-call | flops 100000000 | bytes 100000 | tf_op jit(solution)/shard_map/query_terms/pallas_call | solution.py:515
  77.1 5.2 %all-to-all-done.2.c_ref = bf16[8,256,128]{2,1,0:T(8,128)(2,1)S(1)} async-done(((bf16[8,256,128]{2,1,0:T(8,128)(2,1)}), bf16[8,256,128]{2,1,0:T(8,128)(2,1)S(1)}, u32[]{:S(2)}, u32[]{:S(2)}) %all-to-all-start.2) | async-done | bytes 524320 | tf_op jit(solution)/shard_map/all_to_all | solution.py:627
  82.3 0.0 copy-start
  82.3 1.6 %copy-done = f32[2,512,512]{2,1,0:T(8,128)S(1)} copy-done((f32[2,512,512]{2,1,0:T(8,128)S(1)}, f32[2,512,512]{2,1,0:T(8,128)}, u32[]{:S(2)}) %copy-start) | copy-done | bytes 2097176
  83.9 1.0 %finish.1 = bf16[512,512]{1,0:T(8,128)(2,1)} custom-call(bf16[8,256,128]{2,1,0:T(8,128)(2,1)S(1)} %all-to-all-done.2.c_ref, f32[2,512,512]{2,1,0:T(8,128)S(1)} %copy-done), custom_call_target="tpu_custom_call" | custom-call | tf_op jit(solution)/shard_map/finish/pallas_call | solution.py:554
  (5 shorter events, 0.0 us)
Async XLA Ops:
  2.5 3.1 %collective-permute-start = (bf16[128,4096]{1,0:T(8,128)(2,1)}, bf16[128,4096]{1,0:T(8,128)(2,1)S(1)}, u32[]{:S(2)}, u32[]{:S(2)}) collective-permute-start(bf16[128,4096]{1,0:T(8,128)(2,1)} %get-tuple-element.19.refs_0_), channel_id=1, source_target_pairs={{0,1},{1,0},{2,3},{3,2},{4,5},{5,4},{6,7},{7,6},{8,9},{9,8},{10,11... | collective-permute-start | bytes 3145736 | tf_op jit(solution)/shard_map/ppermute | solution.py:582
  3.0 26.8 %collective-permute-start.3 = (bf16[128,4096]{1,0:T(8,128)(2,1)}, bf16[128,4096]{1,0:T(8,128)(2,1)S(1)}, u32[]{:S(2)}, u32[]{:S(2)}) collective-permute-start(bf16[128,4096]{1,0:T(8,128)(2,1)} %get-tuple-element.19.refs_0_), channel_id=1, source_target_pairs={{0,2},{1,3},{2,0},{3,1},{4,6},{5,7},{6,4},{7,5},{8,10},{9,11},{10,... | collective-permute-start | bytes 3145736 | tf_op jit(solution)/shard_map/ppermute | solution.py:582
  5.5 2.0 %copy-start.2 = (bf16[128,4096]{1,0:T(8,128)(2,1)}, bf16[128,4096]{1,0:T(8,128)(2,1)S(1)}, u32[]{:S(2)}) copy-start(bf16[128,4096]{1,0:T(8,128)(2,1)S(1)} %collective-permute-done.refs_1_) | copy-start | bytes 3145732
  5.5 10.1 %collective-permute-start.2 = (bf16[8,4096]{1,0:T(8,128)(2,1)}, bf16[8,4096]{1,0:T(8,128)(2,1)S(1)}, u32[]{:S(2)}, u32[]{:S(2)}) collective-permute-start(bf16[8,4096]{1,0:T(8,128)(2,1)} %get-tuple-element.22), channel_id=1, source_target_pairs={{3,7},{7,11},{11,15},{15,19},{19,23},{23,27},{27,31},{1,1},{5,5},{... | collective-permute-start | bytes 196616 | tf_op jit(solution)/shard_map/ppermute | solution.py:602
  6.2 9.5 %collective-permute-start.1 = (bf16[8,4096]{1,0:T(8,128)(2,1)}, bf16[8,4096]{1,0:T(8,128)(2,1)S(1)}, u32[]{:S(2)}, u32[]{:S(2)}) collective-permute-start(bf16[8,4096]{1,0:T(8,128)(2,1)} %get-tuple-element.22), channel_id=1, source_target_pairs={{3,6},{7,10},{11,14},{15,18},{19,22},{23,26},{27,30},{1,0},{5,4},{... | collective-permute-start | bytes 196616 | tf_op jit(solution)/shard_map/ppermute | solution.py:602
  15.7 28.9 %all-to-all-start = ((bf16[8,384,128]{2,1,0:T(8,128)(2,1)}), bf16[8,384,128]{2,1,0:T(8,128)(2,1)S(1)}, u32[]{:S(2)}, u32[]{:S(2)}) async-start(bf16[8,384,128]{2,1,0:T(8,128)(2,1)} %get-tuple-element.23), calls=%async_computation | async-start | bytes 1572864 | tf_op jit(solution)/shard_map/all_to_all | solution.py:615
  22.9 8.0 %collective-permute-start.5 = (bf16[8,4096]{1,0:T(8,128)(2,1)S(1)}, bf16[8,4096]{1,0:T(8,128)(2,1)S(1)}, u32[]{:S(2)}, u32[]{:S(2)}) collective-permute-start(bf16[8,4096]{1,0:T(8,128)(2,1)S(1)} %add.12), channel_id=1, source_target_pairs={{0,2},{1,3},{2,0},{3,1},{4,6},{5,7},{6,4},{7,5},{8,10},{9,11},{10,... | collective-permute-start | bytes 196616 | tf_op jit(solution)/shard_map/ppermute | solution.py:582
  29.8 2.7 %copy-start.3 = (bf16[128,4096]{1,0:T(8,128)(2,1)}, bf16[128,4096]{1,0:T(8,128)(2,1)S(1)}, u32[]{:S(2)}) copy-start(bf16[128,4096]{1,0:T(8,128)(2,1)S(1)} %collective-permute-done.3.refs_0_.refs_2_) | copy-start | bytes 3145732
  29.8 2.7 %collective-permute-start.4 = (bf16[128,4096]{1,0:T(8,128)(2,1)S(1)}, bf16[128,4096]{1,0:T(8,128)(2,1)S(1)}, u32[]{:S(2)}, u32[]{:S(2)}) collective-permute-start(bf16[128,4096]{1,0:T(8,128)(2,1)S(1)} %collective-permute-done.3.refs_0_.refs_2_), channel_id=1, source_target_pairs={{0,1},{1,0},{2,3},{3,2},{4,5},{5,4},{6,7},{7,6},{8,9},{9,8},{10,11... | collective-permute-start | bytes 3145736 | tf_op jit(solution)/shard_map/ppermute | solution.py:582
  31.9 0.8 copy-start.5
  32.7 1.0 %copy-start.4 = (bf16[128,4096]{1,0:T(8,128)(2,1)}, bf16[128,4096]{1,0:T(8,128)(2,1)S(1)}, u32[]{:S(2)}) copy-start(bf16[128,4096]{1,0:T(8,128)(2,1)S(1)} %collective-permute-done.4.refs_1_.refs_3_) | copy-start | bytes 3145732
  44.6 3.4 %copy-start.1 = (bf16[8,384,128]{2,1,0:T(8,128)(2,1)}, bf16[8,384,128]{2,1,0:T(8,128)(2,1)S(1)}, u32[]{:S(2)}) copy-start(bf16[8,384,128]{2,1,0:T(8,128)(2,1)S(1)} %all-to-all-done.x_any.early_any) | copy-start | bytes 2359300
  44.6 13.0 %all-to-all-start.1 = ((bf16[8,136,128]{2,1,0:T(8,128)(2,1)}), bf16[8,136,128]{2,1,0:T(8,128)(2,1)S(1)}, u32[]{:S(2)}, u32[]{:S(2)}) async-start(bf16[8,136,128]{2,1,0:T(8,128)(2,1)} %get-tuple-element.26), calls=%async_computation.1 | async-start | bytes 557056 | tf_op jit(solution)/shard_map/all_to_all | solution.py:625
  57.6 0.7 copy-start.6
  64.2 18.1 %all-to-all-start.2 = ((bf16[8,256,128]{2,1,0:T(8,128)(2,1)}), bf16[8,256,128]{2,1,0:T(8,128)(2,1)S(1)}, u32[]{:S(2)}, u32[]{:S(2)}) async-start(bf16[8,256,128]{2,1,0:T(8,128)(2,1)} %convolve.1), calls=%async_computation.2 | async-start | bytes 1048576 | tf_op jit(solution)/shard_map/all_to_all | solution.py:627
  82.3 1.6 %copy-start = (f32[2,512,512]{2,1,0:T(8,128)S(1)}, f32[2,512,512]{2,1,0:T(8,128)}, u32[]{:S(2)}) copy-start(f32[2,512,512]{2,1,0:T(8,128)} %query_terms.1.term_ref) | copy-start | bytes 6291460

commit v6 on v5

--- a/solution.py
+++ b/solution.py
@@ -17,7 +17,7 @@
 TAIL = 8
 PAD = 16
 BIG = 60 * 1024 * 1024
-FINISH_LIMIT = 50
+FINISH_LIMIT = 53
 COST = (10**8, 10**8, 10**8)
 
 VMEM_SPEC = pl.BlockSpec(memory_space=pltpu.VMEM)
@@ -141,6 +141,8 @@
     if ext_rows > PAD:
         rest = ext_rows - PAD
         sources.append((extra[0].at[pl.ds(PAD, rest)], x_ref.at[pl.ds(end, rest)], sem.at[count + 1]))
+    if with_filter:
+        filt_load = start_all([(extra[-1], filt_ref, sem.at[count + 2])])[0]
     waits = start_all(sources)
     loads = {}
     for at, s in enumerate(parts):
@@ -148,7 +150,8 @@
             cols = pl.ds(i * each_cols, each_cols)
             loads[s, i] = start_all([(w_hbm.at[s, :, cols], w_ref.at[at, i], w_sem.at[at, i])])[0]
     if with_filter:
-        filt_load = start_all([(extra[-1], filt_ref, sem.at[count + 2])])[0]
+        filt_load.wait()
+        pack_into(outs[1], length // 2, filt_ref, 0, filt_ref.shape[0])
     for wait in waits:
         wait.wait()
 
@@ -180,9 +183,6 @@
         pack_into(p_ref, 0, g_ref, 0, length)
         if ext_rows > PAD:
             pack_into(p_ref, length // 2, g_ref, length, PAD)
-        if with_filter:
-            filt_load.wait()
-            pack_into(p_ref, length // 2, filt_ref, 0, filt_ref.shape[0])
         sends += send(1)
     if 0 in parts:
         outs[-1][...] = mixed(0)[0]
@@ -539,24 +539,31 @@
     _, length, channels = terms.shape
     tiles = channels // LANES
 
-    def kernel(c_ref, term_ref, out_any, out_ref, sem):
+    def kernel(c_ref, term_any, out_any, term_ref, out_ref, in_sem, sem):
+        cols = [pl.ds(i * LANES, LANES) for i in range(tiles)]
+        loads = start_all((term_any.at[:, :, cols[i]], term_ref.at[i], in_sem.at[i]) for i in range(tiles))
         sends = []
         for i in range(tiles):
-            cols = slice(i * LANES, (i + 1) * LANES)
             top, bot = unpack_pair(c_ref[2 * i].astype(f32), c_ref[2 * i + 1].astype(f32))
+            loads[i].wait()
             for j, part in enumerate((top, bot)):
                 rows = slice(j * FINE, (j + 1) * FINE)
-                out_ref[i, rows] = (term_ref[0, rows, cols] * part + term_ref[1, rows, cols]).astype(bf16)
-            sends += start_all([(out_ref.at[i], out_any.at[:, pl.ds(i * LANES, LANES)], sem.at[i])])
+                out_ref[i, rows] = (term_ref[i, 0, rows] * part + term_ref[i, 1, rows]).astype(bf16)
+            sends += start_all([(out_ref.at[i], out_any.at[:, cols[i]], sem.at[i])])
         for send in sends:
             send.wait()
 
     return pl.pallas_call(
         kernel,
-        in_specs=[VMEM_SPEC] * 2,
+        in_specs=[VMEM_SPEC, ANY_SPEC],
         out_specs=ANY_SPEC,
         out_shape=jax.ShapeDtypeStruct((length, channels), bf16),
-        scratch_shapes=[pltpu.VMEM((tiles, length, LANES), bf16), pltpu.SemaphoreType.DMA((tiles,))],
+        scratch_shapes=[
+            pltpu.VMEM((tiles, 2, length, LANES), f32),
+            pltpu.VMEM((tiles, length, LANES), bf16),
+            pltpu.SemaphoreType.DMA((tiles,)),
+            pltpu.SemaphoreType.DMA((tiles,)),
+        ],
         compiler_params=pltpu.CompilerParams(vmem_limit_bytes=FINISH_LIMIT * 1024 * 1024),
         name="finish",
     )(conv, terms)

time: 85.4 us -> 84.2 us (0.986)
  local copies, waits for them, and re-layouts: 3.64 us -> 2.06 us
    unnamed x18 -> x16, local copies, waits for them, and re-layouts: 3.64 us -> 2.06 us
    pallas_call x1, Pallas kernels: 1.03 us -> 2.3 us  [finish(): pl.pallas_call(kernel, in_specs=[VMEM_SPEC, ANY_SPEC], out_specs=ANY_SPEC...]
    pallas_call x2, Pallas kernels: 15.2 us -> 14.2 us  [project(): pl.pallas_call(functools.partial(project_kernel, len(blocks), parts, spli...]
    ppermute x4, waiting for transfers between devices: 7 us -> 8 us  [swap(): lax.ppermute(x, 'tensor', [(i, i ^ bit) for i in range(tensor_count)])]
    all_to_all x1, waiting for transfers between devices: 3.83 us -> 2.84 us  [local(): early_sent = exchange(packs)]
  transfers between devices with their start and end apart: 9 -> 9, of which waited for: 6 -> 6; matrix products, arithmetic and copies ran while one was open for 2% -> 2% of each run, Pallas kernels for 34% -> 33%
where the time goes in v6:
time: 84.2 us; the launch traced here: 83.7 us
  Pallas kernels  38.2 us (45%)
  waiting for transfers between devices  20.9 us (25%)
  starting transfers between devices  20.7 us (25%)
  local copies, waits for them, and re-layouts  2.06 us (2%)
  other arithmetic  1.61 us (2%)
    pallas_call x2, Pallas kernels, project(): pl.pallas_call(functools.partial(project_kernel, len(blocks), parts, spli...  14.2 us
    pallas_call x1, Pallas kernels, query_terms(): pl.pallas_call(functools.partial(query_kernel, len(blocks)), in_specs=[pl...  8.62 us
    ppermute x4, waiting for transfers between devices, swap(): lax.ppermute(x, 'tensor', [(i, i ^ bit) for i in range(tensor_count)])  8 us
    all_to_all x1, starting transfers between devices, local(): early_sent = exchange(packs)  7.14 us
    pallas_call x1, Pallas kernels, convolve(): pl.pallas_call(functools.partial(conv_kernel, dev_count), in_specs=[pl.Bl...  5.85 us
    all_to_all x1, waiting for transfers between devices, local(): conv = exchange(convolve(half, early_sent, late_sent, spectrum, consts))  5.31 us
    pallas_call x1, Pallas kernels, filter_spectrum(): pl.pallas_call(functools.partial(filter_kernel, dev_count), in_specs=[ANY...  4.79 us
    all_to_all x1, waiting for transfers between devices, local(): late_sent = exchange(packs)  4.75 us
  transfers between devices with their start and end apart: 9, of which 6 were waited for; matrix products, arithmetic and copies ran while one was open for 2% of the time, Pallas kernels for 33%

profile of v6, /device:TPU:0, one launch (start us, length us, event | category | flops | bytes accessed | tf_op | source)
XLA Modules:
  0.0 83.7 jit_solution(2480343917996026312)
XLA Ops:
  0.0 2.5 %norm_rows.1 = (bf16[128,4096]{1,0:T(8,128)(2,1)}, bf16[8,4096]{1,0:T(8,128)(2,1)}) custom-call(bf16[128,4096]{1,0:T(8,128)(2,1)} %tok_hbm.1, f32[1,4096]{1,0:T(1,128)} %bitcast.11), custom_call_target="tpu_custom_call" | custom-call | tf_op jit(solution)/shard_map/norm_rows/pallas_call | solution.py:91
  2.5 0.5 collective-permute-start
  3.0 2.6 %collective-permute-start.3 = (bf16[128,4096]{1,0:T(8,128)(2,1)}, bf16[128,4096]{1,0:T(8,128)(2,1)S(1)}, u32[]{:S(2)}, u32[]{:S(2)}) collective-permute-start(bf16[128,4096]{1,0:T(8,128)(2,1)} %get-tuple-element.19.refs_0_), channel_id=1, source_target_pairs={{0,2},{1,3},{2,0},{3,1},{4,6},{5,7},{6,4},{7,5},{8,10},{9,11},{10,... | collective-permute-start | bytes 3145736 | tf_op jit(solution)/shard_map/ppermute | solution.py:589
  5.6 0.0 collective-permute-done.refs_1_
  5.6 0.0 copy-start.1
  5.6 0.7 collective-permute-start.2
  6.2 1.3 %collective-permute-start.1 = (bf16[8,4096]{1,0:T(8,128)(2,1)}, bf16[8,4096]{1,0:T(8,128)(2,1)S(1)}, u32[]{:S(2)}, u32[]{:S(2)}) collective-permute-start(bf16[8,4096]{1,0:T(8,128)(2,1)} %get-tuple-element.22), channel_id=1, source_target_pairs={{3,6},{7,10},{11,14},{15,18},{19,22},{23,26},{27,30},{1,0},{5,4},{... | collective-permute-start | bytes 196616 | tf_op jit(solution)/shard_map/ppermute | solution.py:609
  7.5 0.0 copy-done.1
  7.6 7.1 %project.2 = (f32[256,512]{1,0:T(8,128)}, bf16[8,384,128]{2,1,0:T(8,128)(2,1)}) custom-call(s32[1]{0:T(128)} %bitcast.1.me_ref, bf16[128,4096]{1,0:T(8,128)(2,1)} %get-tuple-element.19.refs_0_, bf16[128,4096]{1,0:T(8,128)(2,1)} %copy-done.1, bf16[3,4096,512]{2,1,0:T(8,128)(2,1)} %bitcast.8, f32[3,3,512]{2,1,0:T(4,128)} %refs_6_.1, f32[512,512]{1,0:T(8,128)} %refs_4_.1), custom_call_target="tpu_custom_call" | custom-call | flops 100000000 | bytes 100000 | tf_op jit(solution)/shard_map/project/pallas_call | solution.py:211
  14.7 0.0 collective-permute-done.2
  14.7 0.0 collective-permute-done.1
  14.7 7.1 %all-to-all-start = ((bf16[8,384,128]{2,1,0:T(8,128)(2,1)}), bf16[8,384,128]{2,1,0:T(8,128)(2,1)S(1)}, u32[]{:S(2)}, u32[]{:S(2)}) async-start(bf16[8,384,128]{2,1,0:T(8,128)(2,1)} %get-tuple-element.23), calls=%async_computation | async-start | bytes 1572864 | tf_op jit(solution)/shard_map/all_to_all | solution.py:622
  21.9 1.5 %collective-permute-start.5 = (bf16[8,4096]{1,0:T(8,128)(2,1)S(1)}, bf16[8,4096]{1,0:T(8,128)(2,1)S(1)}, u32[]{:S(2)}, u32[]{:S(2)}) collective-permute-start(bf16[8,4096]{1,0:T(8,128)(2,1)S(1)} %add.12), channel_id=1, source_target_pairs={{0,2},{1,3},{2,0},{3,1},{4,6},{5,7},{6,4},{7,5},{8,10},{9,11},{10,... | collective-permute-start | bytes 196616 | tf_op jit(solution)/shard_map/ppermute | solution.py:589
  23.4 6.4 %collective-permute-done.3.refs_0_.refs_2_ = bf16[128,4096]{1,0:T(8,128)(2,1)S(1)} collective-permute-done((bf16[128,4096]{1,0:T(8,128)(2,1)}, bf16[128,4096]{1,0:T(8,128)(2,1)S(1)}, u32[]{:S(2)}, u32[]{:S(2)}) %collective-permute-start.3) | collective-permute-done | bytes 1048608 | tf_op jit(solution)/shard_map/ppermute | solution.py:589
  29.8 0.0 copy-start.2
  29.8 0.0 collective-permute-start.4
  29.8 1.1 %collective-permute-done.5 = bf16[8,4096]{1,0:T(8,128)(2,1)S(1)} collective-permute-done((bf16[8,4096]{1,0:T(8,128)(2,1)S(1)}, bf16[8,4096]{1,0:T(8,128)(2,1)S(1)}, u32[]{:S(2)}, u32[]{:S(2)}) %collective-permute-start.5) | collective-permute-done | bytes 65568 | tf_op jit(solution)/shard_map/ppermute | solution.py:589
  30.9 1.0 %add_dynamic-update-slice_fusion.refs_4_ = bf16[48,4096]{1,0:T(8,128)(2,1)S(1)} fusion(bf16[48,4096]{1,0:T(8,128)(2,1)S(1)} %constant_dynamic-update-slice_fusion, bf16[128,4096]{1,0:T(8,128)(2,1)} %copy-done.1, bf16[128,4096]{1,0:T(8,128)(2,1)} %get-tuple-element.19.refs_0_, pred[]{:T(512)} %bitcast.5, pred[]{:T(512)} %bitcast.4), kind=kLoop, calls=%fused_computation | loop fusion | flops 393216 | bytes 393218 | tf_op jit(solution)/shard_map/concatenate | solution.py:626
  31.9 0.0 copy-start.4
  32.0 0.5 collective-permute-done.4.refs_1_.refs_3_
  32.4 0.0 copy-done.2
  32.4 0.3 copy-done.4
  32.7 0.0 copy-start.3
  32.7 1.0 %copy-done.3 = bf16[128,4096]{1,0:T(8,128)(2,1)} copy-done((bf16[128,4096]{1,0:T(8,128)(2,1)}, bf16[128,4096]{1,0:T(8,128)(2,1)S(1)}, u32[]{:S(2)}) %copy-start.3) | copy-done | bytes 1048600
  33.7 7.1 %project.3 = (f32[272,512]{1,0:T(8,128)}, bf16[8,136,128]{2,1,0:T(8,128)(2,1)}) custom-call(s32[1]{0:T(128)} %bitcast.1.me_ref, bf16[128,4096]{1,0:T(8,128)(2,1)} %copy-done.2, bf16[128,4096]{1,0:T(8,128)(2,1)} %copy-done.3, bf16[3,4096,512]{2,1,0:T(8,128)(2,1)} %bitcast.9, f32[3,3,512]{2,1,0:T(4,128)} %refs_6_.1, bf16[48,4096]{1,0:T(8,128)(2,1)} %copy-done.4), custom_call_target="tpu_custom_call" | custom-call | flops 100000000 | bytes 100000 | tf_op jit(solution)/shard_map/project/pallas_call | solution.py:211
  40.8 2.8 %all-to-all-done.x_any.early_any = bf16[8,384,128]{2,1,0:T(8,128)(2,1)S(1)} async-done(((bf16[8,384,128]{2,1,0:T(8,128)(2,1)}), bf16[8,384,128]{2,1,0:T(8,128)(2,1)S(1)}, u32[]{:S(2)}, u32[]{:S(2)}) %all-to-all-start) | async-done | bytes 786464 | tf_op jit(solution)/shard_map/all_to_all | solution.py:622
  43.6 0.0 copy-start
  43.6 3.4 %all-to-all-start.1 = ((bf16[8,136,128]{2,1,0:T(8,128)(2,1)}), bf16[8,136,128]{2,1,0:T(8,128)(2,1)S(1)}, u32[]{:S(2)}, u32[]{:S(2)}) async-start(bf16[8,136,128]{2,1,0:T(8,128)(2,1)} %get-tuple-element.26), calls=%async_computation.1 | async-start | bytes 557056 | tf_op jit(solution)/shard_map/all_to_all | solution.py:632
  47.1 0.0 copy-done
  47.1 4.8 %filter_spectrum.1.h_hbm = f32[9,256,256]{2,1,0:T(8,128)} custom-call(bf16[8,384,128]{2,1,0:T(8,128)(2,1)} %copy-done, f32[256,256]{1,0:T(8,128)} %constant.44.clone.refs_0_, f32[256,256]{1,0:T(8,128)} %constant.45.clone.refs_1_, f32[9,2,128]{2,1,0:T(2,128)} %constant.46.clone.refs_2_, bf16[512,256]{1,0:T(8,128)(2,1)} %constant.47.clone.refs_3_), custom_call_target="tpu_custom_call" | custom-call | tf_op jit(solution)/shard_map/filter_spectrum/pallas_call | solution.py:443
  51.9 4.7 %all-to-all-done.1.late_any = bf16[8,136,128]{2,1,0:T(8,128)(2,1)S(1)} async-done(((bf16[8,136,128]{2,1,0:T(8,128)(2,1)}), bf16[8,136,128]{2,1,0:T(8,128)(2,1)S(1)}, u32[]{:S(2)}, u32[]{:S(2)}) %all-to-all-start.1) | async-done | bytes 278560 | tf_op jit(solution)/shard_map/all_to_all | solution.py:632
  56.6 0.0 copy-start.5
  56.6 0.7 copy-done.5
  57.4 5.8 %convolve.1 = bf16[8,256,128]{2,1,0:T(8,128)(2,1)} custom-call(s32[1]{0:T(128)} %bitcast.half_ref, bf16[8,384,128]{2,1,0:T(8,128)(2,1)} %copy-done, bf16[8,136,128]{2,1,0:T(8,128)(2,1)} %copy-done.5, f32[9,256,256]{2,1,0:T(8,128)} %filter_spectrum.1.h_hbm, f32[256,256]{1,0:T(8,128)} %constant.44.clone.refs_0_, f32[256,256]{1,0:T(8,128)} %constant.45.clone.refs_1_, ...), custom_call_target="tpu_custom_call" | custom-call | tf_op jit(solution)/shard_map/convolve/pallas_call | solution.py:458
  63.2 3.6 %all-to-all-start.2 = ((bf16[8,256,128]{2,1,0:T(8,128)(2,1)}), bf16[8,256,128]{2,1,0:T(8,128)(2,1)S(1)}, u32[]{:S(2)}, u32[]{:S(2)}) async-start(bf16[8,256,128]{2,1,0:T(8,128)(2,1)} %convolve.1), calls=%async_computation.2 | async-start | bytes 1048576 | tf_op jit(solution)/shard_map/all_to_all | solution.py:634
  66.8 0.6 pad_add_fusion.me_ref
  67.4 8.6 %query_terms.1.term_any = f32[2,512,512]{2,1,0:T(8,128)} custom-call(s32[2]{0:T(128)} %pad_add_fusion.me_ref, bf16[128,4096]{1,0:T(8,128)(2,1)} %get-tuple-element.19.refs_0_, bf16[128,4096]{1,0:T(8,128)(2,1)} %copy-done.1, bf16[128,4096]{1,0:T(8,128)(2,1)} %copy-done.2, bf16[128,4096]{1,0:T(8,128)(2,1)} %copy-done.3, bf16[48,4096]{1,0:T(8,128)(2,1)} %copy-done.4, ...), custom_call_target="tpu_custom_call" | custom-call | flops 100000000 | bytes 100000 | tf_op jit(solution)/shard_map/query_terms/pallas_call | solution.py:515
  76.0 5.3 %all-to-all-done.2.c_ref = bf16[8,256,128]{2,1,0:T(8,128)(2,1)S(1)} async-done(((bf16[8,256,128]{2,1,0:T(8,128)(2,1)}), bf16[8,256,128]{2,1,0:T(8,128)(2,1)S(1)}, u32[]{:S(2)}, u32[]{:S(2)}) %all-to-all-start.2) | async-done | bytes 524320 | tf_op jit(solution)/shard_map/all_to_all | solution.py:634
  81.4 2.3 %finish.1 = bf16[512,512]{1,0:T(8,128)(2,1)} custom-call(bf16[8,256,128]{2,1,0:T(8,128)(2,1)S(1)} %all-to-all-done.2.c_ref, f32[2,512,512]{2,1,0:T(8,128)} %query_terms.1.term_any), custom_call_target="tpu_custom_call" | custom-call | tf_op jit(solution)/shard_map/finish/pallas_call | solution.py:556
  (5 shorter events, 0.0 us)
Async XLA Ops:
  2.5 3.1 %collective-permute-start = (bf16[128,4096]{1,0:T(8,128)(2,1)}, bf16[128,4096]{1,0:T(8,128)(2,1)S(1)}, u32[]{:S(2)}, u32[]{:S(2)}) collective-permute-start(bf16[128,4096]{1,0:T(8,128)(2,1)} %get-tuple-element.19.refs_0_), channel_id=1, source_target_pairs={{0,1},{1,0},{2,3},{3,2},{4,5},{5,4},{6,7},{7,6},{8,9},{9,8},{10,11... | collective-permute-start | bytes 3145736 | tf_op jit(solution)/shard_map/ppermute | solution.py:589
  3.0 26.8 %collective-permute-start.3 = (bf16[128,4096]{1,0:T(8,128)(2,1)}, bf16[128,4096]{1,0:T(8,128)(2,1)S(1)}, u32[]{:S(2)}, u32[]{:S(2)}) collective-permute-start(bf16[128,4096]{1,0:T(8,128)(2,1)} %get-tuple-element.19.refs_0_), channel_id=1, source_target_pairs={{0,2},{1,3},{2,0},{3,1},{4,6},{5,7},{6,4},{7,5},{8,10},{9,11},{10,... | collective-permute-start | bytes 3145736 | tf_op jit(solution)/shard_map/ppermute | solution.py:589
  5.6 2.0 %copy-start.1 = (bf16[128,4096]{1,0:T(8,128)(2,1)}, bf16[128,4096]{1,0:T(8,128)(2,1)S(1)}, u32[]{:S(2)}) copy-start(bf16[128,4096]{1,0:T(8,128)(2,1)S(1)} %collective-permute-done.refs_1_) | copy-start | bytes 3145732
  5.6 9.1 %collective-permute-start.2 = (bf16[8,4096]{1,0:T(8,128)(2,1)}, bf16[8,4096]{1,0:T(8,128)(2,1)S(1)}, u32[]{:S(2)}, u32[]{:S(2)}) collective-permute-start(bf16[8,4096]{1,0:T(8,128)(2,1)} %get-tuple-element.22), channel_id=1, source_target_pairs={{3,7},{7,11},{11,15},{15,19},{19,23},{23,27},{27,31},{1,1},{5,5},{... | collective-permute-start | bytes 196616 | tf_op jit(solution)/shard_map/ppermute | solution.py:609
  6.2 8.5 %collective-permute-start.1 = (bf16[8,4096]{1,0:T(8,128)(2,1)}, bf16[8,4096]{1,0:T(8,128)(2,1)S(1)}, u32[]{:S(2)}, u32[]{:S(2)}) collective-permute-start(bf16[8,4096]{1,0:T(8,128)(2,1)} %get-tuple-element.22), channel_id=1, source_target_pairs={{3,6},{7,10},{11,14},{15,18},{19,22},{23,26},{27,30},{1,0},{5,4},{... | collective-permute-start | bytes 196616 | tf_op jit(solution)/shard_map/ppermute | solution.py:609
  14.7 28.9 %all-to-all-start = ((bf16[8,384,128]{2,1,0:T(8,128)(2,1)}), bf16[8,384,128]{2,1,0:T(8,128)(2,1)S(1)}, u32[]{:S(2)}, u32[]{:S(2)}) async-start(bf16[8,384,128]{2,1,0:T(8,128)(2,1)} %get-tuple-element.23), calls=%async_computation | async-start | bytes 1572864 | tf_op jit(solution)/shard_map/all_to_all | solution.py:622
  21.9 9.0 %collective-permute-start.5 = (bf16[8,4096]{1,0:T(8,128)(2,1)S(1)}, bf16[8,4096]{1,0:T(8,128)(2,1)S(1)}, u32[]{:S(2)}, u32[]{:S(2)}) collective-permute-start(bf16[8,4096]{1,0:T(8,128)(2,1)S(1)} %add.12), channel_id=1, source_target_pairs={{0,2},{1,3},{2,0},{3,1},{4,6},{5,7},{6,4},{7,5},{8,10},{9,11},{10,... | collective-permute-start | bytes 196616 | tf_op jit(solution)/shard_map/ppermute | solution.py:589
  29.8 2.7 %copy-start.2 = (bf16[128,4096]{1,0:T(8,128)(2,1)}, bf16[128,4096]{1,0:T(8,128)(2,1)S(1)}, u32[]{:S(2)}) copy-start(bf16[128,4096]{1,0:T(8,128)(2,1)S(1)} %collective-permute-done.3.refs_0_.refs_2_) | copy-start | bytes 3145732
  29.8 2.7 %collective-permute-start.4 = (bf16[128,4096]{1,0:T(8,128)(2,1)S(1)}, bf16[128,4096]{1,0:T(8,128)(2,1)S(1)}, u32[]{:S(2)}, u32[]{:S(2)}) collective-permute-start(bf16[128,4096]{1,0:T(8,128)(2,1)S(1)} %collective-permute-done.3.refs_0_.refs_2_), channel_id=1, source_target_pairs={{0,1},{1,0},{2,3},{3,2},{4,5},{5,4},{6,7},{7,6},{8,9},{9,8},{10,11... | collective-permute-start | bytes 3145736 | tf_op jit(solution)/shard_map/ppermute | solution.py:589
  31.9 0.8 copy-start.4
  32.7 1.0 %copy-start.3 = (bf16[128,4096]{1,0:T(8,128)(2,1)}, bf16[128,4096]{1,0:T(8,128)(2,1)S(1)}, u32[]{:S(2)}) copy-start(bf16[128,4096]{1,0:T(8,128)(2,1)S(1)} %collective-permute-done.4.refs_1_.refs_3_) | copy-start | bytes 3145732
  43.6 3.4 %copy-start = (bf16[8,384,128]{2,1,0:T(8,128)(2,1)}, bf16[8,384,128]{2,1,0:T(8,128)(2,1)S(1)}, u32[]{:S(2)}) copy-start(bf16[8,384,128]{2,1,0:T(8,128)(2,1)S(1)} %all-to-all-done.x_any.early_any) | copy-start | bytes 2359300
  43.6 13.0 %all-to-all-start.1 = ((bf16[8,136,128]{2,1,0:T(8,128)(2,1)}), bf16[8,136,128]{2,1,0:T(8,128)(2,1)S(1)}, u32[]{:S(2)}, u32[]{:S(2)}) async-start(bf16[8,136,128]{2,1,0:T(8,128)(2,1)} %get-tuple-element.26), calls=%async_computation.1 | async-start | bytes 557056 | tf_op jit(solution)/shard_map/all_to_all | solution.py:632
  56.6 0.7 copy-start.5
  63.2 18.1 %all-to-all-start.2 = ((bf16[8,256,128]{2,1,0:T(8,128)(2,1)}), bf16[8,256,128]{2,1,0:T(8,128)(2,1)S(1)}, u32[]{:S(2)}, u32[]{:S(2)}) async-start(bf16[8,256,128]{2,1,0:T(8,128)(2,1)} %convolve.1), calls=%async_computation.2 | async-start | bytes 1048576 | tf_op jit(solution)/shard_map/all_to_all | solution.py:634

commit v7 on v6

--- a/solution.py
+++ b/solution.py
@@ -68,7 +68,7 @@
 
 def norm_rows(tokens, gain):
     rows, width = tokens.shape
-    step = min(32, rows)
+    step = min(64, rows)
 
     def kernel(tok_hbm, gain_hbm, out_any, tail_any, tok_ref, gain_ref, out_ref, sem, out_sem):
         parts = [pl.ds(i * step, step) for i in range(rows // step)]
@@ -400,9 +400,10 @@
 
     lax.fori_loop(0, dev_count + 1, body, 0, unroll=dev_count <= 8)
     sends = []
-    for i in range(2):
-        rows = pl.ds(i * FINE // 2, FINE // 2)
-        coarse_inverse(dev_count, e_ref, y_ref, i * FINE // 2, FINE // 2)
+    size = FINE // 4
+    for i in range(4):
+        rows = pl.ds(i * size, size)
+        coarse_inverse(dev_count, e_ref, y_ref, i * size, size)
         sends += start_all([(y_ref.at[:, rows], y_any.at[:, rows], y_sem.at[i])])
     for send in sends:
         send.wait()
@@ -471,7 +472,7 @@
             pltpu.VMEM((dev_count + 1, FINE, 2 * LANES), f32),
             pltpu.VMEM((dev_count, FINE, LANES), bf16),
             pltpu.SemaphoreType.DMA((7,)),
-            pltpu.SemaphoreType.DMA((2,)),
+            pltpu.SemaphoreType.DMA((4,)),
         ],
         compiler_params=pltpu.CompilerParams(vmem_limit_bytes=BIG),
         name="convolve",

time: 84.2 us -> 84.2 us (level)
  no operation moved by 1% of the time
where the time goes in v7:
time: 84.2 us; the launch traced here: 83.7 us
  Pallas kernels  38.2 us (45%)
  waiting for transfers between devices  20.9 us (25%)
  starting transfers between devices  20.7 us (25%)
  local copies, waits for them, and re-layouts  2.06 us (2%)
  other arithmetic  1.61 us (2%)
    pallas_call x2, Pallas kernels, project(): pl.pallas_call(functools.partial(project_kernel, len(blocks), parts, spli...  14.2 us
    pallas_call x1, Pallas kernels, query_terms(): pl.pallas_call(functools.partial(query_kernel, len(blocks)), in_specs=[pl...  8.62 us
    ppermute x4, waiting for transfers between devices, swap(): lax.ppermute(x, 'tensor', [(i, i ^ bit) for i in range(tensor_count)])  8 us
    all_to_all x1, starting transfers between devices, local(): early_sent = exchange(packs)  7.14 us
    pallas_call x1, Pallas kernels, convolve(): pl.pallas_call(functools.partial(conv_kernel, dev_count), in_specs=[pl.Bl...  5.87 us
    all_to_all x1, waiting for transfers between devices, local(): conv = exchange(convolve(half, early_sent, late_sent, spectrum, consts))  5.31 us
    pallas_call x1, Pallas kernels, filter_spectrum(): pl.pallas_call(functools.partial(filter_kernel, dev_count), in_specs=[ANY...  4.79 us
    all_to_all x1, waiting for transfers between devices, local(): late_sent = exchange(packs)  4.75 us
  transfers between devices with their start and end apart: 9, of which 6 were waited for; matrix products, arithmetic and copies ran while one was open for 2% of the time, Pallas kernels for 33%

profile of v7, /device:TPU:0, one launch (start us, length us, event | category | flops | bytes accessed | tf_op | source)
XLA Modules:
  0.0 83.7 jit_solution(7546363510067463582)
XLA Ops:
  0.0 2.5 %norm_rows.1 = (bf16[128,4096]{1,0:T(8,128)(2,1)}, bf16[8,4096]{1,0:T(8,128)(2,1)}) custom-call(bf16[128,4096]{1,0:T(8,128)(2,1)} %tok_hbm.1, f32[1,4096]{1,0:T(1,128)} %bitcast.11), custom_call_target="tpu_custom_call" | custom-call | tf_op jit(solution)/shard_map/norm_rows/pallas_call | solution.py:91
  2.5 0.5 collective-permute-start
  3.0 2.6 %collective-permute-start.3 = (bf16[128,4096]{1,0:T(8,128)(2,1)}, bf16[128,4096]{1,0:T(8,128)(2,1)S(1)}, u32[]{:S(2)}, u32[]{:S(2)}) collective-permute-start(bf16[128,4096]{1,0:T(8,128)(2,1)} %get-tuple-element.19.refs_0_), channel_id=1, source_target_pairs={{0,2},{1,3},{2,0},{3,1},{4,6},{5,7},{6,4},{7,5},{8,10},{9,11},{10,... | collective-permute-start | bytes 3145736 | tf_op jit(solution)/shard_map/ppermute | solution.py:590
  5.6 0.0 collective-permute-done.refs_1_
  5.6 0.0 copy-start.1
  5.6 0.7 collective-permute-start.2
  6.2 1.3 %collective-permute-start.1 = (bf16[8,4096]{1,0:T(8,128)(2,1)}, bf16[8,4096]{1,0:T(8,128)(2,1)S(1)}, u32[]{:S(2)}, u32[]{:S(2)}) collective-permute-start(bf16[8,4096]{1,0:T(8,128)(2,1)} %get-tuple-element.22), channel_id=1, source_target_pairs={{3,6},{7,10},{11,14},{15,18},{19,22},{23,26},{27,30},{1,0},{5,4},{... | collective-permute-start | bytes 196616 | tf_op jit(solution)/shard_map/ppermute | solution.py:610
  7.6 0.0 copy-done.1
  7.6 7.1 %project.2 = (f32[256,512]{1,0:T(8,128)}, bf16[8,384,128]{2,1,0:T(8,128)(2,1)}) custom-call(s32[1]{0:T(128)} %bitcast.1.me_ref, bf16[128,4096]{1,0:T(8,128)(2,1)} %get-tuple-element.19.refs_0_, bf16[128,4096]{1,0:T(8,128)(2,1)} %copy-done.1, bf16[3,4096,512]{2,1,0:T(8,128)(2,1)} %bitcast.8, f32[3,3,512]{2,1,0:T(4,128)} %refs_6_.1, f32[512,512]{1,0:T(8,128)} %refs_4_.1), custom_call_target="tpu_custom_call" | custom-call | flops 100000000 | bytes 100000 | tf_op jit(solution)/shard_map/project/pallas_call | solution.py:211
  14.7 0.0 collective-permute-done.2
  14.7 0.0 collective-permute-done.1
  14.7 7.1 %all-to-all-start = ((bf16[8,384,128]{2,1,0:T(8,128)(2,1)}), bf16[8,384,128]{2,1,0:T(8,128)(2,1)S(1)}, u32[]{:S(2)}, u32[]{:S(2)}) async-start(bf16[8,384,128]{2,1,0:T(8,128)(2,1)} %get-tuple-element.23), calls=%async_computation | async-start | bytes 1572864 | tf_op jit(solution)/shard_map/all_to_all | solution.py:623
  21.9 1.5 %collective-permute-start.5 = (bf16[8,4096]{1,0:T(8,128)(2,1)S(1)}, bf16[8,4096]{1,0:T(8,128)(2,1)S(1)}, u32[]{:S(2)}, u32[]{:S(2)}) collective-permute-start(bf16[8,4096]{1,0:T(8,128)(2,1)S(1)} %add.12), channel_id=1, source_target_pairs={{0,2},{1,3},{2,0},{3,1},{4,6},{5,7},{6,4},{7,5},{8,10},{9,11},{10,... | collective-permute-start | bytes 196616 | tf_op jit(solution)/shard_map/ppermute | solution.py:590
  23.4 6.4 %collective-permute-done.3.refs_0_.refs_2_ = bf16[128,4096]{1,0:T(8,128)(2,1)S(1)} collective-permute-done((bf16[128,4096]{1,0:T(8,128)(2,1)}, bf16[128,4096]{1,0:T(8,128)(2,1)S(1)}, u32[]{:S(2)}, u32[]{:S(2)}) %collective-permute-start.3) | collective-permute-done | bytes 1048608 | tf_op jit(solution)/shard_map/ppermute | solution.py:590
  29.8 0.0 copy-start.2
  29.8 0.0 collective-permute-start.4
  29.8 1.1 %collective-permute-done.5 = bf16[8,4096]{1,0:T(8,128)(2,1)S(1)} collective-permute-done((bf16[8,4096]{1,0:T(8,128)(2,1)S(1)}, bf16[8,4096]{1,0:T(8,128)(2,1)S(1)}, u32[]{:S(2)}, u32[]{:S(2)}) %collective-permute-start.5) | collective-permute-done | bytes 65568 | tf_op jit(solution)/shard_map/ppermute | solution.py:590
  30.9 1.0 %add_dynamic-update-slice_fusion.refs_4_ = bf16[48,4096]{1,0:T(8,128)(2,1)S(1)} fusion(bf16[48,4096]{1,0:T(8,128)(2,1)S(1)} %constant_dynamic-update-slice_fusion, bf16[128,4096]{1,0:T(8,128)(2,1)} %copy-done.1, bf16[128,4096]{1,0:T(8,128)(2,1)} %get-tuple-element.19.refs_0_, pred[]{:T(512)} %bitcast.5, pred[]{:T(512)} %bitcast.4), kind=kLoop, calls=%fused_computation | loop fusion | flops 393216 | bytes 393218 | tf_op jit(solution)/shard_map/concatenate | solution.py:627
  31.9 0.0 copy-start.4
  32.0 0.5 collective-permute-done.4.refs_1_.refs_3_
  32.4 0.0 copy-done.2
  32.4 0.3 copy-done.4
  32.7 0.0 copy-start.3
  32.7 1.0 %copy-done.3 = bf16[128,4096]{1,0:T(8,128)(2,1)} copy-done((bf16[128,4096]{1,0:T(8,128)(2,1)}, bf16[128,4096]{1,0:T(8,128)(2,1)S(1)}, u32[]{:S(2)}) %copy-start.3) | copy-done | bytes 1048600
  33.7 7.1 %project.3 = (f32[272,512]{1,0:T(8,128)}, bf16[8,136,128]{2,1,0:T(8,128)(2,1)}) custom-call(s32[1]{0:T(128)} %bitcast.1.me_ref, bf16[128,4096]{1,0:T(8,128)(2,1)} %copy-done.2, bf16[128,4096]{1,0:T(8,128)(2,1)} %copy-done.3, bf16[3,4096,512]{2,1,0:T(8,128)(2,1)} %bitcast.9, f32[3,3,512]{2,1,0:T(4,128)} %refs_6_.1, bf16[48,4096]{1,0:T(8,128)(2,1)} %copy-done.4), custom_call_target="tpu_custom_call" | custom-call | flops 100000000 | bytes 100000 | tf_op jit(solution)/shard_map/project/pallas_call | solution.py:211
  40.8 2.8 %all-to-all-done.x_any.early_any = bf16[8,384,128]{2,1,0:T(8,128)(2,1)S(1)} async-done(((bf16[8,384,128]{2,1,0:T(8,128)(2,1)}), bf16[8,384,128]{2,1,0:T(8,128)(2,1)S(1)}, u32[]{:S(2)}, u32[]{:S(2)}) %all-to-all-start) | async-done | bytes 786464 | tf_op jit(solution)/shard_map/all_to_all | solution.py:623
  43.6 0.0 copy-start
  43.6 3.4 %all-to-all-start.1 = ((bf16[8,136,128]{2,1,0:T(8,128)(2,1)}), bf16[8,136,128]{2,1,0:T(8,128)(2,1)S(1)}, u32[]{:S(2)}, u32[]{:S(2)}) async-start(bf16[8,136,128]{2,1,0:T(8,128)(2,1)} %get-tuple-element.26), calls=%async_computation.1 | async-start | bytes 557056 | tf_op jit(solution)/shard_map/all_to_all | solution.py:633
  47.1 0.0 copy-done
  47.1 4.8 %filter_spectrum.1.h_hbm = f32[9,256,256]{2,1,0:T(8,128)} custom-call(bf16[8,384,128]{2,1,0:T(8,128)(2,1)} %copy-done, f32[256,256]{1,0:T(8,128)} %constant.44.clone.refs_0_, f32[256,256]{1,0:T(8,128)} %constant.45.clone.refs_1_, f32[9,2,128]{2,1,0:T(2,128)} %constant.46.clone.refs_2_, bf16[512,256]{1,0:T(8,128)(2,1)} %constant.47.clone.refs_3_), custom_call_target="tpu_custom_call" | custom-call | tf_op jit(solution)/shard_map/filter_spectrum/pallas_call | solution.py:444
  51.9 4.7 %all-to-all-done.1.late_any = bf16[8,136,128]{2,1,0:T(8,128)(2,1)S(1)} async-done(((bf16[8,136,128]{2,1,0:T(8,128)(2,1)}), bf16[8,136,128]{2,1,0:T(8,128)(2,1)S(1)}, u32[]{:S(2)}, u32[]{:S(2)}) %all-to-all-start.1) | async-done | bytes 278560 | tf_op jit(solution)/shard_map/all_to_all | solution.py:633
  56.6 0.0 copy-start.5
  56.6 0.7 copy-done.5
  57.4 5.9 %convolve.1 = bf16[8,256,128]{2,1,0:T(8,128)(2,1)} custom-call(s32[1]{0:T(128)} %bitcast.half_ref, bf16[8,384,128]{2,1,0:T(8,128)(2,1)} %copy-done, bf16[8,136,128]{2,1,0:T(8,128)(2,1)} %copy-done.5, f32[9,256,256]{2,1,0:T(8,128)} %filter_spectrum.1.h_hbm, f32[256,256]{1,0:T(8,128)} %constant.44.clone.refs_0_, f32[256,256]{1,0:T(8,128)} %constant.45.clone.refs_1_, ...), custom_call_target="tpu_custom_call" | custom-call | tf_op jit(solution)/shard_map/convolve/pallas_call | solution.py:459
  63.2 3.6 %all-to-all-start.2 = ((bf16[8,256,128]{2,1,0:T(8,128)(2,1)}), bf16[8,256,128]{2,1,0:T(8,128)(2,1)S(1)}, u32[]{:S(2)}, u32[]{:S(2)}) async-start(bf16[8,256,128]{2,1,0:T(8,128)(2,1)} %convolve.1), calls=%async_computation.2 | async-start | bytes 1048576 | tf_op jit(solution)/shard_map/all_to_all | solution.py:635
  66.9 0.6 pad_add_fusion.me_ref
  67.4 8.6 %query_terms.1.term_any = f32[2,512,512]{2,1,0:T(8,128)} custom-call(s32[2]{0:T(128)} %pad_add_fusion.me_ref, bf16[128,4096]{1,0:T(8,128)(2,1)} %get-tuple-element.19.refs_0_, bf16[128,4096]{1,0:T(8,128)(2,1)} %copy-done.1, bf16[128,4096]{1,0:T(8,128)(2,1)} %copy-done.2, bf16[128,4096]{1,0:T(8,128)(2,1)} %copy-done.3, bf16[48,4096]{1,0:T(8,128)(2,1)} %copy-done.4, ...), custom_call_target="tpu_custom_call" | custom-call | flops 100000000 | bytes 100000 | tf_op jit(solution)/shard_map/query_terms/pallas_call | solution.py:516
  76.1 5.3 %all-to-all-done.2.c_ref = bf16[8,256,128]{2,1,0:T(8,128)(2,1)S(1)} async-done(((bf16[8,256,128]{2,1,0:T(8,128)(2,1)}), bf16[8,256,128]{2,1,0:T(8,128)(2,1)S(1)}, u32[]{:S(2)}, u32[]{:S(2)}) %all-to-all-start.2) | async-done | bytes 524320 | tf_op jit(solution)/shard_map/all_to_all | solution.py:635
  81.4 2.3 %finish.1 = bf16[512,512]{1,0:T(8,128)(2,1)} custom-call(bf16[8,256,128]{2,1,0:T(8,128)(2,1)S(1)} %all-to-all-done.2.c_ref, f32[2,512,512]{2,1,0:T(8,128)} %query_terms.1.term_any), custom_call_target="tpu_custom_call" | custom-call | tf_op jit(solution)/shard_map/finish/pallas_call | solution.py:557
  (5 shorter events, 0.0 us)
Async XLA Ops:
  2.5 3.1 %collective-permute-start = (bf16[128,4096]{1,0:T(8,128)(2,1)}, bf16[128,4096]{1,0:T(8,128)(2,1)S(1)}, u32[]{:S(2)}, u32[]{:S(2)}) collective-permute-start(bf16[128,4096]{1,0:T(8,128)(2,1)} %get-tuple-element.19.refs_0_), channel_id=1, source_target_pairs={{0,1},{1,0},{2,3},{3,2},{4,5},{5,4},{6,7},{7,6},{8,9},{9,8},{10,11... | collective-permute-start | bytes 3145736 | tf_op jit(solution)/shard_map/ppermute | solution.py:590
  3.0 26.8 %collective-permute-start.3 = (bf16[128,4096]{1,0:T(8,128)(2,1)}, bf16[128,4096]{1,0:T(8,128)(2,1)S(1)}, u32[]{:S(2)}, u32[]{:S(2)}) collective-permute-start(bf16[128,4096]{1,0:T(8,128)(2,1)} %get-tuple-element.19.refs_0_), channel_id=1, source_target_pairs={{0,2},{1,3},{2,0},{3,1},{4,6},{5,7},{6,4},{7,5},{8,10},{9,11},{10,... | collective-permute-start | bytes 3145736 | tf_op jit(solution)/shard_map/ppermute | solution.py:590
  5.6 2.0 %copy-start.1 = (bf16[128,4096]{1,0:T(8,128)(2,1)}, bf16[128,4096]{1,0:T(8,128)(2,1)S(1)}, u32[]{:S(2)}) copy-start(bf16[128,4096]{1,0:T(8,128)(2,1)S(1)} %collective-permute-done.refs_1_) | copy-start | bytes 3145732
  5.6 9.1 %collective-permute-start.2 = (bf16[8,4096]{1,0:T(8,128)(2,1)}, bf16[8,4096]{1,0:T(8,128)(2,1)S(1)}, u32[]{:S(2)}, u32[]{:S(2)}) collective-permute-start(bf16[8,4096]{1,0:T(8,128)(2,1)} %get-tuple-element.22), channel_id=1, source_target_pairs={{3,7},{7,11},{11,15},{15,19},{19,23},{23,27},{27,31},{1,1},{5,5},{... | collective-permute-start | bytes 196616 | tf_op jit(solution)/shard_map/ppermute | solution.py:610
  6.2 8.5 %collective-permute-start.1 = (bf16[8,4096]{1,0:T(8,128)(2,1)}, bf16[8,4096]{1,0:T(8,128)(2,1)S(1)}, u32[]{:S(2)}, u32[]{:S(2)}) collective-permute-start(bf16[8,4096]{1,0:T(8,128)(2,1)} %get-tuple-element.22), channel_id=1, source_target_pairs={{3,6},{7,10},{11,14},{15,18},{19,22},{23,26},{27,30},{1,0},{5,4},{... | collective-permute-start | bytes 196616 | tf_op jit(solution)/shard_map/ppermute | solution.py:610
  14.7 28.9 %all-to-all-start = ((bf16[8,384,128]{2,1,0:T(8,128)(2,1)}), bf16[8,384,128]{2,1,0:T(8,128)(2,1)S(1)}, u32[]{:S(2)}, u32[]{:S(2)}) async-start(bf16[8,384,128]{2,1,0:T(8,128)(2,1)} %get-tuple-element.23), calls=%async_computation | async-start | bytes 1572864 | tf_op jit(solution)/shard_map/all_to_all | solution.py:623
  21.9 9.0 %collective-permute-start.5 = (bf16[8,4096]{1,0:T(8,128)(2,1)S(1)}, bf16[8,4096]{1,0:T(8,128)(2,1)S(1)}, u32[]{:S(2)}, u32[]{:S(2)}) collective-permute-start(bf16[8,4096]{1,0:T(8,128)(2,1)S(1)} %add.12), channel_id=1, source_target_pairs={{0,2},{1,3},{2,0},{3,1},{4,6},{5,7},{6,4},{7,5},{8,10},{9,11},{10,... | collective-permute-start | bytes 196616 | tf_op jit(solution)/shard_map/ppermute | solution.py:590
  29.8 2.7 %copy-start.2 = (bf16[128,4096]{1,0:T(8,128)(2,1)}, bf16[128,4096]{1,0:T(8,128)(2,1)S(1)}, u32[]{:S(2)}) copy-start(bf16[128,4096]{1,0:T(8,128)(2,1)S(1)} %collective-permute-done.3.refs_0_.refs_2_) | copy-start | bytes 3145732
  29.8 2.7 %collective-permute-start.4 = (bf16[128,4096]{1,0:T(8,128)(2,1)S(1)}, bf16[128,4096]{1,0:T(8,128)(2,1)S(1)}, u32[]{:S(2)}, u32[]{:S(2)}) collective-permute-start(bf16[128,4096]{1,0:T(8,128)(2,1)S(1)} %collective-permute-done.3.refs_0_.refs_2_), channel_id=1, source_target_pairs={{0,1},{1,0},{2,3},{3,2},{4,5},{5,4},{6,7},{7,6},{8,9},{9,8},{10,11... | collective-permute-start | bytes 3145736 | tf_op jit(solution)/shard_map/ppermute | solution.py:590
  31.9 0.8 copy-start.4
  32.7 1.0 %copy-start.3 = (bf16[128,4096]{1,0:T(8,128)(2,1)}, bf16[128,4096]{1,0:T(8,128)(2,1)S(1)}, u32[]{:S(2)}) copy-start(bf16[128,4096]{1,0:T(8,128)(2,1)S(1)} %collective-permute-done.4.refs_1_.refs_3_) | copy-start | bytes 3145732
  43.6 3.4 %copy-start = (bf16[8,384,128]{2,1,0:T(8,128)(2,1)}, bf16[8,384,128]{2,1,0:T(8,128)(2,1)S(1)}, u32[]{:S(2)}) copy-start(bf16[8,384,128]{2,1,0:T(8,128)(2,1)S(1)} %all-to-all-done.x_any.early_any) | copy-start | bytes 2359300
  43.6 13.0 %all-to-all-start.1 = ((bf16[8,136,128]{2,1,0:T(8,128)(2,1)}), bf16[8,136,128]{2,1,0:T(8,128)(2,1)S(1)}, u32[]{:S(2)}, u32[]{:S(2)}) async-start(bf16[8,136,128]{2,1,0:T(8,128)(2,1)} %get-tuple-element.26), calls=%async_computation.1 | async-start | bytes 557056 | tf_op jit(solution)/shard_map/all_to_all | solution.py:633
  56.6 0.7 copy-start.5
  63.2 18.1 %all-to-all-start.2 = ((bf16[8,256,128]{2,1,0:T(8,128)(2,1)}), bf16[8,256,128]{2,1,0:T(8,128)(2,1)S(1)}, u32[]{:S(2)}, u32[]{:S(2)}) async-start(bf16[8,256,128]{2,1,0:T(8,128)(2,1)} %convolve.1), calls=%async_computation.2 | async-start | bytes 1048576 | tf_op jit(solution)/shard_map/all_to_all | solution.py:635

commit v8 on v6

--- a/solution.py
+++ b/solution.py
@@ -500,11 +500,13 @@
     total = tap_ref[0, 0:1] * rows_ref[PAD:]
     for lag in (1, 2):
         total += tap_ref[lag, 0:1] * rows_ref[PAD - lag : PAD - lag + length]
-    out_ref[0] = total
+    out_ref[0] = total.astype(bf16)
+    rows_ref[PAD:] = total
     early_ref[:PAD] = late_ref[half:]
     for at, g_ref in ((early_at, early_ref), (1 - early_at, late_ref)):
         rows = pl.ds(pl.multiple_of(at * half, half), half)
-        out_ref[1, rows, :] = out_ref[0, rows, :] * (skip_ref[...] * g_ref[:half])
+        query = rows_ref[pl.ds(pl.multiple_of(PAD + at * half, 16), half), :]
+        out_ref[1, rows, :] = (query * (skip_ref[...] * g_ref[:half])).astype(bf16)
     start_all([(out_ref, out_any, out_sem)])[0].wait()
 
 
@@ -516,7 +518,7 @@
         functools.partial(query_kernel, len(blocks)),
         in_specs=[pl.BlockSpec(memory_space=pltpu.SMEM)] + [ANY_SPEC] * (len(blocks) + 6),
         out_specs=ANY_SPEC,
-        out_shape=jax.ShapeDtypeStruct((2, length, channels), f32),
+        out_shape=jax.ShapeDtypeStruct((2, length, channels), bf16),
         scratch_shapes=[
             pltpu.VMEM((PAD + length, width), bf16),
             pltpu.VMEM((width, channels), bf16),
@@ -525,7 +527,7 @@
             pltpu.VMEM(late.shape, f32),
             pltpu.VMEM(skip.shape, f32),
             pltpu.VMEM((PAD + length, channels), f32),
-            pltpu.VMEM((2, length, channels), f32),
+            pltpu.VMEM((2, length, channels), bf16),
             pltpu.SemaphoreType.DMA((len(blocks) + 6,)),
             pltpu.SemaphoreType.DMA,
         ],
@@ -548,7 +550,7 @@
             loads[i].wait()
             for j, part in enumerate((top, bot)):
                 rows = slice(j * FINE, (j + 1) * FINE)
-                out_ref[i, rows] = (term_ref[i, 0, rows] * part + term_ref[i, 1, rows]).astype(bf16)
+                out_ref[i, rows] = (term_ref[i, 0, rows].astype(f32) * part + term_ref[i, 1, rows].astype(f32)).astype(bf16)
             sends += start_all([(out_ref.at[i], out_any.at[:, cols[i]], sem.at[i])])
         for send in sends:
             send.wait()
@@ -559,7 +561,7 @@
         out_specs=ANY_SPEC,
         out_shape=jax.ShapeDtypeStruct((length, channels), bf16),
         scratch_shapes=[
-            pltpu.VMEM((tiles, 2, length, LANES), f32),
+            pltpu.VMEM((tiles, 2, length, LANES), bf16),
             pltpu.VMEM((tiles, length, LANES), bf16),
             pltpu.SemaphoreType.DMA((tiles,)),
             pltpu.SemaphoreType.DMA((tiles,)),
@@ -647,7 +649,7 @@
     each = channels // dev_count
     conv = conv.reshape(dev_count, FINE, 2, HALF)[..., :each]
     conv = jnp.transpose(conv, (2, 1, 0, 3)).reshape(2 * FINE, channels).astype(f32)
-    return (terms[0] * conv + terms[1]).astype(bf16)
+    return (terms[0].astype(f32) * conv + terms[1].astype(f32)).astype(bf16)
 
 
 def solution(mesh):

time: 84.2 us -> 83.9 us (level)
  no operation moved by 1% of the time
where the time goes in v8:
time: 83.9 us; the launch traced here: 83.4 us
  Pallas kernels  37.7 us (45%)
  waiting for transfers between devices  21.2 us (25%)
  starting transfers between devices  20.7 us (25%)
  local copies, waits for them, and re-layouts  2.06 us (2%)
  other arithmetic  1.63 us (2%)
    pallas_call x2, Pallas kernels, project(): pl.pallas_call(functools.partial(project_kernel, len(blocks), parts, spli...  14.2 us
    pallas_call x1, Pallas kernels, query_terms(): pl.pallas_call(functools.partial(query_kernel, len(blocks)), in_specs=[pl...  8.34 us
    ppermute x4, waiting for transfers between devices, swap(): lax.ppermute(x, 'tensor', [(i, i ^ bit) for i in range(tensor_count)])  8 us
    all_to_all x1, starting transfers between devices, local(): early_sent = exchange(packs)  7.14 us
    pallas_call x1, Pallas kernels, convolve(): pl.pallas_call(functools.partial(conv_kernel, dev_count), in_specs=[pl.Bl...  5.85 us
    all_to_all x1, waiting for transfers between devices, local(): conv = exchange(convolve(half, early_sent, late_sent, spectrum, consts))  5.56 us
    pallas_call x1, Pallas kernels, filter_spectrum(): pl.pallas_call(functools.partial(filter_kernel, dev_count), in_specs=[ANY...  4.79 us
    all_to_all x1, waiting for transfers between devices, local(): late_sent = exchange(packs)  4.75 us
  transfers between devices with their start and end apart: 9, of which 6 were waited for; matrix products, arithmetic and copies ran while one was open for 2% of the time, Pallas kernels for 33%

profile of v8, /device:TPU:0, one launch (start us, length us, event | category | flops | bytes accessed | tf_op | source)
XLA Modules:
  0.0 83.4 jit_solution(2891799132520491498)
XLA Ops:
  0.0 2.5 %norm_rows.1 = (bf16[128,4096]{1,0:T(8,128)(2,1)}, bf16[8,4096]{1,0:T(8,128)(2,1)}) custom-call(bf16[128,4096]{1,0:T(8,128)(2,1)} %tok_hbm.1, f32[1,4096]{1,0:T(1,128)} %bitcast.11), custom_call_target="tpu_custom_call" | custom-call | tf_op jit(solution)/shard_map/norm_rows/pallas_call | solution.py:91
  2.5 0.5 collective-permute-start
  3.0 2.6 %collective-permute-start.3 = (bf16[128,4096]{1,0:T(8,128)(2,1)}, bf16[128,4096]{1,0:T(8,128)(2,1)S(1)}, u32[]{:S(2)}, u32[]{:S(2)}) collective-permute-start(bf16[128,4096]{1,0:T(8,128)(2,1)} %get-tuple-element.19.refs_0_), channel_id=1, source_target_pairs={{0,2},{1,3},{2,0},{3,1},{4,6},{5,7},{6,4},{7,5},{8,10},{9,11},{10,... | collective-permute-start | bytes 3145736 | tf_op jit(solution)/shard_map/ppermute | solution.py:591
  5.6 0.0 collective-permute-done.refs_1_
  5.6 0.0 copy-start.1
  5.6 0.7 collective-permute-start.2
  6.2 1.3 %collective-permute-start.1 = (bf16[8,4096]{1,0:T(8,128)(2,1)}, bf16[8,4096]{1,0:T(8,128)(2,1)S(1)}, u32[]{:S(2)}, u32[]{:S(2)}) collective-permute-start(bf16[8,4096]{1,0:T(8,128)(2,1)} %get-tuple-element.22), channel_id=1, source_target_pairs={{3,6},{7,10},{11,14},{15,18},{19,22},{23,26},{27,30},{1,0},{5,4},{... | collective-permute-start | bytes 196616 | tf_op jit(solution)/shard_map/ppermute | solution.py:611
  7.5 0.0 copy-done.1
  7.6 7.1 %project.2 = (f32[256,512]{1,0:T(8,128)}, bf16[8,384,128]{2,1,0:T(8,128)(2,1)}) custom-call(s32[1]{0:T(128)} %bitcast.1.me_ref, bf16[128,4096]{1,0:T(8,128)(2,1)} %get-tuple-element.19.refs_0_, bf16[128,4096]{1,0:T(8,128)(2,1)} %copy-done.1, bf16[3,4096,512]{2,1,0:T(8,128)(2,1)} %bitcast.8, f32[3,3,512]{2,1,0:T(4,128)} %refs_6_.1, f32[512,512]{1,0:T(8,128)} %refs_4_.1), custom_call_target="tpu_custom_call" | custom-call | flops 100000000 | bytes 100000 | tf_op jit(solution)/shard_map/project/pallas_call | solution.py:211
  14.7 0.0 collective-permute-done.2
  14.7 0.0 collective-permute-done.1
  14.7 7.1 %all-to-all-start = ((bf16[8,384,128]{2,1,0:T(8,128)(2,1)}), bf16[8,384,128]{2,1,0:T(8,128)(2,1)S(1)}, u32[]{:S(2)}, u32[]{:S(2)}) async-start(bf16[8,384,128]{2,1,0:T(8,128)(2,1)} %get-tuple-element.23), calls=%async_computation | async-start | bytes 1572864 | tf_op jit(solution)/shard_map/all_to_all | solution.py:624
  21.9 1.5 %collective-permute-start.5 = (bf16[8,4096]{1,0:T(8,128)(2,1)S(1)}, bf16[8,4096]{1,0:T(8,128)(2,1)S(1)}, u32[]{:S(2)}, u32[]{:S(2)}) collective-permute-start(bf16[8,4096]{1,0:T(8,128)(2,1)S(1)} %add.12), channel_id=1, source_target_pairs={{0,2},{1,3},{2,0},{3,1},{4,6},{5,7},{6,4},{7,5},{8,10},{9,11},{10,... | collective-permute-start | bytes 196616 | tf_op jit(solution)/shard_map/ppermute | solution.py:591
  23.4 6.4 %collective-permute-done.3.refs_0_.refs_2_ = bf16[128,4096]{1,0:T(8,128)(2,1)S(1)} collective-permute-done((bf16[128,4096]{1,0:T(8,128)(2,1)}, bf16[128,4096]{1,0:T(8,128)(2,1)S(1)}, u32[]{:S(2)}, u32[]{:S(2)}) %collective-permute-start.3) | collective-permute-done | bytes 1048608 | tf_op jit(solution)/shard_map/ppermute | solution.py:591
  29.8 0.0 copy-start.2
  29.8 0.0 collective-permute-start.4
  29.8 1.1 %collective-permute-done.5 = bf16[8,4096]{1,0:T(8,128)(2,1)S(1)} collective-permute-done((bf16[8,4096]{1,0:T(8,128)(2,1)S(1)}, bf16[8,4096]{1,0:T(8,128)(2,1)S(1)}, u32[]{:S(2)}, u32[]{:S(2)}) %collective-permute-start.5) | collective-permute-done | bytes 65568 | tf_op jit(solution)/shard_map/ppermute | solution.py:591
  30.9 1.0 %add_dynamic-update-slice_fusion.refs_4_ = bf16[48,4096]{1,0:T(8,128)(2,1)S(1)} fusion(bf16[48,4096]{1,0:T(8,128)(2,1)S(1)} %constant_dynamic-update-slice_fusion, bf16[128,4096]{1,0:T(8,128)(2,1)} %copy-done.1, bf16[128,4096]{1,0:T(8,128)(2,1)} %get-tuple-element.19.refs_0_, pred[]{:T(512)} %bitcast.5, pred[]{:T(512)} %bitcast.4), kind=kLoop, calls=%fused_computation | loop fusion | flops 393216 | bytes 393218 | tf_op jit(solution)/shard_map/concatenate | solution.py:628
  31.9 0.0 copy-start.4
  32.0 0.5 collective-permute-done.4.refs_1_.refs_3_
  32.4 0.0 copy-done.2
  32.4 0.3 copy-done.4
  32.7 0.0 copy-start.3
  32.7 1.0 %copy-done.3 = bf16[128,4096]{1,0:T(8,128)(2,1)} copy-done((bf16[128,4096]{1,0:T(8,128)(2,1)}, bf16[128,4096]{1,0:T(8,128)(2,1)S(1)}, u32[]{:S(2)}) %copy-start.3) | copy-done | bytes 1048600
  33.7 7.1 %project.3 = (f32[272,512]{1,0:T(8,128)}, bf16[8,136,128]{2,1,0:T(8,128)(2,1)}) custom-call(s32[1]{0:T(128)} %bitcast.1.me_ref, bf16[128,4096]{1,0:T(8,128)(2,1)} %copy-done.2, bf16[128,4096]{1,0:T(8,128)(2,1)} %copy-done.3, bf16[3,4096,512]{2,1,0:T(8,128)(2,1)} %bitcast.9, f32[3,3,512]{2,1,0:T(4,128)} %refs_6_.1, bf16[48,4096]{1,0:T(8,128)(2,1)} %copy-done.4), custom_call_target="tpu_custom_call" | custom-call | flops 100000000 | bytes 100000 | tf_op jit(solution)/shard_map/project/pallas_call | solution.py:211
  40.8 2.8 %all-to-all-done.x_any.early_any = bf16[8,384,128]{2,1,0:T(8,128)(2,1)S(1)} async-done(((bf16[8,384,128]{2,1,0:T(8,128)(2,1)}), bf16[8,384,128]{2,1,0:T(8,128)(2,1)S(1)}, u32[]{:S(2)}, u32[]{:S(2)}) %all-to-all-start) | async-done | bytes 786464 | tf_op jit(solution)/shard_map/all_to_all | solution.py:624
  43.6 0.0 copy-start
  43.6 3.4 %all-to-all-start.1 = ((bf16[8,136,128]{2,1,0:T(8,128)(2,1)}), bf16[8,136,128]{2,1,0:T(8,128)(2,1)S(1)}, u32[]{:S(2)}, u32[]{:S(2)}) async-start(bf16[8,136,128]{2,1,0:T(8,128)(2,1)} %get-tuple-element.26), calls=%async_computation.1 | async-start | bytes 557056 | tf_op jit(solution)/shard_map/all_to_all | solution.py:634
  47.1 0.0 copy-done
  47.1 4.8 %filter_spectrum.1.h_hbm = f32[9,256,256]{2,1,0:T(8,128)} custom-call(bf16[8,384,128]{2,1,0:T(8,128)(2,1)} %copy-done, f32[256,256]{1,0:T(8,128)} %constant.44.clone.refs_0_, f32[256,256]{1,0:T(8,128)} %constant.45.clone.refs_1_, f32[9,2,128]{2,1,0:T(2,128)} %constant.46.clone.refs_2_, bf16[512,256]{1,0:T(8,128)(2,1)} %constant.47.clone.refs_3_), custom_call_target="tpu_custom_call" | custom-call | tf_op jit(solution)/shard_map/filter_spectrum/pallas_call | solution.py:443
  51.9 4.7 %all-to-all-done.1.late_any = bf16[8,136,128]{2,1,0:T(8,128)(2,1)S(1)} async-done(((bf16[8,136,128]{2,1,0:T(8,128)(2,1)}), bf16[8,136,128]{2,1,0:T(8,128)(2,1)S(1)}, u32[]{:S(2)}, u32[]{:S(2)}) %all-to-all-start.1) | async-done | bytes 278560 | tf_op jit(solution)/shard_map/all_to_all | solution.py:634
  56.6 0.0 copy-start.5
  56.6 0.7 copy-done.5
  57.4 5.8 %convolve.1 = bf16[8,256,128]{2,1,0:T(8,128)(2,1)} custom-call(s32[1]{0:T(128)} %bitcast.half_ref, bf16[8,384,128]{2,1,0:T(8,128)(2,1)} %copy-done, bf16[8,136,128]{2,1,0:T(8,128)(2,1)} %copy-done.5, f32[9,256,256]{2,1,0:T(8,128)} %filter_spectrum.1.h_hbm, f32[256,256]{1,0:T(8,128)} %constant.44.clone.refs_0_, f32[256,256]{1,0:T(8,128)} %constant.45.clone.refs_1_, ...), custom_call_target="tpu_custom_call" | custom-call | tf_op jit(solution)/shard_map/convolve/pallas_call | solution.py:458
  63.2 3.6 %all-to-all-start.2 = ((bf16[8,256,128]{2,1,0:T(8,128)(2,1)}), bf16[8,256,128]{2,1,0:T(8,128)(2,1)S(1)}, u32[]{:S(2)}, u32[]{:S(2)}) async-start(bf16[8,256,128]{2,1,0:T(8,128)(2,1)} %convolve.1), calls=%async_computation.2 | async-start | bytes 1048576 | tf_op jit(solution)/shard_map/all_to_all | solution.py:636
  66.8 0.6 pad_add_fusion.me_ref
  67.4 8.3 %query_terms.1.term_any = bf16[2,512,512]{2,1,0:T(8,128)(2,1)} custom-call(s32[2]{0:T(128)} %pad_add_fusion.me_ref, bf16[128,4096]{1,0:T(8,128)(2,1)} %get-tuple-element.19.refs_0_, bf16[128,4096]{1,0:T(8,128)(2,1)} %copy-done.1, bf16[128,4096]{1,0:T(8,128)(2,1)} %copy-done.2, bf16[128,4096]{1,0:T(8,128)(2,1)} %copy-done.3, bf16[48,4096]{1,0:T(8,128)(2,1)} %copy-done.4, ...), custom_call_target="tpu_custom_call" | custom-call | flops 100000000 | bytes 100000 | tf_op jit(solution)/shard_map/query_terms/pallas_call | solution.py:517
  75.8 5.6 %all-to-all-done.2.c_ref = bf16[8,256,128]{2,1,0:T(8,128)(2,1)S(1)} async-done(((bf16[8,256,128]{2,1,0:T(8,128)(2,1)}), bf16[8,256,128]{2,1,0:T(8,128)(2,1)S(1)}, u32[]{:S(2)}, u32[]{:S(2)}) %all-to-all-start.2) | async-done | bytes 524320 | tf_op jit(solution)/shard_map/all_to_all | solution.py:636
  81.4 2.0 %finish.1 = bf16[512,512]{1,0:T(8,128)(2,1)} custom-call(bf16[8,256,128]{2,1,0:T(8,128)(2,1)S(1)} %all-to-all-done.2.c_ref, bf16[2,512,512]{2,1,0:T(8,128)(2,1)} %query_terms.1.term_any), custom_call_target="tpu_custom_call" | custom-call | tf_op jit(solution)/shard_map/finish/pallas_call | solution.py:558
  (5 shorter events, 0.0 us)
Async XLA Ops:
  2.5 3.1 %collective-permute-start = (bf16[128,4096]{1,0:T(8,128)(2,1)}, bf16[128,4096]{1,0:T(8,128)(2,1)S(1)}, u32[]{:S(2)}, u32[]{:S(2)}) collective-permute-start(bf16[128,4096]{1,0:T(8,128)(2,1)} %get-tuple-element.19.refs_0_), channel_id=1, source_target_pairs={{0,1},{1,0},{2,3},{3,2},{4,5},{5,4},{6,7},{7,6},{8,9},{9,8},{10,11... | collective-permute-start | bytes 3145736 | tf_op jit(solution)/shard_map/ppermute | solution.py:591
  3.0 26.8 %collective-permute-start.3 = (bf16[128,4096]{1,0:T(8,128)(2,1)}, bf16[128,4096]{1,0:T(8,128)(2,1)S(1)}, u32[]{:S(2)}, u32[]{:S(2)}) collective-permute-start(bf16[128,4096]{1,0:T(8,128)(2,1)} %get-tuple-element.19.refs_0_), channel_id=1, source_target_pairs={{0,2},{1,3},{2,0},{3,1},{4,6},{5,7},{6,4},{7,5},{8,10},{9,11},{10,... | collective-permute-start | bytes 3145736 | tf_op jit(solution)/shard_map/ppermute | solution.py:591
  5.6 2.0 %copy-start.1 = (bf16[128,4096]{1,0:T(8,128)(2,1)}, bf16[128,4096]{1,0:T(8,128)(2,1)S(1)}, u32[]{:S(2)}) copy-start(bf16[128,4096]{1,0:T(8,128)(2,1)S(1)} %collective-permute-done.refs_1_) | copy-start | bytes 3145732
  5.6 9.1 %collective-permute-start.2 = (bf16[8,4096]{1,0:T(8,128)(2,1)}, bf16[8,4096]{1,0:T(8,128)(2,1)S(1)}, u32[]{:S(2)}, u32[]{:S(2)}) collective-permute-start(bf16[8,4096]{1,0:T(8,128)(2,1)} %get-tuple-element.22), channel_id=1, source_target_pairs={{3,7},{7,11},{11,15},{15,19},{19,23},{23,27},{27,31},{1,1},{5,5},{... | collective-permute-start | bytes 196616 | tf_op jit(solution)/shard_map/ppermute | solution.py:611
  6.2 8.5 %collective-permute-start.1 = (bf16[8,4096]{1,0:T(8,128)(2,1)}, bf16[8,4096]{1,0:T(8,128)(2,1)S(1)}, u32[]{:S(2)}, u32[]{:S(2)}) collective-permute-start(bf16[8,4096]{1,0:T(8,128)(2,1)} %get-tuple-element.22), channel_id=1, source_target_pairs={{3,6},{7,10},{11,14},{15,18},{19,22},{23,26},{27,30},{1,0},{5,4},{... | collective-permute-start | bytes 196616 | tf_op jit(solution)/shard_map/ppermute | solution.py:611
  14.7 28.9 %all-to-all-start = ((bf16[8,384,128]{2,1,0:T(8,128)(2,1)}), bf16[8,384,128]{2,1,0:T(8,128)(2,1)S(1)}, u32[]{:S(2)}, u32[]{:S(2)}) async-start(bf16[8,384,128]{2,1,0:T(8,128)(2,1)} %get-tuple-element.23), calls=%async_computation | async-start | bytes 1572864 | tf_op jit(solution)/shard_map/all_to_all | solution.py:624
  21.9 9.0 %collective-permute-start.5 = (bf16[8,4096]{1,0:T(8,128)(2,1)S(1)}, bf16[8,4096]{1,0:T(8,128)(2,1)S(1)}, u32[]{:S(2)}, u32[]{:S(2)}) collective-permute-start(bf16[8,4096]{1,0:T(8,128)(2,1)S(1)} %add.12), channel_id=1, source_target_pairs={{0,2},{1,3},{2,0},{3,1},{4,6},{5,7},{6,4},{7,5},{8,10},{9,11},{10,... | collective-permute-start | bytes 196616 | tf_op jit(solution)/shard_map/ppermute | solution.py:591
  29.8 2.7 %copy-start.2 = (bf16[128,4096]{1,0:T(8,128)(2,1)}, bf16[128,4096]{1,0:T(8,128)(2,1)S(1)}, u32[]{:S(2)}) copy-start(bf16[128,4096]{1,0:T(8,128)(2,1)S(1)} %collective-permute-done.3.refs_0_.refs_2_) | copy-start | bytes 3145732
  29.8 2.7 %collective-permute-start.4 = (bf16[128,4096]{1,0:T(8,128)(2,1)S(1)}, bf16[128,4096]{1,0:T(8,128)(2,1)S(1)}, u32[]{:S(2)}, u32[]{:S(2)}) collective-permute-start(bf16[128,4096]{1,0:T(8,128)(2,1)S(1)} %collective-permute-done.3.refs_0_.refs_2_), channel_id=1, source_target_pairs={{0,1},{1,0},{2,3},{3,2},{4,5},{5,4},{6,7},{7,6},{8,9},{9,8},{10,11... | collective-permute-start | bytes 3145736 | tf_op jit(solution)/shard_map/ppermute | solution.py:591
  31.9 0.8 copy-start.4
  32.7 1.0 %copy-start.3 = (bf16[128,4096]{1,0:T(8,128)(2,1)}, bf16[128,4096]{1,0:T(8,128)(2,1)S(1)}, u32[]{:S(2)}) copy-start(bf16[128,4096]{1,0:T(8,128)(2,1)S(1)} %collective-permute-done.4.refs_1_.refs_3_) | copy-start | bytes 3145732
  43.6 3.4 %copy-start = (bf16[8,384,128]{2,1,0:T(8,128)(2,1)}, bf16[8,384,128]{2,1,0:T(8,128)(2,1)S(1)}, u32[]{:S(2)}) copy-start(bf16[8,384,128]{2,1,0:T(8,128)(2,1)S(1)} %all-to-all-done.x_any.early_any) | copy-start | bytes 2359300
  43.6 13.0 %all-to-all-start.1 = ((bf16[8,136,128]{2,1,0:T(8,128)(2,1)}), bf16[8,136,128]{2,1,0:T(8,128)(2,1)S(1)}, u32[]{:S(2)}, u32[]{:S(2)}) async-start(bf16[8,136,128]{2,1,0:T(8,128)(2,1)} %get-tuple-element.26), calls=%async_computation.1 | async-start | bytes 557056 | tf_op jit(solution)/shard_map/all_to_all | solution.py:634
  56.6 0.7 copy-start.5
  63.2 18.1 %all-to-all-start.2 = ((bf16[8,256,128]{2,1,0:T(8,128)(2,1)}), bf16[8,256,128]{2,1,0:T(8,128)(2,1)S(1)}, u32[]{:S(2)}, u32[]{:S(2)}) async-start(bf16[8,256,128]{2,1,0:T(8,128)(2,1)} %convolve.1), calls=%async_computation.2 | async-start | bytes 1048576 | tf_op jit(solution)/shard_map/all_to_all | solution.py:636

commit v9 on v8

--- a/solution.py
+++ b/solution.py
@@ -68,7 +68,7 @@
 
 def norm_rows(tokens, gain):
     rows, width = tokens.shape
-    step = min(32, rows)
+    step = min(64, rows)
 
     def kernel(tok_hbm, gain_hbm, out_any, tail_any, tok_ref, gain_ref, out_ref, sem, out_sem):
         parts = [pl.ds(i * step, step) for i in range(rows // step)]

time: 83.9 us -> 83.9 us (level)
  no operation moved by 1% of the time
where the time goes in v9:
time: 83.9 us; the launch traced here: 83.4 us
  Pallas kernels  37.7 us (45%)
  waiting for transfers between devices  21.2 us (25%)
  starting transfers between devices  20.7 us (25%)
  local copies, waits for them, and re-layouts  2.06 us (2%)
  other arithmetic  1.63 us (2%)
    pallas_call x2, Pallas kernels, project(): pl.pallas_call(functools.partial(project_kernel, len(blocks), parts, spli...  14.2 us
    pallas_call x1, Pallas kernels, query_terms(): pl.pallas_call(functools.partial(query_kernel, len(blocks)), in_specs=[pl...  8.34 us
    ppermute x4, waiting for transfers between devices, swap(): lax.ppermute(x, 'tensor', [(i, i ^ bit) for i in range(tensor_count)])  8 us
    all_to_all x1, starting transfers between devices, local(): early_sent = exchange(packs)  7.14 us
    pallas_call x1, Pallas kernels, convolve(): pl.pallas_call(functools.partial(conv_kernel, dev_count), in_specs=[pl.Bl...  5.85 us
    all_to_all x1, waiting for transfers between devices, local(): conv = exchange(convolve(half, early_sent, late_sent, spectrum, consts))  5.57 us
    pallas_call x1, Pallas kernels, filter_spectrum(): pl.pallas_call(functools.partial(filter_kernel, dev_count), in_specs=[ANY...  4.79 us
    all_to_all x1, waiting for transfers between devices, local(): late_sent = exchange(packs)  4.75 us
  transfers between devices with their start and end apart: 9, of which 6 were waited for; matrix products, arithmetic and copies ran while one was open for 2% of the time, Pallas kernels for 33%

profile of v9, /device:TPU:0, one launch (start us, length us, event | category | flops | bytes accessed | tf_op | source)
XLA Modules:
  0.0 83.4 jit_solution(11001157123153442280)
XLA Ops:
  0.0 2.5 %norm_rows.1 = (bf16[128,4096]{1,0:T(8,128)(2,1)}, bf16[8,4096]{1,0:T(8,128)(2,1)}) custom-call(bf16[128,4096]{1,0:T(8,128)(2,1)} %tok_hbm.1, f32[1,4096]{1,0:T(1,128)} %bitcast.11), custom_call_target="tpu_custom_call" | custom-call | tf_op jit(solution)/shard_map/norm_rows/pallas_call | solution.py:91
  2.5 0.5 collective-permute-start
  3.0 2.6 %collective-permute-start.3 = (bf16[128,4096]{1,0:T(8,128)(2,1)}, bf16[128,4096]{1,0:T(8,128)(2,1)S(1)}, u32[]{:S(2)}, u32[]{:S(2)}) collective-permute-start(bf16[128,4096]{1,0:T(8,128)(2,1)} %get-tuple-element.19.refs_0_), channel_id=1, source_target_pairs={{0,2},{1,3},{2,0},{3,1},{4,6},{5,7},{6,4},{7,5},{8,10},{9,11},{10,... | collective-permute-start | bytes 3145736 | tf_op jit(solution)/shard_map/ppermute | solution.py:591
  5.6 0.0 collective-permute-done.refs_1_
  5.6 0.0 copy-start.1
  5.6 0.7 collective-permute-start.2
  6.2 1.3 %collective-permute-start.1 = (bf16[8,4096]{1,0:T(8,128)(2,1)}, bf16[8,4096]{1,0:T(8,128)(2,1)S(1)}, u32[]{:S(2)}, u32[]{:S(2)}) collective-permute-start(bf16[8,4096]{1,0:T(8,128)(2,1)} %get-tuple-element.22), channel_id=1, source_target_pairs={{3,6},{7,10},{11,14},{15,18},{19,22},{23,26},{27,30},{1,0},{5,4},{... | collective-permute-start | bytes 196616 | tf_op jit(solution)/shard_map/ppermute | solution.py:611
  7.6 0.0 copy-done.1
  7.6 7.1 %project.2 = (f32[256,512]{1,0:T(8,128)}, bf16[8,384,128]{2,1,0:T(8,128)(2,1)}) custom-call(s32[1]{0:T(128)} %bitcast.1.me_ref, bf16[128,4096]{1,0:T(8,128)(2,1)} %get-tuple-element.19.refs_0_, bf16[128,4096]{1,0:T(8,128)(2,1)} %copy-done.1, bf16[3,4096,512]{2,1,0:T(8,128)(2,1)} %bitcast.8, f32[3,3,512]{2,1,0:T(4,128)} %refs_6_.1, f32[512,512]{1,0:T(8,128)} %refs_4_.1), custom_call_target="tpu_custom_call" | custom-call | flops 100000000 | bytes 100000 | tf_op jit(solution)/shard_map/project/pallas_call | solution.py:211
  14.7 0.0 collective-permute-done.2
  14.7 0.0 collective-permute-done.1
  14.7 7.1 %all-to-all-start = ((bf16[8,384,128]{2,1,0:T(8,128)(2,1)}), bf16[8,384,128]{2,1,0:T(8,128)(2,1)S(1)}, u32[]{:S(2)}, u32[]{:S(2)}) async-start(bf16[8,384,128]{2,1,0:T(8,128)(2,1)} %get-tuple-element.23), calls=%async_computation | async-start | bytes 1572864 | tf_op jit(solution)/shard_map/all_to_all | solution.py:624
  21.9 1.5 %collective-permute-start.5 = (bf16[8,4096]{1,0:T(8,128)(2,1)S(1)}, bf16[8,4096]{1,0:T(8,128)(2,1)S(1)}, u32[]{:S(2)}, u32[]{:S(2)}) collective-permute-start(bf16[8,4096]{1,0:T(8,128)(2,1)S(1)} %add.12), channel_id=1, source_target_pairs={{0,2},{1,3},{2,0},{3,1},{4,6},{5,7},{6,4},{7,5},{8,10},{9,11},{10,... | collective-permute-start | bytes 196616 | tf_op jit(solution)/shard_map/ppermute | solution.py:591
  23.4 6.4 %collective-permute-done.3.refs_0_.refs_2_ = bf16[128,4096]{1,0:T(8,128)(2,1)S(1)} collective-permute-done((bf16[128,4096]{1,0:T(8,128)(2,1)}, bf16[128,4096]{1,0:T(8,128)(2,1)S(1)}, u32[]{:S(2)}, u32[]{:S(2)}) %collective-permute-start.3) | collective-permute-done | bytes 1048608 | tf_op jit(solution)/shard_map/ppermute | solution.py:591
  29.8 0.0 copy-start.2
  29.8 0.0 collective-permute-start.4
  29.8 1.1 %collective-permute-done.5 = bf16[8,4096]{1,0:T(8,128)(2,1)S(1)} collective-permute-done((bf16[8,4096]{1,0:T(8,128)(2,1)S(1)}, bf16[8,4096]{1,0:T(8,128)(2,1)S(1)}, u32[]{:S(2)}, u32[]{:S(2)}) %collective-permute-start.5) | collective-permute-done | bytes 65568 | tf_op jit(solution)/shard_map/ppermute | solution.py:591
  30.9 1.0 %add_dynamic-update-slice_fusion.refs_4_ = bf16[48,4096]{1,0:T(8,128)(2,1)S(1)} fusion(bf16[48,4096]{1,0:T(8,128)(2,1)S(1)} %constant_dynamic-update-slice_fusion, bf16[128,4096]{1,0:T(8,128)(2,1)} %copy-done.1, bf16[128,4096]{1,0:T(8,128)(2,1)} %get-tuple-element.19.refs_0_, pred[]{:T(512)} %bitcast.5, pred[]{:T(512)} %bitcast.4), kind=kLoop, calls=%fused_computation | loop fusion | flops 393216 | bytes 393218 | tf_op jit(solution)/shard_map/concatenate | solution.py:628
  31.9 0.0 copy-start.4
  32.0 0.5 collective-permute-done.4.refs_1_.refs_3_
  32.4 0.0 copy-done.2
  32.4 0.3 copy-done.4
  32.7 0.0 copy-start.3
  32.7 1.0 %copy-done.3 = bf16[128,4096]{1,0:T(8,128)(2,1)} copy-done((bf16[128,4096]{1,0:T(8,128)(2,1)}, bf16[128,4096]{1,0:T(8,128)(2,1)S(1)}, u32[]{:S(2)}) %copy-start.3) | copy-done | bytes 1048600
  33.7 7.1 %project.3 = (f32[272,512]{1,0:T(8,128)}, bf16[8,136,128]{2,1,0:T(8,128)(2,1)}) custom-call(s32[1]{0:T(128)} %bitcast.1.me_ref, bf16[128,4096]{1,0:T(8,128)(2,1)} %copy-done.2, bf16[128,4096]{1,0:T(8,128)(2,1)} %copy-done.3, bf16[3,4096,512]{2,1,0:T(8,128)(2,1)} %bitcast.9, f32[3,3,512]{2,1,0:T(4,128)} %refs_6_.1, bf16[48,4096]{1,0:T(8,128)(2,1)} %copy-done.4), custom_call_target="tpu_custom_call" | custom-call | flops 100000000 | bytes 100000 | tf_op jit(solution)/shard_map/project/pallas_call | solution.py:211
  40.8 2.8 %all-to-all-done.x_any.early_any = bf16[8,384,128]{2,1,0:T(8,128)(2,1)S(1)} async-done(((bf16[8,384,128]{2,1,0:T(8,128)(2,1)}), bf16[8,384,128]{2,1,0:T(8,128)(2,1)S(1)}, u32[]{:S(2)}, u32[]{:S(2)}) %all-to-all-start) | async-done | bytes 786464 | tf_op jit(solution)/shard_map/all_to_all | solution.py:624
  43.6 0.0 copy-start
  43.6 3.4 %all-to-all-start.1 = ((bf16[8,136,128]{2,1,0:T(8,128)(2,1)}), bf16[8,136,128]{2,1,0:T(8,128)(2,1)S(1)}, u32[]{:S(2)}, u32[]{:S(2)}) async-start(bf16[8,136,128]{2,1,0:T(8,128)(2,1)} %get-tuple-element.26), calls=%async_computation.1 | async-start | bytes 557056 | tf_op jit(solution)/shard_map/all_to_all | solution.py:634
  47.1 0.0 copy-done
  47.1 4.8 %filter_spectrum.1.h_hbm = f32[9,256,256]{2,1,0:T(8,128)} custom-call(bf16[8,384,128]{2,1,0:T(8,128)(2,1)} %copy-done, f32[256,256]{1,0:T(8,128)} %constant.44.clone.refs_0_, f32[256,256]{1,0:T(8,128)} %constant.45.clone.refs_1_, f32[9,2,128]{2,1,0:T(2,128)} %constant.46.clone.refs_2_, bf16[512,256]{1,0:T(8,128)(2,1)} %constant.47.clone.refs_3_), custom_call_target="tpu_custom_call" | custom-call | tf_op jit(solution)/shard_map/filter_spectrum/pallas_call | solution.py:443
  51.9 4.7 %all-to-all-done.1.late_any = bf16[8,136,128]{2,1,0:T(8,128)(2,1)S(1)} async-done(((bf16[8,136,128]{2,1,0:T(8,128)(2,1)}), bf16[8,136,128]{2,1,0:T(8,128)(2,1)S(1)}, u32[]{:S(2)}, u32[]{:S(2)}) %all-to-all-start.1) | async-done | bytes 278560 | tf_op jit(solution)/shard_map/all_to_all | solution.py:634
  56.6 0.0 copy-start.5
  56.6 0.7 copy-done.5
  57.4 5.8 %convolve.1 = bf16[8,256,128]{2,1,0:T(8,128)(2,1)} custom-call(s32[1]{0:T(128)} %bitcast.half_ref, bf16[8,384,128]{2,1,0:T(8,128)(2,1)} %copy-done, bf16[8,136,128]{2,1,0:T(8,128)(2,1)} %copy-done.5, f32[9,256,256]{2,1,0:T(8,128)} %filter_spectrum.1.h_hbm, f32[256,256]{1,0:T(8,128)} %constant.44.clone.refs_0_, f32[256,256]{1,0:T(8,128)} %constant.45.clone.refs_1_, ...), custom_call_target="tpu_custom_call" | custom-call | tf_op jit(solution)/shard_map/convolve/pallas_call | solution.py:458
  63.2 3.6 %all-to-all-start.2 = ((bf16[8,256,128]{2,1,0:T(8,128)(2,1)}), bf16[8,256,128]{2,1,0:T(8,128)(2,1)S(1)}, u32[]{:S(2)}, u32[]{:S(2)}) async-start(bf16[8,256,128]{2,1,0:T(8,128)(2,1)} %convolve.1), calls=%async_computation.2 | async-start | bytes 1048576 | tf_op jit(solution)/shard_map/all_to_all | solution.py:636
  66.8 0.6 pad_add_fusion.me_ref
  67.4 8.3 %query_terms.1.term_any = bf16[2,512,512]{2,1,0:T(8,128)(2,1)} custom-call(s32[2]{0:T(128)} %pad_add_fusion.me_ref, bf16[128,4096]{1,0:T(8,128)(2,1)} %get-tuple-element.19.refs_0_, bf16[128,4096]{1,0:T(8,128)(2,1)} %copy-done.1, bf16[128,4096]{1,0:T(8,128)(2,1)} %copy-done.2, bf16[128,4096]{1,0:T(8,128)(2,1)} %copy-done.3, bf16[48,4096]{1,0:T(8,128)(2,1)} %copy-done.4, ...), custom_call_target="tpu_custom_call" | custom-call | flops 100000000 | bytes 100000 | tf_op jit(solution)/shard_map/query_terms/pallas_call | solution.py:517
  75.8 5.6 %all-to-all-done.2.c_ref = bf16[8,256,128]{2,1,0:T(8,128)(2,1)S(1)} async-done(((bf16[8,256,128]{2,1,0:T(8,128)(2,1)}), bf16[8,256,128]{2,1,0:T(8,128)(2,1)S(1)}, u32[]{:S(2)}, u32[]{:S(2)}) %all-to-all-start.2) | async-done | bytes 524320 | tf_op jit(solution)/shard_map/all_to_all | solution.py:636
  81.4 2.0 %finish.1 = bf16[512,512]{1,0:T(8,128)(2,1)} custom-call(bf16[8,256,128]{2,1,0:T(8,128)(2,1)S(1)} %all-to-all-done.2.c_ref, bf16[2,512,512]{2,1,0:T(8,128)(2,1)} %query_terms.1.term_any), custom_call_target="tpu_custom_call" | custom-call | tf_op jit(solution)/shard_map/finish/pallas_call | solution.py:558
  (5 shorter events, 0.0 us)
Async XLA Ops:
  2.5 3.1 %collective-permute-start = (bf16[128,4096]{1,0:T(8,128)(2,1)}, bf16[128,4096]{1,0:T(8,128)(2,1)S(1)}, u32[]{:S(2)}, u32[]{:S(2)}) collective-permute-start(bf16[128,4096]{1,0:T(8,128)(2,1)} %get-tuple-element.19.refs_0_), channel_id=1, source_target_pairs={{0,1},{1,0},{2,3},{3,2},{4,5},{5,4},{6,7},{7,6},{8,9},{9,8},{10,11... | collective-permute-start | bytes 3145736 | tf_op jit(solution)/shard_map/ppermute | solution.py:591
  3.0 26.8 %collective-permute-start.3 = (bf16[128,4096]{1,0:T(8,128)(2,1)}, bf16[128,4096]{1,0:T(8,128)(2,1)S(1)}, u32[]{:S(2)}, u32[]{:S(2)}) collective-permute-start(bf16[128,4096]{1,0:T(8,128)(2,1)} %get-tuple-element.19.refs_0_), channel_id=1, source_target_pairs={{0,2},{1,3},{2,0},{3,1},{4,6},{5,7},{6,4},{7,5},{8,10},{9,11},{10,... | collective-permute-start | bytes 3145736 | tf_op jit(solution)/shard_map/ppermute | solution.py:591
  5.6 2.0 %copy-start.1 = (bf16[128,4096]{1,0:T(8,128)(2,1)}, bf16[128,4096]{1,0:T(8,128)(2,1)S(1)}, u32[]{:S(2)}) copy-start(bf16[128,4096]{1,0:T(8,128)(2,1)S(1)} %collective-permute-done.refs_1_) | copy-start | bytes 3145732
  5.6 9.1 %collective-permute-start.2 = (bf16[8,4096]{1,0:T(8,128)(2,1)}, bf16[8,4096]{1,0:T(8,128)(2,1)S(1)}, u32[]{:S(2)}, u32[]{:S(2)}) collective-permute-start(bf16[8,4096]{1,0:T(8,128)(2,1)} %get-tuple-element.22), channel_id=1, source_target_pairs={{3,7},{7,11},{11,15},{15,19},{19,23},{23,27},{27,31},{1,1},{5,5},{... | collective-permute-start | bytes 196616 | tf_op jit(solution)/shard_map/ppermute | solution.py:611
  6.2 8.5 %collective-permute-start.1 = (bf16[8,4096]{1,0:T(8,128)(2,1)}, bf16[8,4096]{1,0:T(8,128)(2,1)S(1)}, u32[]{:S(2)}, u32[]{:S(2)}) collective-permute-start(bf16[8,4096]{1,0:T(8,128)(2,1)} %get-tuple-element.22), channel_id=1, source_target_pairs={{3,6},{7,10},{11,14},{15,18},{19,22},{23,26},{27,30},{1,0},{5,4},{... | collective-permute-start | bytes 196616 | tf_op jit(solution)/shard_map/ppermute | solution.py:611
  14.7 28.9 %all-to-all-start = ((bf16[8,384,128]{2,1,0:T(8,128)(2,1)}), bf16[8,384,128]{2,1,0:T(8,128)(2,1)S(1)}, u32[]{:S(2)}, u32[]{:S(2)}) async-start(bf16[8,384,128]{2,1,0:T(8,128)(2,1)} %get-tuple-element.23), calls=%async_computation | async-start | bytes 1572864 | tf_op jit(solution)/shard_map/all_to_all | solution.py:624
  21.9 9.0 %collective-permute-start.5 = (bf16[8,4096]{1,0:T(8,128)(2,1)S(1)}, bf16[8,4096]{1,0:T(8,128)(2,1)S(1)}, u32[]{:S(2)}, u32[]{:S(2)}) collective-permute-start(bf16[8,4096]{1,0:T(8,128)(2,1)S(1)} %add.12), channel_id=1, source_target_pairs={{0,2},{1,3},{2,0},{3,1},{4,6},{5,7},{6,4},{7,5},{8,10},{9,11},{10,... | collective-permute-start | bytes 196616 | tf_op jit(solution)/shard_map/ppermute | solution.py:591
  29.8 2.7 %copy-start.2 = (bf16[128,4096]{1,0:T(8,128)(2,1)}, bf16[128,4096]{1,0:T(8,128)(2,1)S(1)}, u32[]{:S(2)}) copy-start(bf16[128,4096]{1,0:T(8,128)(2,1)S(1)} %collective-permute-done.3.refs_0_.refs_2_) | copy-start | bytes 3145732
  29.8 2.7 %collective-permute-start.4 = (bf16[128,4096]{1,0:T(8,128)(2,1)S(1)}, bf16[128,4096]{1,0:T(8,128)(2,1)S(1)}, u32[]{:S(2)}, u32[]{:S(2)}) collective-permute-start(bf16[128,4096]{1,0:T(8,128)(2,1)S(1)} %collective-permute-done.3.refs_0_.refs_2_), channel_id=1, source_target_pairs={{0,1},{1,0},{2,3},{3,2},{4,5},{5,4},{6,7},{7,6},{8,9},{9,8},{10,11... | collective-permute-start | bytes 3145736 | tf_op jit(solution)/shard_map/ppermute | solution.py:591
  31.9 0.8 copy-start.4
  32.7 1.0 %copy-start.3 = (bf16[128,4096]{1,0:T(8,128)(2,1)}, bf16[128,4096]{1,0:T(8,128)(2,1)S(1)}, u32[]{:S(2)}) copy-start(bf16[128,4096]{1,0:T(8,128)(2,1)S(1)} %collective-permute-done.4.refs_1_.refs_3_) | copy-start | bytes 3145732
  43.6 3.4 %copy-start = (bf16[8,384,128]{2,1,0:T(8,128)(2,1)}, bf16[8,384,128]{2,1,0:T(8,128)(2,1)S(1)}, u32[]{:S(2)}) copy-start(bf16[8,384,128]{2,1,0:T(8,128)(2,1)S(1)} %all-to-all-done.x_any.early_any) | copy-start | bytes 2359300
  43.6 13.0 %all-to-all-start.1 = ((bf16[8,136,128]{2,1,0:T(8,128)(2,1)}), bf16[8,136,128]{2,1,0:T(8,128)(2,1)S(1)}, u32[]{:S(2)}, u32[]{:S(2)}) async-start(bf16[8,136,128]{2,1,0:T(8,128)(2,1)} %get-tuple-element.26), calls=%async_computation.1 | async-start | bytes 557056 | tf_op jit(solution)/shard_map/all_to_all | solution.py:634
  56.6 0.7 copy-start.5
  63.2 18.1 %all-to-all-start.2 = ((bf16[8,256,128]{2,1,0:T(8,128)(2,1)}), bf16[8,256,128]{2,1,0:T(8,128)(2,1)S(1)}, u32[]{:S(2)}, u32[]{:S(2)}) async-start(bf16[8,256,128]{2,1,0:T(8,128)(2,1)} %convolve.1), calls=%async_computation.2 | async-start | bytes 1048576 | tf_op jit(solution)/shard_map/all_to_all | solution.py:636
